TPU v7x, 32 devices: a whole 2x2x4 slice. The times are simulated.
32 devices in a mesh: dp: 8 (over y, x, core), head: 4 (over z).
Axes of the slice: x: 2, y: 2, z: 4, core: 2. Of those that a mesh axis runs over, the one named last changes fastest.
Arguments:
- block_input: bfloat16 [16384, 1024], P('dp'), may hold values from -6 to 6
- cotangent: bfloat16 [16384, 1024], P(('dp', 'head')), may hold values from -6 to 6
- expert_ids: int32 [16384, 2], P(('dp', 'head')), may hold values from 0 to 7, all different within a row
- priority: int32 [32, 512], P(('dp', 'head')), may hold values from 0 to 511, each once within a row
- rel_bucket: int32 [1023], replicated, may hold values from 0 to 31, as said below
- norm1_gain: float32 [1024], replicated, may hold values from 0.5 to 1.5
- w_query: bfloat16 [1024, 1024], P(None, 'head'), may hold values from -0.1875 to 0.1875
- w_key: bfloat16 [1024, 1024], P(None, 'head'), may hold values from -0.1875 to 0.1875
- w_value: bfloat16 [1024, 1024], P(None, 'head'), may hold values from -0.1875 to 0.1875
- w_out: bfloat16 [1024, 1024], P('head'), may hold values from -1.5 to 1.5
- pos_bias: float32 [32, 16], P(None, 'head'), may hold values from -4 to 4
- norm2_gain: float32 [1024], replicated, may hold values from 0.5 to 1.5
- w_router: bfloat16 [1024, 8], replicated, may hold values from -0.125 to 0.125
- w_gate: bfloat16 [8, 1024, 2816], P('dp'), may hold values from -0.1875 to 0.1875
- w_up: bfloat16 [8, 1024, 2816], P('dp'), may hold values from -0.1875 to 0.1875
- w_down: bfloat16 [8, 2816, 1024], P('dp'), may hold values from -0.109375 to 0.109375
Outputs:
- output: float32 [16384, 1024], P(('dp', 'head'))
- grad_input: float32 [16384, 1024], P(('dp', 'head'))
- grad_norm1: float32 [1024], replicated
- grad_query_w: float32 [1024, 1024], P(None, 'head')
- grad_key_w: float32 [1024, 1024], P(None, 'head')
- grad_value_w: float32 [1024, 1024], P(None, 'head')
- grad_out_proj: float32 [1024, 1024], P('head')
- grad_pos_bias: float32 [32, 16], P(None, 'head')
- grad_norm2: float32 [1024], replicated
- grad_router: float32 [1024, 8], replicated
- grad_gate_w: float32 [8, 1024, 2816], P('dp', 'head')
- grad_up_w: float32 [8, 1024, 2816], P('dp', 'head')
- grad_down_w: float32 [8, 2816, 1024], P('dp', 'head')
Inputs may be any that keep to these rules, and one draw needn't show every extreme that they name: `expert_ids`: the two ids of a row differ. `priority`: each row is a permutation of 0 to 511. `rel_bucket`: entry 511 + d is the bucket of a key d positions after its query; distances under 8 have buckets of their own, buckets never fall as the distance grows on either side, and keys after the query use buckets 16 and above.
All inputs are finite; a program needn't handle non-finite values.
Results may differ from a plain program's by a relative error of at most 0.024.
Values may be sent and summed in bfloat16 or wider, within the bound.
A program may use at most 256 MiB of HBM per device.

v0:
```python
import jax
import jax.numpy as jnp
from jax import lax
from jax.sharding import PartitionSpec as P

EPS = 1e-06
SCALE = 0.125
HIGH = lax.Precision.HIGHEST


def rms_norm(value, gain):
    return value * lax.rsqrt(jnp.mean(value * value, axis=-1, keepdims=True) + EPS) * gain


def geglu(gate, up_part):
    return jax.nn.gelu(gate) * up_part


def contract(left, right, left_dim, right_dim, precision=None):
    return lax.dot_general(
        left,
        right,
        (((left_dim,), (right_dim,)), ((), ())),
        precision=precision,
        preferred_element_type=jnp.float32,
    )


def route_slots(chosen, ranks, experts, capacity):
    count = chosen.shape[0]
    keys = jnp.concatenate([ranks, ranks + count])
    wanted = jnp.concatenate([chosen[:, 0], chosen[:, 1]])
    by_key = jnp.zeros((2 * count,), jnp.int32).at[keys].set(wanted)
    member = (by_key[:, None] == jnp.arange(experts, dtype=jnp.int32)[None, :]).astype(jnp.int32)
    before = jnp.cumsum(member, axis=0) - member
    rank_key = jnp.sum(before * member, axis=1)
    place = rank_key[keys]
    dest = jnp.where(place < capacity, wanted * capacity + place, experts * capacity)
    return jnp.stack([dest[:count], dest[count:]], axis=1)


def attend_forward(query, key, value, bias_mat):
    scores = (
        jnp.einsum("qhd,khd->hqk", query, key, preferred_element_type=jnp.float32) * SCALE
        + bias_mat
    )
    top = jnp.max(scores, axis=-1, keepdims=True)
    shifted = jnp.exp(scores - top)
    total = jnp.sum(shifted, axis=-1, keepdims=True)
    probs = shifted / total
    attended = jnp.einsum(
        "hqk,khd->qhd", probs.astype(jnp.bfloat16), value, preferred_element_type=jnp.float32
    )
    return (attended.astype(jnp.bfloat16), top + jnp.log(total))


def attend_backward(query, key, value, grad_attended, log_total, bias_mat, onehot):
    scores = (
        jnp.einsum("qhd,khd->hqk", query, key, preferred_element_type=jnp.float32) * SCALE
        + bias_mat
    )
    probs = jnp.exp(scores - log_total)
    grad_probs = jnp.einsum(
        "qhd,khd->hqk", grad_attended, value, preferred_element_type=jnp.float32
    )
    grad_value = jnp.einsum(
        "hqk,qhd->khd",
        probs.astype(jnp.bfloat16),
        grad_attended,
        preferred_element_type=jnp.float32,
    )
    delta = jnp.sum(probs * grad_probs, axis=-1, keepdims=True)
    grad_scores = (probs * (grad_probs - delta)).astype(jnp.bfloat16)
    grad_query = (
        jnp.einsum("hqk,khd->qhd", grad_scores, key, preferred_element_type=jnp.float32) * SCALE
    )
    grad_key = (
        jnp.einsum("hqk,qhd->khd", grad_scores, query, preferred_element_type=jnp.float32) * SCALE
    )
    heads_here = grad_scores.shape[0]
    grad_bias = jnp.dot(
        grad_scores.reshape(heads_here, -1), onehot, preferred_element_type=jnp.float32
    )
    return (
        grad_query.astype(jnp.bfloat16),
        grad_key.astype(jnp.bfloat16),
        grad_value.astype(jnp.bfloat16),
        grad_bias,
    )


def body(
    block_input,
    cotangent,
    expert_ids,
    priority,
    rel_bucket,
    norm1_gain,
    w_query,
    w_key,
    w_value,
    w_out,
    pos_bias,
    norm2_gain,
    w_router,
    w_gate,
    w_up,
    w_down,
):
    group_rows, width = block_input.shape
    own_rows = cotangent.shape[0]
    heads_here = pos_bias.shape[1]
    buckets = pos_bias.shape[0]
    head_cols = w_query.shape[1]
    head_dim = head_cols // heads_here
    length = (rel_bucket.shape[0] + 1) // 2
    sequences = group_rows // length
    experts = w_router.shape[1]
    capacity = 5 * 2 * own_rows // (4 * experts)
    start_own = lax.axis_index("head") * own_rows
    inputs_all = block_input.astype(jnp.float32)
    normed = rms_norm(inputs_all, norm1_gain).astype(jnp.bfloat16)
    query = jnp.dot(normed, w_query, preferred_element_type=jnp.float32).astype(jnp.bfloat16)
    key_rows = jnp.dot(normed, w_key, preferred_element_type=jnp.float32).astype(jnp.bfloat16)
    value_rows = jnp.dot(normed, w_value, preferred_element_type=jnp.float32).astype(jnp.bfloat16)
    positions = jnp.arange(length, dtype=jnp.int32)
    table = rel_bucket[positions[None, :] - positions[:, None] + length - 1]
    onehot = (table.reshape(-1)[:, None] == jnp.arange(buckets, dtype=jnp.int32)[None, :]).astype(
        jnp.bfloat16
    )
    bias_mat = contract(pos_bias, onehot.astype(jnp.float32), 0, 1, HIGH).reshape(
        heads_here, length, length
    )
    seq_shape = (sequences, length, heads_here, head_dim)
    seq_query = query.reshape(seq_shape)
    seq_key = key_rows.reshape(seq_shape)
    seq_value = value_rows.reshape(seq_shape)

    def forward_step(carry, parts):
        attended_seq, log_total = attend_forward(parts[0], parts[1], parts[2], bias_mat)
        return (carry, (attended_seq, log_total))

    _, (attended, log_totals) = lax.scan(
        forward_step, jnp.zeros((), jnp.float32), (seq_query, seq_key, seq_value)
    )
    attended = attended.reshape(group_rows, head_cols)
    partial_value = jnp.dot(attended, w_out, preferred_element_type=jnp.float32)
    summed = lax.psum(partial_value.astype(jnp.bfloat16), "head").astype(jnp.float32)
    branch = lax.dynamic_slice_in_dim(summed, start_own, own_rows, 0)
    inputs_own = lax.dynamic_slice_in_dim(inputs_all, start_own, own_rows, 0)
    mixed = inputs_own + branch
    normed2_full, norm2_pull = jax.vjp(rms_norm, mixed, norm2_gain)
    normed2 = normed2_full.astype(jnp.bfloat16)
    logits = jnp.dot(normed2, w_router, preferred_element_type=jnp.float32)
    gates = jax.nn.softmax(jnp.take_along_axis(logits, expert_ids, axis=1), axis=-1)
    dest = route_slots(expert_ids, priority[0], experts, capacity)
    slot_count = experts * capacity
    slot_range = jnp.arange(slot_count, dtype=jnp.int32)
    selector = (dest.reshape(-1)[:, None] == slot_range[None, :]).astype(jnp.bfloat16)
    rows_sent = jnp.broadcast_to(normed2[:, None, :], (own_rows, 2, width)).reshape(
        own_rows * 2, width
    )
    send = (
        contract(selector, rows_sent, 0, 0).astype(jnp.bfloat16).reshape(experts, capacity, width)
    )
    received = lax.all_to_all(send, "dp", split_axis=0, concat_axis=0, tiled=True).reshape(
        -1, width
    )
    gate_w = w_gate[0]
    up_w = w_up[0]
    down_w = w_down[0]
    gate_pre = jnp.dot(received, gate_w, preferred_element_type=jnp.float32)
    up_pre = jnp.dot(received, up_w, preferred_element_type=jnp.float32)
    hidden = geglu(gate_pre, up_pre).astype(jnp.bfloat16)
    returned = jnp.dot(hidden, down_w, preferred_element_type=jnp.float32).astype(jnp.bfloat16)
    came_back = lax.all_to_all(
        returned.reshape(-1, capacity, width), "dp", split_axis=0, concat_axis=0, tiled=True
    ).reshape(-1, width)
    chosen_rows = jnp.dot(selector, came_back, preferred_element_type=jnp.float32).reshape(
        own_rows, 2, width
    )
    output = mixed + jnp.sum(gates[:, :, None] * chosen_rows, axis=1)
    grad_output = cotangent.astype(jnp.float32)
    grad_gates = jnp.sum(grad_output[:, None, :] * chosen_rows, axis=2)
    grad_sent = (
        (gates[:, :, None] * grad_output[:, None, :])
        .astype(jnp.bfloat16)
        .reshape(own_rows * 2, width)
    )
    grad_buffer = (
        contract(selector, grad_sent, 0, 0).astype(jnp.bfloat16).reshape(experts, capacity, width)
    )
    grad_returned = lax.all_to_all(
        grad_buffer, "dp", split_axis=0, concat_axis=0, tiled=True
    ).reshape(-1, width)
    gate_again = jnp.dot(received, gate_w, preferred_element_type=jnp.float32)
    up_again = jnp.dot(received, up_w, preferred_element_type=jnp.float32)
    hidden_again, geglu_pull = jax.vjp(geglu, gate_again, up_again)
    hidden_low = hidden_again.astype(jnp.bfloat16)
    grad_hidden = contract(grad_returned, down_w, 1, 1)
    grad_gate_pre, grad_up_pre = geglu_pull(grad_hidden)
    grad_gate_pre = grad_gate_pre.astype(jnp.bfloat16)
    grad_up_pre = grad_up_pre.astype(jnp.bfloat16)
    grad_routed = (
        contract(grad_gate_pre, gate_w, 1, 1) + contract(grad_up_pre, up_w, 1, 1)
    ).astype(jnp.bfloat16)
    grad_back = lax.all_to_all(
        grad_routed.reshape(-1, capacity, width), "dp", split_axis=0, concat_axis=0, tiled=True
    ).reshape(-1, width)
    grad_down = contract(hidden_low, grad_returned, 0, 0)
    grad_gate = contract(received, grad_gate_pre, 0, 0)
    grad_up = contract(received, grad_up_pre, 0, 0)
    grad_gate_w, grad_up_w, grad_down_w = (
        lax.psum_scatter(
            grad_gate[None].astype(jnp.bfloat16), "head", scatter_dimension=1, tiled=True
        ).astype(jnp.float32),
        lax.psum_scatter(
            grad_up[None].astype(jnp.bfloat16), "head", scatter_dimension=1, tiled=True
        ).astype(jnp.float32),
        lax.psum_scatter(
            grad_down[None].astype(jnp.bfloat16), "head", scatter_dimension=1, tiled=True
        ).astype(jnp.float32),
    )
    both_picks = jnp.sum(selector.reshape(own_rows, 2, slot_count), axis=1)
    grad_normed2 = jnp.dot(both_picks, grad_back, preferred_element_type=jnp.float32)
    grad_picked = gates * (grad_gates - jnp.sum(gates * grad_gates, axis=1, keepdims=True))
    expert_range = jnp.arange(experts, dtype=jnp.int32)
    grad_logits = jnp.sum(
        (expert_ids[:, :, None] == expert_range[None, None, :]).astype(jnp.float32)
        * grad_picked[:, :, None],
        axis=1,
    )
    router_full = w_router.astype(jnp.float32)
    grad_normed2 = grad_normed2 + contract(grad_logits, router_full, 1, 1, HIGH)
    grad_router = contract(normed2.astype(jnp.float32), grad_logits, 0, 0, HIGH)
    grad_mixed, grad_norm2 = norm2_pull(grad_normed2)
    grad_mixed = grad_mixed + grad_output
    grad_branch = grad_mixed.astype(jnp.bfloat16)
    piece = lax.all_gather(grad_branch, "head", axis=0, tiled=True)
    grad_wout = contract(attended, piece, 0, 0)
    grad_heads = contract(piece, w_out, 1, 1)
    grad_out_proj, grad_heads = (grad_wout, grad_heads)
    grad_heads = grad_heads.astype(jnp.bfloat16).reshape(seq_shape)

    def backward_step(grad_bias, parts):
        grad_query, grad_key, grad_value, bias_term = attend_backward(
            parts[0], parts[1], parts[2], parts[3], parts[4], bias_mat, onehot
        )
        return (grad_bias + bias_term, (grad_query, grad_key, grad_value))

    grad_bias, (grad_query, grad_key, grad_value) = lax.scan(
        backward_step,
        jnp.zeros((heads_here, buckets), jnp.float32),
        (seq_query, seq_key, seq_value, grad_heads, log_totals),
    )
    grad_query = grad_query.reshape(group_rows, head_cols)
    grad_key = grad_key.reshape(group_rows, head_cols)
    grad_value = grad_value.reshape(group_rows, head_cols)
    grad_query_w = contract(normed, grad_query, 0, 0)
    grad_key_w = contract(normed, grad_key, 0, 0)
    grad_value_w = contract(normed, grad_value, 0, 0)
    total = jnp.zeros((own_rows * lax.axis_size("head"), width), jnp.float32)
    for grad_rows, weight in ((grad_query, w_query), (grad_key, w_key), (grad_value, w_value)):
        piece = grad_rows
        total = total + contract(piece, weight, 1, 1)
    grad_normed = lax.psum_scatter(
        total.astype(jnp.bfloat16), "head", scatter_dimension=0, tiled=True
    ).astype(jnp.float32)
    _, norm1_pull = jax.vjp(rms_norm, inputs_own, norm1_gain)
    grad_first, grad_norm1 = norm1_pull(grad_normed)
    grad_input = grad_mixed + grad_first
    grad_query_w, grad_key_w, grad_value_w, grad_out_proj, grad_bias = (
        lax.psum(grad_query_w.astype(jnp.bfloat16), "dp").astype(jnp.float32),
        lax.psum(grad_key_w.astype(jnp.bfloat16), "dp").astype(jnp.float32),
        lax.psum(grad_value_w.astype(jnp.bfloat16), "dp").astype(jnp.float32),
        lax.psum(grad_out_proj.astype(jnp.bfloat16), "dp").astype(jnp.float32),
        lax.psum(grad_bias.astype(jnp.bfloat16), "dp").astype(jnp.float32),
    )
    grad_norm1, grad_norm2, grad_router = lax.psum(
        (grad_norm1, grad_norm2, grad_router), ("dp", "head")
    )
    return (
        output,
        grad_input,
        grad_norm1,
        grad_query_w,
        grad_key_w,
        grad_value_w,
        grad_out_proj,
        jnp.transpose(grad_bias),
        grad_norm2,
        grad_router,
        grad_gate_w,
        grad_up_w,
        grad_down_w,
    )


def solution(mesh):
    placed = (
        P("dp", None),
        P(("dp", "head"), None),
        P(("dp", "head"), None),
        P(("dp", "head"), None),
        P(),
        P(),
        P(None, "head"),
        P(None, "head"),
        P(None, "head"),
        P("head", None),
        P(None, "head"),
        P(),
        P(),
        P("dp", None, None),
        P("dp", None, None),
        P("dp", None, None),
    )
    return jax.shard_map(
        body,
        mesh=mesh,
        in_specs=placed,
        out_specs=(
            P(("dp", "head"), None),
            P(("dp", "head"), None),
            P(),
            P(None, "head"),
            P(None, "head"),
            P(None, "head"),
            P("head", None),
            P(None, "head"),
            P(),
            P(),
            P("dp", "head", None),
            P("dp", "head", None),
            P("dp", "head", None),
        ),
        check_vma=False,
    )
```

profile of v0, /device:TPU:0, one launch (start us, length us, event | category | flops | bytes accessed | tf_op | source)
XLA Modules:
  0.0 2250.0 jit_solution(2709492240434155704)
XLA Ops:
  8.4 3.2 multiply_reduce_fusion.1
  17.1 3.4 reshape.435
  22.8 4.4 convolution_convert_fusion.3
  27.2 3.4 reshape.436
  32.9 4.4 convolution_convert_fusion.2
  37.4 3.3 reshape.437
  44.7 1041.2 %gather_fusion = s32[262144]{0:T(1024)S(1)} fusion(s32[1023]{0:T(1024)S(1)} %copy-done.1, s32[262144]{0:T(1024)S(1)} %broadcast_clamp_fusion), kind=kCustom, calls=%fused_computation | custom fusion | bytes 3145728 | tf_op jit(solution)/shard_map/gather | solution.py:127
  1085.9 10.5 fusion.59
  1096.4 3.2 copy.216
  1099.6 5.2 copy.176
  1105.0 24.6 %while.29 = (s32[]{:T(128)}, bf16[4,512,4,64]{1,3,2,0:T(8,128)(2,1)S(1)}, f32[4,4,512,1]{2,1,3,0:T(4,128)}, bf16[4,512,4,64]{1,3,2,0:T(8,128)(2,1)}, bf16[4,512,...) while((s32[]{:T(128)}, ...), condition=%wide.region_4.5_spmd, body=%wide.region_1.4_spmd.sunk | while | flops 276953088 | bytes 17893972 | solution.py:143
  1105.0 3.1 fusion.195
  1111.1 3.1 fusion.195
  1117.3 3.1 fusion.195
  1123.4 3.1 fusion.195
  1131.6 3.2 convolution_convert_fusion
  1134.9 6.5 convert_element_type.173
  1141.9 4.3 scatter_custom_fusion
  1149.5 4.5 gather_fusion.1
  1157.5 6.1 mul.277
  1163.6 129.1 %all-reduce.5.cloned.1.call-done = bf16[2048,1024]{1,0:T(8,128)(2,1)} async-done(((bf16[2048,1024]{1,0:T(8,128)(2,1)}), bf16[2048,1024]{1,0:T(8,128)(2,1)}) %all-reduce.5.cloned.1.call-update) | async-done | bytes 4194320 | tf_op jit(solution)/shard_map/psum | solution.py:148
  1297.7 6.5 gather_fusion.2
  1304.9 6.8 fusion.89
  1311.7 4.4 all-to-all-start.2
  1321.3 4.4 fusion.88
  1325.7 22.7 %all-to-all-done.2 = bf16[8,160,1024]{2,1,0:T(8,128)(2,1)} async-done(((bf16[8,160,1024]{2,1,0:T(8,128)(2,1)}), bf16[8,160,1024]{2,1,0:T(8,128)(2,1)}, u32[]{:S(2)}, u32[]{:S(2)}) %all-to-all-start.2) | async-done | bytes 2621472 | tf_op jit(solution)/shard_map/all_to_all | solution.py:193
  1348.4 3.8 all-to-all-start
  1352.2 13.9 fusion.68
  1366.1 18.3 all-to-all-done
  1384.4 13.8 fusion.74
  1398.2 25.4 %fusion.67 = (bf16[1280,2816]{1,0:T(8,128)(2,1)}, bf16[1280,2816]{1,0:T(8,128)(2,1)}, bf16[1280,2816]{1,0:T(8,128)(2,1)}) fusion(f32[1280,2816]{1,0:T(8,128)} %fusion.68, f32[1280,2816]{1,0:T(8,128)} %fusion.74, bf16[1280,1024]{1,0:T(8,128)(2,1)S(1)} %bitcast.280, bf16[1,1024,2816]{2,1,0:T(8,128)(2,1)} %param.33), kind=kOutput, calls=%fused_computation.75 | convolution fusion | flops 7475691520 | bytes 58851328 | tf_op jit(solution)/shard_map/dot_general | solution.py:172
  1423.6 12.6 fusion.90
  1436.2 4.8 all-to-all-start.1
  1441.0 11.7 fusion.72
  1452.7 11.0 add_convert_fusion.1
  1463.7 9.5 all-to-all-done.1
  1473.2 4.5 all-to-all-start.3
  1478.6 6.8 multiply_reduce_fusion.2
  1485.5 24.5 %all-to-all-done.3 = bf16[8,160,1024]{2,1,0:T(8,128)(2,1)} async-done(((bf16[8,160,1024]{2,1,0:T(8,128)(2,1)}), bf16[8,160,1024]{2,1,0:T(8,128)(2,1)}, u32[]{:S(2)}, u32[]{:S(2)}) %all-to-all-start.3) | async-done | bytes 2621472 | tf_op jit(solution)/shard_map/all_to_all | solution.py:207
  1510.1 3.4 fusion.121
  1518.8 78.1 %all-gather.2.cloned.1.call-done = bf16[2048,1024]{1,0:T(8,128)(2,1)} async-done(((bf16[512,1024]{1,0:T(8,128)(2,1)}), bf16[2048,1024]{1,0:T(8,128)(2,1)}) %all-gather.2.cloned.1.call-update) | async-done | bytes 4194320 | tf_op jit(solution)/shard_map/all_gather | solution.py:239
  1596.9 4.5 convolution_convert_fusion.1
  1601.3 3.7 reshape.434
  1610.6 114.5 %while.30 = (s32[]{:T(128)}, f32[4,32]{1,0:T(4,128)S(1)}, bf16[4,512,4,64]{1,3,2,0:T(8,128)(2,1)}, bf16[4,512,4,64]{1,3,2,0:T(8,128)(2,1)}, bf16[4,512,4,64]{1,3...) while((s32[]{:T(128)}, f32[4,32]{1,0:T(4,128)S(1)}, ...), condition=%wide.region_21.22_spmd.clone, body=%wide.region_19.21_spmd.clone.sunk | while | flops 765065472 | bytes 100186336 | solution.py:251
  1621.2 4.5 copy.220
  1625.8 6.3 fusion.209
  1649.8 4.5 copy.220
  1654.4 6.3 fusion.209
  1678.4 4.5 copy.220
  1683.0 6.3 fusion.209
  1707.0 4.5 copy.220
  1711.5 6.3 fusion.209
  1738.9 13.2 convert_bitcast_fusion.1
  1752.2 12.5 convert_bitcast_fusion
  1764.7 13.0 convert_bitcast_fusion.2
  1781.5 3.3 add_convert_fusion
  1786.6 13.9 psum.69
  1808.5 94.8 %reduce-scatter.9.cloned.1.call-done = bf16[1,256,2816]{2,1,0:T(8,128)(2,1)} async-done(((bf16[1,1024,2816]{2,1,0:T(8,128)(2,1)}), bf16[1,256,2816]{2,1,0:T(8,128)(2,1)}) %reduce-scatter.9.cloned.1.call-update) | async-done | bytes 1441808 | tf_op jit(solution)/shard_map/reduce_scatter | solution.py:217
  1906.4 101.9 %reduce-scatter.11.cloned.1.call-done = bf16[1,704,1024]{2,1,0:T(8,128)(2,1)} async-done(((bf16[1,2816,1024]{2,1,0:T(8,128)(2,1)}), bf16[1,704,1024]{2,1,0:T(8,128)(2,1)}) %reduce-scatter.11.cloned.1.call-update) | async-done | bytes 1441808 | tf_op jit(solution)/shard_map/reduce_scatter | solution.py:220
  2008.3 3.3 convert_element_type.215
  2011.6 101.7 %reduce-scatter.7.cloned.1.call-done = bf16[1,256,2816]{2,1,0:T(8,128)(2,1)} async-done(((bf16[1,1024,2816]{2,1,0:T(8,128)(2,1)}), bf16[1,256,2816]{2,1,0:T(8,128)(2,1)}) %reduce-scatter.7.cloned.1.call-update) | async-done | bytes 1441808 | tf_op jit(solution)/shard_map/reduce_scatter | solution.py:214
  2116.5 76.6 %reduce-scatter.5.cloned.1.call-done = bf16[512,1024]{1,0:T(8,128)(2,1)} async-done(((bf16[2048,1024]{1,0:T(8,128)(2,1)}), bf16[512,1024]{1,0:T(8,128)(2,1)}) %reduce-scatter.5.cloned.1.call-update) | async-done | bytes 1048592 | tf_op jit(solution)/shard_map/reduce_scatter | solution.py:266
  2195.7 41.7 %all-reduce = (f32[1024]{0:T(1024)}, f32[1024]{0:T(1024)}, f32[1024,8]{0,1:T(8,128)}) all-reduce(f32[1024]{0:T(1024)S(1)} %get-tuple-element.278, f32[1024]{0:T(1024)S(1)} %copy-done.51, f32[1024,8]{0,1:T(8,128)S(1)} %fusion.124), channel_id=1, replica_groups=mesh['dp'=8,'head'=4] {'dp','head'}, use_global_device_ids=true, to_apply=%region_26.27 | all-reduce | flops 10240 | bytes 81920 | tf_op jit(solution)/shard_map/psum | solution.py:279
  2237.4 5.3 fusion.102
  (275 shorter events, 166.1 us)
Async XLA Ops:
  7.2 1124.4 %copy-start = (bf16[256,1024]{1,0:T(8,128)(2,1)S(1)}, bf16[256,1024]{1,0:T(8,128)(2,1)}, u32[]{:S(2)}) copy-start(bf16[256,1024]{1,0:T(8,128)(2,1)} %param.29) | copy-start | bytes 1572868
  7.2 4.4 copy-start.42
  7.2 1285.5 %all-reduce.5.cloned.1.call-start = ((), (), s32[]{:S(2)}) async-start(), calls=%async_computation.8 | async-start | bytes 8388608 | tf_op jit(solution)/shard_map/psum | solution.py:148
  8.4 3.4 copy-start.8
  11.8 3.1 copy-start.28
  12.9 1.9 copy-start.18
  17.1 5.7 copy-start.24
  27.2 5.7 copy-start.26
  40.7 4.0 copy-start.1
  44.7 1041.2 %copy-start.54 = (f32[32,4]{0,1:T(4,128)S(1)}, f32[32,4]{0,1:T(4,128)}, u32[]{:S(2)}) copy-start(f32[32,4]{0,1:T(4,128)} %param.30) | copy-start | bytes 1540
  1085.9 10.5 copy-start.23
  1134.9 6.6 copy-start.35
  1134.9 6.9 copy-start.52
  1141.5 13.0 copy-start.10
  1154.1 3.5 copy-start.44
  1163.6 133.4 %copy-start.36 = (f32[1024]{0:T(1024)S(1)}, f32[1024]{0:T(1024)}, u32[]{:S(2)}) copy-start(f32[1024]{0:T(1024)} %param.31) | copy-start | bytes 12292
  1163.6 133.6 %copy-start.33 = (bf16[1024,8]{0,1:T(8,128)(2,1)S(1)}, bf16[1024,8]{0,1:T(8,128)(2,1)}, u32[]{:S(2)}) copy-start(bf16[1024,8]{0,1:T(8,128)(2,1)} %param.32) | copy-start | bytes 49156
  1297.3 18.9 copy-start.12
  1311.7 36.7 %all-to-all-start.2 = ((bf16[8,160,1024]{2,1,0:T(8,128)(2,1)}), bf16[8,160,1024]{2,1,0:T(8,128)(2,1)}, u32[]{:S(2)}, u32[]{:S(2)}) async-start(bf16[8,160,1024]{2,1,0:T(8,128)(2,1)} %bitcast.284), calls=%async_computation.2 | async-start | bytes 5242880 | tf_op jit(solution)/shard_map/all_to_all | solution.py:193
  1348.4 36.0 %all-to-all-start = ((bf16[8,160,1024]{2,1,0:T(8,128)(2,1)}), bf16[8,160,1024]{2,1,0:T(8,128)(2,1)S(1)}, u32[]{:S(2)}, u32[]{:S(2)}) async-start(bf16[8,160,1024]{2,1,0:T(8,128)(2,1)} %bitcast.285), calls=%async_computation | async-start | bytes 5242880 | tf_op jit(solution)/shard_map/all_to_all | solution.py:166
  1384.4 13.8 copy-start.22
  1436.2 16.5 slice-start
  1436.2 37.1 %all-to-all-start.1 = ((bf16[8,160,1024]{2,1,0:T(8,128)(2,1)}), bf16[8,160,1024]{2,1,0:T(8,128)(2,1)}, u32[]{:S(2)}, u32[]{:S(2)}) async-start(bf16[8,160,1024]{2,1,0:T(8,128)(2,1)} %bitcast.23), calls=%async_computation.1 | async-start | bytes 5242880 | tf_op jit(solution)/shard_map/all_to_all | solution.py:176
  1441.0 11.7 slice-start.1
  1463.7 14.1 copy-start.11
  1473.2 4.8 copy-start.45
  1473.2 36.8 %all-to-all-start.3 = ((bf16[8,160,1024]{2,1,0:T(8,128)(2,1)}), bf16[8,160,1024]{2,1,0:T(8,128)(2,1)}, u32[]{:S(2)}, u32[]{:S(2)}) async-start(bf16[8,160,1024]{2,1,0:T(8,128)(2,1)} %bitcast.283), calls=%async_computation.3 | async-start | bytes 5242880 | tf_op jit(solution)/shard_map/all_to_all | solution.py:207
  1477.8 119.1 %all-gather.2.cloned.1.call-start = ((), (), s32[]{:S(2)}) async-start(), calls=%async_computation.9 | async-start | bytes 5242880 | tf_op jit(solution)/shard_map/all_gather | solution.py:239
  1485.5 28.0 %copy-start.31 = (f32[512,8]{0,1:T(8,128)}, f32[512,8]{0,1:T(8,128)S(1)}, u32[]{:S(2)}) copy-start(f32[512,8]{0,1:T(8,128)S(1)} %select_reduce_fusion) | copy-start | bytes 49156
  1510.0 3.4 copy-start.6
  1510.0 3.4 copy-start.34
  1510.0 3.5 copy-start.37
  1510.0 3.5 copy-start.40
  1513.5 2.2 copy-start.50
  1518.7 282.3 %all-reduce.7.cloned.1.call-start = ((), (), s32[]{:S(2)}) async-start(), calls=%async_computation.14 | async-start | bytes 4194304 | tf_op jit(solution)/shard_map/psum | solution.py:273
  1610.6 2.6 copy-start.4
  1615.7 2.0 copy-start.2
  1632.1 4.7 copy-start.3
  1639.2 2.6 copy-start.4
  1644.3 2.0 copy-start.2
  1660.7 4.7 copy-start.3
  1667.8 2.6 copy-start.4
  1672.9 2.0 copy-start.2
  1689.2 4.7 copy-start.3
  1696.3 2.6 copy-start.4
  1701.5 2.0 copy-start.2
  1717.8 4.7 copy-start.3
  1725.1 2.5 copy-start.19
  1727.6 3.0 copy-start.16
  1727.6 2.1 copy-start.21
  1730.8 2.1 copy-start.20
  1734.1 2.2 copy-start.15
  1734.1 2.7 copy-start.53
  1738.9 164.4 %reduce-scatter.9.cloned.1.call-start = ((), (), s32[]{:S(2)}) async-start(), calls=%async_computation.12 | async-start | bytes 7208960 | tf_op jit(solution)/shard_map/reduce_scatter | solution.py:217
  1752.1 256.2 %reduce-scatter.11.cloned.1.call-start = ((), (), s32[]{:S(2)}) async-start(), calls=%async_computation.13 | async-start | bytes 7208960 | tf_op jit(solution)/shard_map/reduce_scatter | solution.py:220
  1764.7 348.7 %reduce-scatter.7.cloned.1.call-start = ((), (), s32[]{:S(2)}) async-start(), calls=%async_computation.11 | async-start | bytes 7208960 | tf_op jit(solution)/shard_map/reduce_scatter | solution.py:214
  1777.8 415.3 %reduce-scatter.5.cloned.1.call-start = ((), (), s32[]{:S(2)}) async-start(), calls=%async_computation.10 | async-start | bytes 5242880 | tf_op jit(solution)/shard_map/reduce_scatter | solution.py:266
  1801.0 6.3 copy-start.30
  1906.4 286.7 %copy-start.43 = (f32[1024]{0:T(1024)S(1)}, f32[1024]{0:T(1024)}, u32[]{:S(2)}) copy-start(f32[1024]{0:T(1024)} %param.25) | copy-start | bytes 12292
  2011.6 184.1 %copy-start.51 = (f32[1024]{0:T(1024)S(1)}, f32[1024]{0:T(1024)}, u32[]{:S(2)}) copy-start(f32[1024]{0:T(1024)} %get-tuple-element.280) | copy-start | bytes 12292
  2011.6 225.8 %copy-start.7 = (f32[512,1024]{1,0:T(8,128)S(1)}, f32[512,1024]{1,0:T(8,128)}, u32[]{:S(2)}) copy-start(f32[512,1024]{1,0:T(8,128)} %copy-done.5) | copy-start | bytes 6291460
  2011.6 225.8 %copy-start.38 = (f32[1024]{0:T(1024)S(1)}, f32[1024]{0:T(1024)}, u32[]{:S(2)}) copy-start(f32[1024]{0:T(1024)} %param.31) | copy-start | bytes 12292
  2011.6 225.8 %copy-start.41 = (f32[512]{0:T(512)S(1)}, f32[512]{0:T(512)}, u32[]{:S(2)}) copy-start(f32[512]{0:T(512)} %copy-done.39) | copy-start | bytes 6148
  2011.6 225.8 %copy-start.47 = (f32[512]{0:T(512)S(1)}, f32[512]{0:T(512)}, u32[]{:S(2)}) copy-start(f32[512]{0:T(512)} %copy-done.46) | copy-start | bytes 6148
  (13 other events, 15.9 us)
Sparse Core Ops, SparseCore 0:
  1135.0 157.6 all-reduce.4
  1518.8 77.9 all-gather.1
  1739.0 60.3 all-reduce.6
  1801.7 101.5 reduce-scatter.8
  1905.5 102.7 reduce-scatter.10
  2010.6 102.7 reduce-scatter.6
  2115.8 77.2 reduce-scatter.4
where the time goes:
time: 2260 us; the launch traced here: 2250 us
  local copies, waits for them, and re-layouts  1160 us (51%)
  waiting for transfers between devices  657 us (29%)
  matrix products  286 us (13%)
  other arithmetic  55.8 us (2%)
  blocking collectives  55.5 us (2%)
    gather x1, local copies, waits for them, and re-layouts, body(): table = rel_bucket[positions[None, :] - positions[:, None] + length - 1]  1040 us
    psum x1, waiting for transfers between devices, body(): lax.psum(partial_value.astype(jnp.bfloat16), 'head').astype(jnp.float32)  129 us
    dot_general x19, matrix products, contract(): lax.dot_general(left, right, (((left_dim,), (right_dim,)), ((), ())), pre...  119 us
    reduce_scatter x1, waiting for transfers between devices, body(): lax.psum_scatter(grad_down[None].astype(jnp.bfloat16), 'head', scatter_di...  102 us
    reduce_scatter x1, waiting for transfers between devices, body(): lax.psum_scatter(grad_gate[None].astype(jnp.bfloat16), 'head', scatter_di...  102 us
    reduce_scatter x1, waiting for transfers between devices, body(): lax.psum_scatter(grad_up[None].astype(jnp.bfloat16), 'head', scatter_dime...  94.8 us
    all_gather x1, waiting for transfers between devices, body(): piece = lax.all_gather(grad_branch, 'head', axis=0, tiled=True)  78.1 us
    reduce_scatter x1, waiting for transfers between devices, body(): lax.psum_scatter(total.astype(jnp.bfloat16), 'head', scatter_dimension=0,...  76.6 us
  transfers between devices with their start and end apart: 11, of which 10 were waited for; matrix products, arithmetic and copies ran while one was open for 6% of the time, Pallas kernels for 0%

commit v1 on v0

v1 whole, which is shorter than its diff:
```python
import functools

import jax
import jax.numpy as jnp
from jax import lax
from jax.experimental import pallas as pl
from jax.experimental.pallas import tpu as pltpu
from jax.sharding import PartitionSpec as P

EPS = 1e-06
SCALE = 0.125
HIGH = lax.Precision.HIGHEST
TILE = 128
BF = jnp.bfloat16
F32 = jnp.float32
VMEM_LIMIT = 48 << 20


def rms_norm(value, gain):
    return value * lax.rsqrt(jnp.mean(value * value, axis=-1, keepdims=True) + EPS) * gain


def geglu(gate, up_part):
    return jax.nn.gelu(gate) * up_part


def contract(left, right, left_dim, right_dim, precision=None):
    return lax.dot_general(
        left,
        right,
        (((left_dim,), (right_dim,)), ((), ())),
        precision=precision,
        preferred_element_type=jnp.float32,
    )


def route_slots(chosen, ranks, experts, capacity):
    count = chosen.shape[0]
    keys = jnp.concatenate([ranks, ranks + count])
    wanted = jnp.concatenate([chosen[:, 0], chosen[:, 1]])
    smaller = (wanted[:, None] == wanted[None, :]) & (keys[None, :] < keys[:, None])
    place = jnp.sum(smaller.astype(jnp.int32), axis=1)
    dest = jnp.where(place < capacity, wanted * capacity + place, experts * capacity)
    return jnp.stack([dest[:count], dest[count:]], axis=1)


def skew_kernel(line_ref, table_ref):
    heads, rows, cols = table_ref.shape
    row = lax.broadcasted_iota(jnp.int32, (rows, cols), 0)
    for h in range(heads):
        value = jnp.broadcast_to(line_ref[h], (rows, cols))
        shift = 1
        while shift < rows:
            value = jnp.where((row & shift) != 0, pltpu.roll(value, shift, 1), value)
            shift *= 2
        table_ref[h] = value


def unskew_kernel(table_ref, line_ref):
    heads, rows, cols = table_ref.shape
    row = lax.broadcasted_iota(jnp.int32, (rows, cols), 0)
    for h in range(heads):
        value = table_ref[h]
        shift = 1
        while shift < rows:
            value = jnp.where((row & shift) != 0, pltpu.roll(value, cols - shift, 1), value)
            shift *= 2
        line_ref[h] = jnp.sum(value, axis=0, keepdims=True)


def skew(line):
    heads, cols = line.shape
    return pl.pallas_call(
        skew_kernel,
        out_shape=jax.ShapeDtypeStruct((heads, TILE, cols), F32),
        compiler_params=pltpu.CompilerParams(vmem_limit_bytes=VMEM_LIMIT),
        name="skew",
    )(line[:, None, :])


def unskew(table):
    heads, _, cols = table.shape
    return pl.pallas_call(
        unskew_kernel,
        out_shape=jax.ShapeDtypeStruct((heads, 1, cols), F32),
        compiler_params=pltpu.CompilerParams(vmem_limit_bytes=VMEM_LIMIT),
        name="unskew",
    )(table)[:, 0]


def lanes_of(shape, half, part):
    lane = lax.broadcasted_iota(jnp.int32, shape, 1)
    return (lane >= half) if part else (lane < half)


def attend_fwd_kernel(seq_ref, q_ref, k_ref, v_ref, table_ref, out_ref, probs_ref, acc_ref):
    del seq_ref
    length, lanes = q_ref.shape
    half = lanes // 2
    chunk = 2 * TILE
    key = k_ref[...]
    value_t = v_ref[...].T
    for part in range(2):
        query = jnp.where(lanes_of((length, lanes), half, part), q_ref[...] * SCALE, 0).astype(BF)
        for c in range(length // chunk):
            cols = slice(c * chunk, (c + 1) * chunk)
            scores = contract(key, query[cols], 1, 1)
            pieces = []
            for kb in range(length // TILE):
                at = length - TILE * kb + chunk * c
                pieces.append(
                    scores[kb * TILE : (kb + 1) * TILE] + table_ref[part, :, at : at + chunk]
                )
            scores = jnp.concatenate(pieces, axis=0)
            top = jnp.max(scores, axis=0, keepdims=True)
            shifted = jnp.exp(scores - top)
            total = jnp.sum(shifted, axis=0, keepdims=True)
            probs = (shifted * (1.0 / total)).astype(BF)
            probs_ref[part, :, cols] = probs
            acc_ref[part * half : (part + 1) * half, cols] = jnp.dot(
                value_t[part * half : (part + 1) * half], probs, preferred_element_type=F32
            )
    out_ref[...] = acc_ref[...].T.astype(BF)


def attend_fwd(seq, qkv, table, length):
    heads, _, width = table.shape
    columns = qkv.shape[1] // 3
    pairs = heads // 2
    lanes = columns // pairs
    spec = [
        pl.BlockSpec((length, lanes), lambda p, s, j=j: (s[0], j * pairs + p)) for j in range(3)
    ]
    return pl.pallas_call(
        attend_fwd_kernel,
        out_shape=(
            jax.ShapeDtypeStruct((length, columns), BF),
            jax.ShapeDtypeStruct((heads, length, length), BF),
        ),
        grid_spec=pltpu.PrefetchScalarGridSpec(
            num_scalar_prefetch=1,
            grid=(pairs,),
            in_specs=spec + [pl.BlockSpec((2, TILE, width), lambda p, s: (p, 0, 0))],
            out_specs=[
                pl.BlockSpec((length, lanes), lambda p, s: (0, p)),
                pl.BlockSpec((2, length, length), lambda p, s: (p, 0, 0)),
            ],
            scratch_shapes=[pltpu.VMEM((lanes, length), F32)],
        ),
        compiler_params=pltpu.CompilerParams(vmem_limit_bytes=VMEM_LIMIT),
        cost_estimate=pl.CostEstimate(
            flops=heads * 8 * length * length * lanes,
            bytes_accessed=heads * length * length * 2 + 8 * length * columns,
            transcendentals=heads * length * length,
        ),
        name="attend_fwd",
    )(seq, qkv, qkv, qkv, table)


def attend_bwd_kernel(
    seq_ref, q_ref, k_ref, v_ref, grad_ref, probs_ref, sums_in_ref, out_ref, sums_ref, acc_ref
):
    del seq_ref
    length, lanes = q_ref.shape
    half = lanes // 2
    chunk = 2 * TILE
    pair = pl.program_id(0)
    columns = out_ref.shape[1] // 3
    key_t = k_ref[...].T
    value = v_ref[...]
    sums_ref[...] = sums_in_ref[...]
    grad_keys, grad_values = [], []
    for part in range(2):
        mask = lanes_of((length, lanes), half, part)
        grad = jnp.where(mask, grad_ref[...], 0).astype(BF)
        grad_key = jnp.zeros((length, lanes), F32)
        grad_value = jnp.zeros((length, lanes), F32)
        for c in range(length // chunk):
            cols = slice(c * chunk, (c + 1) * chunk)
            grad_probs = contract(value, grad[cols], 1, 1)
            probs_low = probs_ref[part, :, cols]
            probs = probs_low.astype(F32)
            delta = jnp.sum(probs * grad_probs, axis=0, keepdims=True)
            grad_scores = (probs * (grad_probs - delta)).astype(BF)
            grad_value += jnp.dot(probs_low, grad_ref[cols, :], preferred_element_type=F32)
            grad_key += jnp.dot(grad_scores, q_ref[cols, :], preferred_element_type=F32)
            acc_ref[part * half : (part + 1) * half, cols] = jnp.dot(
                key_t[part * half : (part + 1) * half], grad_scores, preferred_element_type=F32
            )
            for kb in range(length // TILE):
                at = length - TILE * kb + chunk * c
                sums_ref[part, :, at : at + chunk] += grad_scores[
                    kb * TILE : (kb + 1) * TILE
                ].astype(F32)
        grad_keys.append(grad_key)
        grad_values.append(grad_value)
    first = lanes_of((length, lanes), half, 0)
    at = pl.multiple_of(pair * lanes, lanes)
    out_ref[:, pl.ds(at, lanes)] = (acc_ref[...].T * SCALE).astype(BF)
    at = pl.multiple_of(columns + pair * lanes, lanes)
    out_ref[:, pl.ds(at, lanes)] = (jnp.where(first, *grad_keys) * SCALE).astype(BF)
    at = pl.multiple_of(2 * columns + pair * lanes, lanes)
    out_ref[:, pl.ds(at, lanes)] = jnp.where(first, *grad_values).astype(BF)


def attend_bwd(seq, qkv, grad, probs, sums, length):
    heads, _, width = sums.shape
    columns = qkv.shape[1] // 3
    pairs = heads // 2
    lanes = columns // pairs
    spec = [
        pl.BlockSpec((length, lanes), lambda p, s, j=j: (s[0], j * pairs + p)) for j in range(3)
    ]
    sums_spec = pl.BlockSpec((2, TILE, width), lambda p, s: (p, 0, 0))
    return pl.pallas_call(
        attend_bwd_kernel,
        out_shape=(
            jax.ShapeDtypeStruct((length, 3 * columns), BF),
            jax.ShapeDtypeStruct(sums.shape, F32),
        ),
        grid_spec=pltpu.PrefetchScalarGridSpec(
            num_scalar_prefetch=1,
            grid=(pairs,),
            in_specs=spec
            + [
                pl.BlockSpec((length, lanes), lambda p, s: (0, p)),
                pl.BlockSpec((2, length, length), lambda p, s: (p, 0, 0)),
                sums_spec,
            ],
            out_specs=[pl.BlockSpec((length, 3 * columns), lambda p, s: (0, 0)), sums_spec],
            scratch_shapes=[pltpu.VMEM((lanes, length), F32)],
        ),
        compiler_params=pltpu.CompilerParams(vmem_limit_bytes=VMEM_LIMIT),
        cost_estimate=pl.CostEstimate(
            flops=heads * 16 * length * length * lanes,
            bytes_accessed=heads * length * length * 2 + 16 * length * columns,
            transcendentals=0,
        ),
        name="attend_bwd",
    )(seq, qkv, qkv, qkv, grad, probs, sums)


def expert_forward(rows, gate_w, up_w, grad_unscaled, slot_gates):
    gate_pre = jnp.dot(rows, gate_w, preferred_element_type=F32)
    up_pre = jnp.dot(rows, up_w, preferred_element_type=F32)
    hidden, pull = jax.vjp(geglu, gate_pre, up_pre)
    grad_gate_pre, grad_up_pre = pull(grad_unscaled * slot_gates)
    return hidden.astype(BF), grad_gate_pre.astype(BF), grad_up_pre.astype(BF)


def body(
    block_input,
    cotangent,
    expert_ids,
    priority,
    rel_bucket,
    norm1_gain,
    w_query,
    w_key,
    w_value,
    w_out,
    pos_bias,
    norm2_gain,
    w_router,
    w_gate,
    w_up,
    w_down,
):
    group_rows, width = block_input.shape
    own_rows = cotangent.shape[0]
    buckets, heads_here = pos_bias.shape
    head_cols = w_query.shape[1]
    length = (rel_bucket.shape[0] + 1) // 2
    sequences = group_rows // length
    experts = w_router.shape[1]
    capacity = 5 * 2 * own_rows // (4 * experts)
    slot_count = experts * capacity
    replicas = lax.axis_size("head")
    groups = lax.axis_size("dp")
    me = lax.axis_index("head")
    far = replicas // 2
    far_perm = [(i, i ^ far) for i in range(replicas)]
    stepwise = own_rows == length and sequences == replicas

    def hop(value, r):
        return lax.ppermute(value, "head", [(i, i ^ r) for i in range(replicas)])

    def exchange(value):
        parts = value.reshape(experts, capacity, -1)
        return lax.all_to_all(parts, "dp", split_axis=0, concat_axis=0, tiled=True).reshape(
            slot_count, -1
        )

    dest = route_slots(expert_ids, priority[0], experts, capacity)
    dest_far = lax.ppermute(dest, "head", far_perm)
    slot_range = jnp.arange(slot_count, dtype=jnp.int32)[None, :]
    picks = [(dest[:, k : k + 1] == slot_range).astype(BF) for k in range(2)]
    both = picks[0] + picks[1]
    both_far = sum((dest_far[:, k : k + 1] == slot_range).astype(BF) for k in range(2))

    down_w, gate_w, up_w = w_down[0], w_gate[0], w_up[0]
    cot_here = exchange(contract(both, cotangent, 0, 0).astype(BF))
    cot_far_own = lax.ppermute(cotangent, "head", far_perm)
    cot_far = exchange(contract(both_far, cot_far_own, 0, 0).astype(BF))
    unscaled_here = contract(cot_here, down_w, 1, 1)
    unscaled_far = contract(cot_far, down_w, 1, 1)

    dp_at = lax.axis_index("dp")
    out_rows = head_cols // groups
    piece = lax.dynamic_slice_in_dim(w_out, dp_at * out_rows, out_rows, 0)
    w_out_all = lax.all_gather(piece, ("head", "dp"), axis=0, tiled=True)
    w_qkv = jnp.concatenate([w_query, w_key, w_value], axis=1)
    qkv_rows = width // groups
    piece = lax.dynamic_slice_in_dim(w_qkv, dp_at * qkv_rows, qkv_rows, 0)
    w_qkv_all = lax.all_gather(piece, ("head", "dp"), axis=0, tiled=True)
    if stepwise:
        order = [me ^ r for r in range(replicas)]
    else:
        order = list(range(replicas))
    w_out_all = w_out_all.reshape(replicas, head_cols, width)
    w_qkv_all = w_qkv_all.reshape(replicas, width, 3 * head_cols)
    w_out_cat = jnp.concatenate(
        [lax.dynamic_index_in_dim(w_out_all, o, 0, keepdims=False) for o in order], axis=0
    )

    inputs_all = block_input.astype(F32)
    normed = rms_norm(inputs_all, norm1_gain).astype(BF)
    qkv = jnp.dot(normed, w_qkv, preferred_element_type=F32).astype(BF)
    line = (rel_bucket[::-1][None, :] == jnp.arange(buckets, dtype=jnp.int32)[:, None]).astype(F32)
    line = jnp.pad(line, ((0, 0), (1, 0)))
    table = skew(contract(pos_bias, line, 0, 0, HIGH))
    kept = {}
    if stepwise:
        blocks = [None] * replicas
        for r in reversed(range(replicas)):
            attended_seq, probs = attend_fwd(order[r].reshape(1), qkv, table, length)
            kept[r] = probs
            blocks[r] = hop(attended_seq, r) if r else attended_seq
    else:
        seqs = []
        for s in range(sequences):
            attended_seq, kept[s] = attend_fwd(jnp.full((1,), s, jnp.int32), qkv, table, length)
            seqs.append(attended_seq)
        attended_all = jnp.concatenate(seqs, axis=0).reshape(replicas, own_rows, head_cols)
        attended_all = lax.all_to_all(attended_all, "head", split_axis=0, concat_axis=0, tiled=True)
        blocks = [attended_all[i] for i in range(replicas)]
    attended = jnp.concatenate(blocks, axis=1)

    branch = jnp.dot(attended, w_out_cat, preferred_element_type=F32)
    start_own = me * own_rows
    inputs_own = lax.dynamic_slice_in_dim(block_input, start_own, own_rows, 0).astype(F32)
    mixed = inputs_own + branch
    normed2_full, norm2_pull = jax.vjp(rms_norm, mixed, norm2_gain)
    normed2 = normed2_full.astype(BF)
    logits = jnp.dot(normed2, w_router, preferred_element_type=F32)
    expert_range = jnp.arange(experts, dtype=jnp.int32)
    chosen = (expert_ids[:, :, None] == expert_range[None, None, :]).astype(F32)
    gates = jax.nn.softmax(jnp.sum(chosen * logits[:, None, :], axis=2), axis=-1)

    def slot_gates_of(places, values):
        terms = sum(
            jnp.where(places[:, k : k + 1] == slot_range, values[:, k : k + 1], 0.0)
            for k in range(2)
        )
        return jnp.sum(terms, axis=0)

    rows_here = exchange(contract(both, normed2, 0, 0).astype(BF))
    gates_here = exchange(slot_gates_of(dest, gates))
    normed2_far = lax.ppermute(normed2, "head", far_perm)
    gates_far_own = lax.ppermute(gates, "head", far_perm)
    rows_far = exchange(contract(both_far, normed2_far, 0, 0).astype(BF))
    gates_far = exchange(slot_gates_of(dest_far, gates_far_own))

    hidden_here, ggp_here, gup_here = expert_forward(
        rows_here, gate_w, up_w, unscaled_here, gates_here
    )
    returned = jnp.dot(hidden_here, down_w, preferred_element_type=F32).astype(BF)
    came_back = exchange(returned)
    grad_routed = (contract(ggp_here, gate_w, 1, 1) + contract(gup_here, up_w, 1, 1)).astype(BF)
    grad_back = exchange(grad_routed)
    hidden_far, ggp_far, gup_far = expert_forward(rows_far, gate_w, up_w, unscaled_far, gates_far)
    scaled_here = (cot_here.astype(F32) * gates_here).astype(BF)
    scaled_far = (cot_far.astype(F32) * gates_far).astype(BF)

    low = me % far
    high = me // far

    def reduced(lefts, rights):
        rows = lefts[0].shape[1] // replicas

        def part(at):
            return sum(
                contract(lax.dynamic_slice_in_dim(left, at * rows, rows, 1), right, 0, 0)
                for left, right in zip(lefts, rights)
            )

        if far == 2:
            sent = hop(part(high * far + (1 - low)).astype(BF), 1)
            return (part(me) + sent.astype(F32))[None]
        whole = jnp.concatenate([part(high * far + i) for i in range(far)], axis=0).astype(BF)
        member = [[h * far + i for i in range(far)] for h in range(2)]
        return lax.psum_scatter(
            whole, "head", scatter_dimension=0, axis_index_groups=member, tiled=True
        ).astype(F32)[None]

    grad_down_w = reduced((hidden_here, hidden_far), (scaled_here, scaled_far))
    grad_gate_w = reduced((rows_here, rows_far), (ggp_here, ggp_far))
    grad_up_w = reduced((rows_here, rows_far), (gup_here, gup_far))

    chosen_rows = [jnp.dot(pick, came_back, preferred_element_type=F32) for pick in picks]
    output = mixed + sum(gates[:, k : k + 1] * chosen_rows[k] for k in range(2))
    grad_output = cotangent.astype(F32)
    grad_gates = jnp.stack([jnp.sum(grad_output * rows, axis=1) for rows in chosen_rows], axis=1)
    grad_normed2 = jnp.dot(both, grad_back, preferred_element_type=F32)
    grad_picked = gates * (grad_gates - jnp.sum(gates * grad_gates, axis=1, keepdims=True))
    grad_logits = jnp.sum(chosen * grad_picked[:, :, None], axis=1)
    grad_normed2 = grad_normed2 + contract(grad_logits, w_router.astype(F32), 1, 1, HIGH)
    grad_router = contract(normed2.astype(F32), grad_logits, 0, 0, HIGH)
    grad_mixed, grad_norm2 = norm2_pull(grad_normed2)
    grad_mixed = grad_mixed + grad_output
    grad_branch = grad_mixed.astype(BF)

    grad_wout = contract(attended, grad_branch, 0, 0).astype(BF)
    grad_wout = grad_wout.reshape(replicas, groups, out_rows, width)
    grad_wout = lax.psum_scatter(grad_wout, "dp", scatter_dimension=1, tiled=True)[:, 0]
    if stepwise:
        grad_wout = sum(
            (hop(grad_wout[r], r) if r else grad_wout[r]).astype(F32) for r in range(replicas)
        ).astype(BF)
    else:
        grad_wout = lax.psum_scatter(
            grad_wout.reshape(replicas * out_rows, width), "head", scatter_dimension=0, tiled=True
        )
    grad_out_proj = lax.all_gather(grad_wout, "dp", axis=0, tiled=True).astype(F32)

    grad_heads = contract(grad_branch, w_out_cat, 1, 1).astype(BF)
    sums = jnp.zeros((heads_here, TILE, 2 * length), F32)
    grad_blocks = [grad_heads[:, i * head_cols : (i + 1) * head_cols] for i in range(replicas)]
    grad_total = None
    weight_terms = []
    if stepwise:
        arrived = [hop(grad_blocks[r], r) if r else grad_blocks[0] for r in range(replicas)]
        for r in (0, 2, 3, 1):
            grad_qkv, sums = attend_bwd(order[r].reshape(1), qkv, arrived[r], kept[r], sums, length)
            normed_seq = lax.dynamic_slice_in_dim(normed, order[r] * length, length, 0)
            weight_terms.append(contract(normed_seq, grad_qkv, 0, 0))
            mine = hop(grad_qkv, r) if r else grad_qkv
            weight = lax.dynamic_index_in_dim(w_qkv_all, order[r], 0, keepdims=False)
            term = contract(mine, weight, 1, 1)
            grad_total = term if grad_total is None else grad_total + term
        grad_normed = grad_total
        grad_qkv_w = sum(weight_terms)
    else:
        stacked = jnp.stack(grad_blocks, axis=0)
        stacked = lax.all_to_all(stacked, "head", split_axis=0, concat_axis=0, tiled=True)
        stacked = stacked.reshape(group_rows, head_cols)
        seqs = []
        for s in range(sequences):
            grad_seq = stacked[s * length : (s + 1) * length]
            grad_qkv, sums = attend_bwd(
                jnp.full((1,), s, jnp.int32), qkv, grad_seq, kept[s], sums, length
            )
            seqs.append(grad_qkv)
        grad_qkv = jnp.concatenate(seqs, axis=0)
        grad_qkv_w = contract(normed, grad_qkv, 0, 0)
        grad_qkv = lax.all_to_all(
            grad_qkv.reshape(replicas, own_rows, 3 * head_cols),
            "head",
            split_axis=0,
            concat_axis=0,
            tiled=True,
        )
        grad_normed = sum(contract(grad_qkv[i], w_qkv_all[i], 1, 1) for i in range(replicas))

    _, norm1_pull = jax.vjp(rms_norm, inputs_own, norm1_gain)
    grad_first, grad_norm1 = norm1_pull(grad_normed)
    grad_input = grad_mixed + grad_first
    grad_bias = contract(unskew(sums), line, 1, 1, HIGH)
    grad_qkv_w, grad_bias = lax.psum((grad_qkv_w.astype(BF), grad_bias), "dp")
    grad_qkv_w = grad_qkv_w.astype(F32)
    grad_norm1, grad_norm2, grad_router = lax.psum(
        (grad_norm1, grad_norm2, grad_router), ("dp", "head")
    )
    return (
        output,
        grad_input,
        grad_norm1,
        grad_qkv_w[:, :head_cols],
        grad_qkv_w[:, head_cols : 2 * head_cols],
        grad_qkv_w[:, 2 * head_cols :],
        grad_out_proj,
        jnp.transpose(grad_bias),
        grad_norm2,
        grad_router,
        grad_gate_w,
        grad_up_w,
        grad_down_w,
    )


def solution(mesh):
    placed = (
        P("dp", None),
        P(("dp", "head"), None),
        P(("dp", "head"), None),
        P(("dp", "head"), None),
        P(),
        P(),
        P(None, "head"),
        P(None, "head"),
        P(None, "head"),
        P("head", None),
        P(None, "head"),
        P(),
        P(),
        P("dp", None, None),
        P("dp", None, None),
        P("dp", None, None),
    )
    return jax.shard_map(
        body,
        mesh=mesh,
        in_specs=placed,
        out_specs=(
            P(("dp", "head"), None),
            P(("dp", "head"), None),
            P(),
            P(None, "head"),
            P(None, "head"),
            P(None, "head"),
            P("head", None),
            P(None, "head"),
            P(),
            P(),
            P("dp", "head", None),
            P("dp", "head", None),
            P("dp", "head", None),
        ),
        check_vma=False,
    )
```

time: 2260 us -> 796 us (0.35)
  local copies, waits for them, and re-layouts: 1160 us -> 26.9 us
  waiting for transfers between devices: 657 us -> 259 us
  Pallas kernels: 0 us -> 54.4 us
  blocking collectives: 55.5 us -> 97.1 us
  other arithmetic: 55.8 us -> 18.1 us
  starting transfers between devices: 18 us -> 55.2 us
    gather x7 -> x0, local copies, waits for them, and re-layouts: 1050 us -> none  [the longest x1 1040 us: body(): table = rel_bucket[positions[None, :] - positions[:, None] + length - 1]]
    reduce_scatter x4 -> x0, waiting for transfers between devices: 375 us -> none  [the longest x1 102 us: body(): lax.psum_scatter(grad_down[None].astype(jnp.bfloat16), 'head', scatter_di...]
    ppermute x0 -> x19, waiting for transfers between devices: none -> 192 us  [the longest x15 123 us: hop(): return lax.ppermute(value, 'head', [(i, i ^ r) for i in range(replicas)])]
    psum x2 -> x1, waiting for transfers between devices: 129 us -> 0.01 us  [body(): grad_qkv_w, grad_bias = lax.psum((grad_qkv_w.astype(BF), grad_bias), 'dp')]
    dot_general x42 -> x11, matrix products: 168 us -> 101 us  [the longest x2 44.2 us: expert_forward(): up_pre = jnp.dot(rows, up_w, preferred_element_type=F32)]
    all_gather x1 -> x2, waiting for transfers between devices: 78.1 us -> 15.2 us  [the longest x1 15.2 us: body(): w_out_all = lax.all_gather(piece, ('head', 'dp'), axis=0, tiled=True)]
    pallas_call x0 -> x10, Pallas kernels: none -> 54.4 us  [the longest x4 25.5 us: attend_bwd(): pl.pallas_call(attend_bwd_kernel, out_shape=(jax.ShapeDtypeStruct((length...]
    dot_general x19 -> x34, matrix products: 119 us -> 163 us  [contract(): lax.dot_general(left, right, (((left_dim,), (right_dim,)), ((), ())), pre...]
  transfers between devices with their start and end apart: 11 -> 29, of which waited for: 10 -> 15; matrix products, arithmetic and copies ran while one was open for 6% -> 31% of each run, Pallas kernels for 0% -> 7%
where the time goes in v1:
time: 796 us; the launch traced here: 791 us
  matrix products  265 us (33%)
  waiting for transfers between devices  259 us (33%)
  blocking collectives  97.1 us (12%)
  starting transfers between devices  55.2 us (7%)
  Pallas kernels  54.4 us (7%)
  local copies, waits for them, and re-layouts  26.9 us (3%)
  other arithmetic  18.1 us (2%)
  between operations  15.4 us (2%)
    dot_general x34, matrix products, contract(): lax.dot_general(left, right, (((left_dim,), (right_dim,)), ((), ())), pre...  163 us
    ppermute x15, waiting for transfers between devices, hop(): return lax.ppermute(value, 'head', [(i, i ^ r) for i in range(replicas)])  123 us
    ppermute x1, waiting for transfers between devices, body(): dest_far = lax.ppermute(dest, 'head', far_perm)  65.9 us
    all_to_all x7, waiting for transfers between devices, exchange(): lax.all_to_all(parts, 'dp', split_axis=0, concat_axis=0, tiled=True)  51.3 us
    dot_general x2, matrix products, expert_forward(): up_pre = jnp.dot(rows, up_w, preferred_element_type=F32)  44.2 us
    psum x1, blocking collectives, body(): lax.psum((grad_norm1, grad_norm2, grad_router), ('dp', 'head'))  39.5 us
    all_to_all x1, blocking collectives, exchange(): lax.all_to_all(parts, 'dp', split_axis=0, concat_axis=0, tiled=True)  34.9 us
    all_to_all x7, starting transfers between devices, exchange(): lax.all_to_all(parts, 'dp', split_axis=0, concat_axis=0, tiled=True)  29.2 us
  transfers between devices with their start and end apart: 29, of which 15 were waited for; matrix products, arithmetic and copies ran while one was open for 31% of the time, Pallas kernels for 7%

profile of v1, /device:TPU:0, one launch (start us, length us, event | category | flops | bytes accessed | tf_op | source)
XLA Modules:
  0.0 791.0 jit_solution(15423019675073231827)
XLA Ops:
  12.6 3.7 skew.1.table_ref
  18.0 3.2 fusion.14
  22.8 4.8 convolution_convert_fusion.4.q_ref.k_ref.v_ref
  27.7 5.5 attend_fwd.5
  37.6 5.5 attend_fwd.6
  47.0 5.5 attend_fwd.7
  53.8 5.7 attend_fwd.4
  61.0 4.7 collective-permute-done.1
  66.7 15.2 %all-gather.3.cloned.1.call-done = bf16[1024,1024]{1,0:T(8,128)(2,1)} async-done(((bf16[32,1024]{1,0:T(8,128)(2,1)}), bf16[1024,1024]{1,0:T(8,128)(2,1)}) %all-gather.3.cloned.1.call-update) | async-done | bytes 2097168 | tf_op jit(solution)/shard_map/all_gather | solution.py:311
  83.7 3.3 multiply_reduce_fusion.2
  89.3 34.9 %all_to_all.40 = bf16[8,160,1024]{2,1,0:T(8,128)(2,1)S(1)} all-to-all(bf16[8,160,1024]{2,1,0:T(8,128)(2,1)S(1)} %bitcast.175), channel_id=1, replica_groups=mesh['dp'=8,'head'=4] {'dp'}, dimensions={0} | all-to-all | bytes 5242880 | tf_op jit(solution)/shard_map/all_to_all | solution.py:290
  124.3 10.3 %fusion.31 = f32[1280,2816]{1,0:T(8,128)} fusion(bf16[1280,1024]{1,0:T(8,128)(2,1)S(1)} %bitcast.164, bf16[1,1024,2816]{2,1,0:T(8,128)(2,1)S(1)} %bitcast.208), kind=kOutput, calls=%fused_computation.45 | convolution fusion | flops 7381975040 | bytes 22806528 | tf_op jit(solution)/shard_map/dot_general | solution.py:244
  134.5 19.2 %multiply_convert_fusion.3 = (bf16[1280,2816]{1,0:T(8,128)(2,1)}, f32[1280,2816]{1,0:T(8,128)}) fusion(f32[1280,2816]{1,0:T(8,128)} %fusion.31, bf16[1280,1024]{1,0:T(8,128)(2,1)S(1)} %bitcast.165, bf16[1,1024,2816]{2,1,0:T(8,128)(2,1)} %param.30), kind=kOutput, calls=%fused_computation.23 | convolution fusion | flops 7418019840 | bytes 44433408 | tf_op jit(solution)/shard_map/dot_general | solution.py:245
  153.7 10.9 %fusion.37 = bf16[1280,1024]{1,0:T(8,128)(2,1)} fusion(bf16[1280,2816]{1,0:T(8,128)(2,1)} %get-tuple-element.91, bf16[1,2816,1024]{2,1,0:T(8,128)(2,1)S(1)} %bitcast.210), kind=kOutput, calls=%fused_computation.62 | convolution fusion | flops 7383285760 | bytes 15597568 | tf_op jit(solution)/shard_map/dot_general | solution.py:377
  164.6 4.4 all-to-all-start.1
  175.2 4.6 convolution_convert_fusion.2
  179.8 65.9 %collective-permute-done.12 = s32[512,2]{0,1:T(2,128)S(1)} collective-permute-done((s32[512,2]{0,1:T(2,128)S(1)}, s32[512,2]{0,1:T(2,128)S(1)}, u32[]{:S(2)}, u32[]{:S(2)}) %collective-permute-start.12) | collective-permute-done | bytes 4128 | tf_op jit(solution)/shard_map/ppermute | solution.py:295
  245.7 4.6 convolution_convert_fusion.1
  250.3 4.5 all-to-all-start.5
  259.3 3.4 fusion.42
  262.7 5.5 fusion.46
  269.7 22.9 %all-to-all-done.5 = bf16[8,160,1024]{2,1,0:T(8,128)(2,1)} async-done(((bf16[8,160,1024]{2,1,0:T(8,128)(2,1)}), bf16[8,160,1024]{2,1,0:T(8,128)(2,1)}, u32[]{:S(2)}, u32[]{:S(2)}) %all-to-all-start.5) | async-done | bytes 2621472 | tf_op jit(solution)/shard_map/all_to_all | solution.py:290
  292.7 3.3 all-to-all-start.3
  296.0 4.6 convolution_convert_fusion
  300.7 4.6 all-to-all-start.2
  305.2 14.0 %fusion.27 = f32[1280,2816]{1,0:T(8,128)} fusion(bf16[1280,1024]{1,0:T(8,128)(2,1)} %bitcast.43, bf16[1,1024,2816]{2,1,0:T(8,128)(2,1)} %param.29), kind=kOutput, calls=%fused_computation.41 | convolution fusion | flops 7381975040 | bytes 22806528 | tf_op jit(solution)/shard_map/dot_general | solution.py:244
  320.4 3.5 collective-permute-done.15
  325.4 14.8 %all-to-all-done.2 = bf16[8,160,1024]{2,1,0:T(8,128)(2,1)} async-done(((bf16[8,160,1024]{2,1,0:T(8,128)(2,1)}), bf16[8,160,1024]{2,1,0:T(8,128)(2,1)}, u32[]{:S(2)}, u32[]{:S(2)}) %all-to-all-start.2) | async-done | bytes 2621472 | tf_op jit(solution)/shard_map/all_to_all | solution.py:290
  340.2 3.3 all-to-all-start.7
  343.5 25.5 %fusion.6 = (bf16[1280,2816]{1,0:T(8,128)(2,1)}, bf16[1280,2816]{1,0:T(8,128)(2,1)}) fusion(f32[1280,2816]{1,0:T(8,128)} %fusion.31, f32[1280,2816]{1,0:T(8,128)} %get-tuple-element.92, f32[1280]{0:T(1024)S(1)} %mul.378, bf16[1280,1024]{1,0:T(8,128)(2,1)} %bitcast.23, bf16[1,2816,1024]{2,1,0:T(8,128)(2,1)} %param.31), kind=kOutput, calls=%fused_computation.12 | convolution fusion | flops 7472087040 | bytes 51647488 | tf_op jit(solution)/shard_map/dot_general | solution.py:28
  369.0 13.3 %fusion.23 = f32[1280,1024]{1,0:T(8,128)} fusion(bf16[1280,2816]{1,0:T(8,128)(2,1)} %get-tuple-element.62, bf16[1,1024,2816]{2,1,0:T(8,128)(2,1)} %param.30), kind=kOutput, calls=%fused_computation.37 | convolution fusion | flops 7381975040 | bytes 18219008 | tf_op jit(solution)/shard_map/dot_general | solution.py:28
  382.3 3.7 fusion.111
  386.0 3.7 fusion.113
  389.7 3.7 fusion.123
  393.4 4.7 all-to-all-start.6
  398.1 7.0 fusion.121
  405.2 11.6 %add_convert_fusion = bf16[1280,1024]{1,0:T(8,128)(2,1)} fusion(f32[1280,1024]{1,0:T(8,128)} %fusion.23, bf16[1280,2816]{1,0:T(8,128)(2,1)S(1)} %bitcast.161, bf16[1,1024,2816]{2,1,0:T(8,128)(2,1)} %param.29), kind=kOutput, calls=%fused_computation.49 | convolution fusion | flops 7384596480 | bytes 20840448 | tf_op jit(solution)/shard_map/dot_general | solution.py:28
  416.9 13.5 %all-to-all-done.6 = bf16[8,160,1024]{2,1,0:T(8,128)(2,1)} async-done(((bf16[8,160,1024]{2,1,0:T(8,128)(2,1)}), bf16[8,160,1024]{2,1,0:T(8,128)(2,1)}, u32[]{:S(2)}, u32[]{:S(2)}) %all-to-all-start.6) | async-done | bytes 2621472 | tf_op jit(solution)/shard_map/all_to_all | solution.py:290
  430.4 4.4 all-to-all-start.4
  434.9 14.4 %convolution_multiply_fusion = f32[1280,2816]{1,0:T(8,128)} fusion(bf16[1280,1024]{1,0:T(8,128)(2,1)} %bitcast.45, f32[1280]{0:T(1024)S(1)} %mul.422, bf16[1,2816,1024]{2,1,0:T(8,128)(2,1)} %param.31), kind=kOutput, calls=%fused_computation.4 | convolution fusion | flops 7385579520 | bytes 22811648 | tf_op jit(solution)/shard_map/dot_general | solution.py:28
  449.2 25.0 %multiply_convert_fusion = (bf16[1280,2816]{1,0:T(8,128)(2,1)}, bf16[1280,2816]{1,0:T(8,128)(2,1)}, bf16[1280,2816]{1,0:T(8,128)(2,1)S(1)}) fusion(f32[1280,2816]{1,0:T(8,128)} %fusion.27, f32[1280,2816]{1,0:T(8,128)} %convolution_multiply_fusion, bf16[1280,1024]{1,0:T(8,128)(2,1)} %bitcast.43, bf16[1,1024,2816]{2,1,0:T(8,128)(2,1)} %param.30), kind=kOutput, calls=%fused_computation.20 | convolution fusion | flops 7475691520 | bytes 58851328 | tf_op jit(solution)/shard_map/dot_general | solution.py:245
  474.3 5.0 fusion.53
  479.3 5.1 add_convert_fusion.2
  486.0 3.3 fusion.35
  490.0 3.3 fusion.36
  494.8 4.9 fusion.57
  499.7 19.2 %collective-permute-done.18 = bf16[704,1024]{1,0:T(8,128)(2,1)S(1)} collective-permute-done((bf16[704,1024]{1,0:T(8,128)(2,1)S(1)}, bf16[704,1024]{1,0:T(8,128)(2,1)S(1)}, u32[]{:S(2)}, u32[]{:S(2)}) %collective-permute-start.18) | collective-permute-done | bytes 1441824 | tf_op jit(solution)/shard_map/ppermute | solution.py:286
  518.9 6.7 add_bitcast_fusion
  525.6 24.2 %collective-permute-done.16 = bf16[256,2816]{1,0:T(8,128)(2,1)S(1)} collective-permute-done((bf16[256,2816]{1,0:T(8,128)(2,1)S(1)}, bf16[256,2816]{1,0:T(8,128)(2,1)S(1)}, u32[]{:S(2)}, u32[]{:S(2)}) %collective-permute-start.16) | collective-permute-done | bytes 1441824 | tf_op jit(solution)/shard_map/ppermute | solution.py:286
  549.8 4.8 add_bitcast_fusion.2
  554.6 25.6 %collective-permute-done.17 = bf16[256,2816]{1,0:T(8,128)(2,1)S(1)} collective-permute-done((bf16[256,2816]{1,0:T(8,128)(2,1)S(1)}, bf16[256,2816]{1,0:T(8,128)(2,1)S(1)}, u32[]{:S(2)}, u32[]{:S(2)}) %collective-permute-start.17) | collective-permute-done | bytes 1441824 | tf_op jit(solution)/shard_map/ppermute | solution.py:286
  580.2 4.9 add_bitcast_fusion.1
  585.1 3.5 fusion.80
  600.4 6.6 attend_bwd.4
  612.1 9.2 %collective-permute-done.3.grad_ref = bf16[512,256]{1,0:T(8,128)(2,1)S(1)} collective-permute-done((bf16[512,256]{1,0:T(8,128)(2,1)S(1)}, bf16[512,256]{1,0:T(8,128)(2,1)S(1)}, u32[]{:S(2)}, u32[]{:S(2)}) %collective-permute-start.3) | collective-permute-done | bytes 262176 | tf_op jit(solution)/shard_map/ppermute | solution.py:286
  621.3 6.3 attend_bwd.5
  629.0 6.3 attend_bwd.6
  636.6 6.3 attend_bwd.7
  655.8 13.0 %psum.37 = f32[32,4]{0,1:T(4,128)} all-reduce(f32[32,4]{0,1:T(4,128)S(1)} %fusion.131), channel_id=1, replica_groups=mesh['dp'=8,'head'=4] {'dp'}, use_global_device_ids=true, to_apply=%region_18.19 | all-reduce | flops 128 | bytes 1024 | tf_op jit(solution)/shard_map/psum | solution.py:479
  671.4 9.8 %collective-permute-done.6 = bf16[512,768]{1,0:T(8,128)(2,1)} collective-permute-done((bf16[512,768]{1,0:T(8,128)(2,1)S(1)}, bf16[512,768]{1,0:T(8,128)(2,1)}, u32[]{:S(2)}, u32[]{:S(2)}) %collective-permute-start.6) | collective-permute-done | bytes 786464 | tf_op jit(solution)/shard_map/ppermute | solution.py:286
  683.9 29.0 %collective-permute-done.4 = bf16[512,768]{1,0:T(8,128)(2,1)} collective-permute-done((bf16[512,768]{1,0:T(8,128)(2,1)S(1)}, bf16[512,768]{1,0:T(8,128)(2,1)}, u32[]{:S(2)}, u32[]{:S(2)}) %collective-permute-start.4) | collective-permute-done | bytes 786464 | tf_op jit(solution)/shard_map/ppermute | solution.py:286
  718.4 39.5 %all-reduce.2 = (f32[1024]{0:T(1024)}, f32[1024]{0:T(1024)}, f32[1024,8]{0,1:T(8,128)}) all-reduce(f32[1024]{0:T(1024)S(1)} %get-tuple-element.45, f32[1024]{0:T(1024)S(1)} %get-tuple-element.47, f32[1024,8]{0,1:T(8,128)S(1)} %copy-done.49), channel_id=1, replica_groups=mesh['dp'=8,'head'=4] {'dp','head'}, use_global_device_ids=true, to_apply=%region_15.16 | all-reduce | flops 10240 | bytes 81920 | tf_op jit(solution)/shard_map/psum | solution.py:481
  757.9 3.7 fusion.48
  773.5 9.7 %all_gather.11 = bf16[256,1024]{1,0:T(8,128)(2,1)S(1)} all-gather(bf16[32,1024]{1,0:T(8,128)(2,1)S(1)} %fusion.129), channel_id=1, replica_groups=mesh['dp'=8,'head'=4] {'dp'}, dimensions={0}, use_global_device_ids=true | all-gather | bytes 589824 | tf_op jit(solution)/shard_map/all_gather | solution.py:434
  (284 shorter events, 99.0 us)
Async XLA Ops:
  7.2 9.1 %copy-start.33 = (bf16[1024,256]{1,0:T(8,128)(2,1)S(1)}, bf16[1024,256]{1,0:T(8,128)(2,1)}, u32[]{:S(2)}) copy-start(bf16[1024,256]{1,0:T(8,128)(2,1)} %param.23) | copy-start | bytes 1572868
  7.2 9.9 %copy-start.34 = (bf16[1024,256]{1,0:T(8,128)(2,1)S(1)}, bf16[1024,256]{1,0:T(8,128)(2,1)}, u32[]{:S(2)}) copy-start(bf16[1024,256]{1,0:T(8,128)(2,1)} %param.24) | copy-start | bytes 1572868
  7.2 74.8 %all-gather.3.cloned.1.call-start = ((), (), s32[]{:S(2)}) async-start(), calls=%async_computation.8 | async-start | bytes 2162688 | tf_op jit(solution)/shard_map/all_gather | solution.py:311
  34.5 26.4 %collective-permute-start = (bf16[512,256]{1,0:T(8,128)(2,1)S(1)}, bf16[512,256]{1,0:T(8,128)(2,1)S(1)}, u32[]{:S(2)}, u32[]{:S(2)}) collective-permute-start(bf16[512,256]{1,0:T(8,128)(2,1)S(1)} %get-tuple-element.30), channel_id=1, source_target_pairs={{0,1},{1,0},{2,3},{3,2},{4,5},{5,4},{6,7},{7,6},{8,9},{9,8},{10,11... | collective-permute-start | bytes 786440 | tf_op jit(solution)/shard_map/ppermute | solution.py:286
  44.4 21.3 %collective-permute-start.1 = (bf16[512,256]{1,0:T(8,128)(2,1)S(1)}, bf16[512,256]{1,0:T(8,128)(2,1)S(1)}, u32[]{:S(2)}, u32[]{:S(2)}) collective-permute-start(bf16[512,256]{1,0:T(8,128)(2,1)S(1)} %get-tuple-element.31), channel_id=1, source_target_pairs={{0,2},{1,3},{2,0},{3,1},{4,6},{5,7},{6,4},{7,5},{8,10},{9,11},{10,... | collective-permute-start | bytes 786440 | tf_op jit(solution)/shard_map/ppermute | solution.py:286
  52.5 7.0 copy-start.4
  52.6 13.2 %collective-permute-start.2 = (bf16[512,256]{1,0:T(8,128)(2,1)S(1)}, bf16[512,256]{1,0:T(8,128)(2,1)}, u32[]{:S(2)}, u32[]{:S(2)}) collective-permute-start(bf16[512,256]{1,0:T(8,128)(2,1)S(1)} %get-tuple-element.32), channel_id=1, source_target_pairs={{0,3},{1,2},{2,1},{3,0},{4,7},{5,6},{6,5},{7,4},{8,11},{9,10},{10,... | collective-permute-start | bytes 786440 | tf_op jit(solution)/shard_map/ppermute | solution.py:286
  53.8 214.5 %copy-start.64 = (s32[512]{0:T(512)}, s32[512]{0:T(512)S(1)}, u32[]{:S(2)}) copy-start(s32[512]{0:T(512)S(1)} %get-tuple-element.85) | copy-start | bytes 6148
  53.8 214.5 %copy-start.66 = (s32[512]{0:T(512)}, s32[512]{0:T(512)S(1)}, u32[]{:S(2)}) copy-start(s32[512]{0:T(512)S(1)} %get-tuple-element.86) | copy-start | bytes 6148
  66.7 20.3 %copy-start.52 = (bf16[512,1024]{1,0:T(8,128)(2,1)}, bf16[512,1024]{1,0:T(8,128)(2,1)S(1)}, u32[]{:S(2)}) copy-start(bf16[512,1024]{1,0:T(8,128)(2,1)S(1)} %constant_dynamic-update-slice_fusion.3) | copy-start | bytes 3145732
  87.1 37.1 %slice-start.4 = ((s8[5767168]{0:T(1024)(128)(4,1)}), s8[4194304]{0:T(1024)(128)(4,1)S(1)}, s32[]{:S(2)}) async-start(s8[5767168]{0:T(1024)(128)(4,1)} %bitcast.207), calls=%async_computation.15 | async-start | bytes 8388608
  87.4 36.8 %copy-start.23 = (bf16[512,1024]{1,0:T(8,128)(2,1)}, bf16[512,1024]{1,0:T(8,128)(2,1)S(1)}, u32[]{:S(2)}) copy-start(bf16[512,1024]{1,0:T(8,128)(2,1)S(1)} %multiply_convert_fusion.6) | copy-start | bytes 3145732
  87.4 36.8 %slice-start.5 = ((s8[5767168]{0:T(1024)(128)(4,1)}), s8[1572864]{0:T(1024)(128)(4,1)S(1)}, s32[]{:S(2)}) async-start(s8[5767168]{0:T(1024)(128)(4,1)} %bitcast.207), calls=%async_computation.16 | async-start | bytes 3145728
  124.2 265.5 %copy-start.22 = (bf16[8,160,1024]{2,1,0:T(8,128)(2,1)}, bf16[8,160,1024]{2,1,0:T(8,128)(2,1)S(1)}, u32[]{:S(2)}) copy-start(bf16[8,160,1024]{2,1,0:T(8,128)(2,1)S(1)} %all_to_all.40) | copy-start | bytes 7864324
  124.2 29.4 %slice-start.6 = ((s8[5767168]{0:T(1024)(128)(4,1)}), s8[4194304]{0:T(1024)(128)(4,1)S(1)}, s32[]{:S(2)}) async-start(s8[5767168]{0:T(1024)(128)(4,1)} %bitcast.209), calls=%async_computation.17 | async-start | bytes 8388608
  134.5 19.2 %slice-start.7 = ((s8[5767168]{0:T(1024)(128)(4,1)}), s8[1572864]{0:T(1024)(128)(4,1)S(1)}, s32[]{:S(2)}) async-start(s8[5767168]{0:T(1024)(128)(4,1)} %bitcast.209), calls=%async_computation.18 | async-start | bytes 3145728
  164.6 85.6 %all-to-all-start.1 = ((bf16[8,160,1024]{2,1,0:T(8,128)(2,1)}), bf16[8,160,1024]{2,1,0:T(8,128)(2,1)}, u32[]{:S(2)}, u32[]{:S(2)}) async-start(bf16[8,160,1024]{2,1,0:T(8,128)(2,1)} %bitcast.174), calls=%async_computation.1 | async-start | bytes 5242880 | tf_op jit(solution)/shard_map/all_to_all | solution.py:290
  169.0 499.8 %all-gather.5.cloned.1.call-start = ((), (), s32[]{:S(2)}) async-start(), calls=%async_computation.9 | async-start | bytes 6488064 | tf_op jit(solution)/shard_map/all_gather | solution.py:315
  169.6 76.1 %collective-permute-start.13 = (bf16[512,1024]{1,0:T(8,128)(2,1)}, bf16[512,1024]{1,0:T(8,128)(2,1)}, u32[]{:S(2)}, u32[]{:S(2)}) collective-permute-start(bf16[512,1024]{1,0:T(8,128)(2,1)} %copy-done.23), channel_id=1, source_target_pairs={{0,2},{1,3},{2,0},{3,1},{4,6},{5,7},{6,4},{7,5},{8,10},{9,11},{10,... | collective-permute-start | bytes 3145736 | tf_op jit(solution)/shard_map/ppermute | solution.py:369
  172.2 73.4 %collective-permute-start.12 = (s32[512,2]{0,1:T(2,128)S(1)}, s32[512,2]{0,1:T(2,128)S(1)}, u32[]{:S(2)}, u32[]{:S(2)}) collective-permute-start(s32[512,2]{0,1:T(2,128)S(1)} %pad_add_fusion.2), channel_id=1, source_target_pairs={{0,2},{1,3},{2,0},{3,1},{4,6},{5,7},{6,4},{7,5},{8,10},{9,11},{10,... | collective-permute-start | bytes 12296 | tf_op jit(solution)/shard_map/ppermute | solution.py:295
  174.3 121.8 %collective-permute-start.14 = (bf16[512,1024]{1,0:T(8,128)(2,1)}, bf16[512,1024]{1,0:T(8,128)(2,1)}, u32[]{:S(2)}, u32[]{:S(2)}) collective-permute-start(bf16[512,1024]{1,0:T(8,128)(2,1)} %param.17), channel_id=1, source_target_pairs={{0,2},{1,3},{2,0},{3,1},{4,6},{5,7},{6,4},{7,5},{8,10},{9,11},{10,... | collective-permute-start | bytes 3145736 | tf_op jit(solution)/shard_map/ppermute | solution.py:303
  250.3 7.3 copy-start.50
  250.3 42.4 %all-to-all-start.5 = ((bf16[8,160,1024]{2,1,0:T(8,128)(2,1)}), bf16[8,160,1024]{2,1,0:T(8,128)(2,1)}, u32[]{:S(2)}, u32[]{:S(2)}) async-start(bf16[8,160,1024]{2,1,0:T(8,128)(2,1)} %bitcast.171), calls=%async_computation.5 | async-start | bytes 5242880 | tf_op jit(solution)/shard_map/all_to_all | solution.py:290
  268.3 32.3 %copy-start.68 = (f32[512,1]{0,1:T(1,128)}, f32[512,1]{0,1:T(1,128)S(1)}, u32[]{:S(2)}) copy-start(f32[512,1]{0,1:T(1,128)S(1)} %get-tuple-element.83) | copy-start | bytes 6148
  268.3 32.3 %copy-start.70 = (f32[512,1]{0,1:T(1,128)}, f32[512,1]{0,1:T(1,128)S(1)}, u32[]{:S(2)}) copy-start(f32[512,1]{0,1:T(1,128)S(1)} %get-tuple-element.84) | copy-start | bytes 6148
  292.7 8.0 %all-to-all-start.3 = ((f32[8,160,1]{1,2,0:T(1,128)}), f32[8,160,1]{1,2,0:T(1,128)S(1)}, u32[]{:S(2)}, u32[]{:S(2)}) async-start(f32[8,160,1]{1,2,0:T(1,128)} %reshape.252), calls=%async_computation.3 | async-start | bytes 16384 | tf_op jit(solution)/shard_map/all_to_all | solution.py:290
  300.7 39.5 %all-to-all-start.2 = ((bf16[8,160,1024]{2,1,0:T(8,128)(2,1)}), bf16[8,160,1024]{2,1,0:T(8,128)(2,1)}, u32[]{:S(2)}, u32[]{:S(2)}) async-start(bf16[8,160,1024]{2,1,0:T(8,128)(2,1)} %bitcast.170), calls=%async_computation.2 | async-start | bytes 5242880 | tf_op jit(solution)/shard_map/all_to_all | solution.py:290
  305.2 14.0 %copy-start.24 = (bf16[512,1024]{1,0:T(8,128)(2,1)S(1)}, bf16[512,1024]{1,0:T(8,128)(2,1)}, u32[]{:S(2)}) copy-start(bf16[512,1024]{1,0:T(8,128)(2,1)} %copy-done.23) | copy-start | bytes 3145732
  319.2 4.6 collective-permute-start.15
  340.2 53.3 %all-to-all-start.7 = ((f32[8,160,1]{1,2,0:T(1,128)}), f32[8,160,1]{1,2,0:T(1,128)S(1)}, u32[]{:S(2)}, u32[]{:S(2)}) async-start(f32[8,160,1]{1,2,0:T(1,128)} %reshape.253), calls=%async_computation.7 | async-start | bytes 16384 | tf_op jit(solution)/shard_map/all_to_all | solution.py:290
  368.9 13.4 %copy-start.14 = (bf16[1280,2816]{1,0:T(8,128)(2,1)S(1)}, bf16[1280,2816]{1,0:T(8,128)(2,1)}, u32[]{:S(2)}) copy-start(bf16[1280,2816]{1,0:T(8,128)(2,1)} %get-tuple-element.62) | copy-start | bytes 21626884
  393.4 11.7 %slice-start = ((s8[7208960]{0:T(1024)(128)(4,1)}), s8[3014656]{0:T(1024)(128)(4,1)S(1)}, s32[]{:S(2)}) async-start(s8[7208960]{0:T(1024)(128)(4,1)} %bitcast.160), calls=%async_computation.11 | async-start | bytes 6029312
  393.4 37.0 %all-to-all-start.6 = ((bf16[8,160,1024]{2,1,0:T(8,128)(2,1)}), bf16[8,160,1024]{2,1,0:T(8,128)(2,1)}, u32[]{:S(2)}, u32[]{:S(2)}) async-start(bf16[8,160,1024]{2,1,0:T(8,128)(2,1)} %bitcast.172), calls=%async_computation.6 | async-start | bytes 5242880 | tf_op jit(solution)/shard_map/all_to_all | solution.py:290
  398.1 7.1 slice-start.1
  430.4 154.6 %all-to-all-start.4 = ((bf16[8,160,1024]{2,1,0:T(8,128)(2,1)}), bf16[8,160,1024]{2,1,0:T(8,128)(2,1)}, u32[]{:S(2)}, u32[]{:S(2)}) async-start(bf16[8,160,1024]{2,1,0:T(8,128)(2,1)} %bitcast.173), calls=%async_computation.4 | async-start | bytes 5242880 | tf_op jit(solution)/shard_map/all_to_all | solution.py:290
  434.8 326.8 %all-reduce.6.cloned.1.call-start = ((), (), s32[]{:S(2)}) async-start(), calls=%async_computation.10 | async-start | bytes 7340032 | tf_op jit(solution)/shard_map/psum | solution.py:479
  474.3 11.8 %slice-start.2 = ((s8[7208960]{0:T(1024)(128)(4,1)}), s8[4194304]{0:T(1024)(128)(4,1)S(1)}, s32[]{:S(2)}) async-start(s8[7208960]{0:T(1024)(128)(4,1)} %bitcast.162), calls=%async_computation.13 | async-start | bytes 8388608
  479.3 6.7 slice-start.3
  479.3 6.7 copy-start.19
  484.5 34.5 %collective-permute-start.18 = (bf16[704,1024]{1,0:T(8,128)(2,1)S(1)}, bf16[704,1024]{1,0:T(8,128)(2,1)S(1)}, u32[]{:S(2)}, u32[]{:S(2)}) collective-permute-start(bf16[704,1024]{1,0:T(8,128)(2,1)S(1)} %add_convert_fusion.2), channel_id=1, source_target_pairs={{0,1},{1,0},{2,3},{3,2},{4,5},{5,4},{6,7},{7,6},{8,9},{9,8},{10,11... | collective-permute-start | bytes 4325384 | tf_op jit(solution)/shard_map/ppermute | solution.py:286
  489.4 60.5 %collective-permute-start.16 = (bf16[256,2816]{1,0:T(8,128)(2,1)S(1)}, bf16[256,2816]{1,0:T(8,128)(2,1)S(1)}, u32[]{:S(2)}, u32[]{:S(2)}) collective-permute-start(bf16[256,2816]{1,0:T(8,128)(2,1)S(1)} %fusion.35), channel_id=1, source_target_pairs={{0,1},{1,0},{2,3},{3,2},{4,5},{5,4},{6,7},{7,6},{8,9},{9,8},{10,11... | collective-permute-start | bytes 4325384 | tf_op jit(solution)/shard_map/ppermute | solution.py:286
  493.3 86.9 %collective-permute-start.17 = (bf16[256,2816]{1,0:T(8,128)(2,1)S(1)}, bf16[256,2816]{1,0:T(8,128)(2,1)S(1)}, u32[]{:S(2)}, u32[]{:S(2)}) collective-permute-start(bf16[256,2816]{1,0:T(8,128)(2,1)S(1)} %fusion.36), channel_id=1, source_target_pairs={{0,1},{1,0},{2,3},{3,2},{4,5},{5,4},{6,7},{7,6},{8,9},{9,8},{10,11... | collective-permute-start | bytes 4325384 | tf_op jit(solution)/shard_map/ppermute | solution.py:286
  499.7 50.1 %copy-start.20 = (f32[256,2816]{1,0:T(8,128)S(1)}, f32[256,2816]{1,0:T(8,128)}, u32[]{:S(2)}) copy-start(f32[256,2816]{1,0:T(8,128)} %fusion.123) | copy-start | bytes 8650756
  525.6 54.5 %copy-start.21 = (f32[256,2816]{1,0:T(8,128)S(1)}, f32[256,2816]{1,0:T(8,128)}, u32[]{:S(2)}) copy-start(f32[256,2816]{1,0:T(8,128)} %fusion.121) | copy-start | bytes 8650756
  554.6 30.5 %copy-start.65 = (s32[512]{0:T(512)S(1)}, s32[512]{0:T(512)}, u32[]{:S(2)}) copy-start(s32[512]{0:T(512)} %copy-done.64) | copy-start | bytes 6148
  554.6 30.5 %copy-start.67 = (s32[512]{0:T(512)S(1)}, s32[512]{0:T(512)}, u32[]{:S(2)}) copy-start(s32[512]{0:T(512)} %copy-done.66) | copy-start | bytes 6148
  593.4 13.6 %copy-start.25 = (f32[512,1024]{1,0:T(8,128)}, f32[512,1024]{1,0:T(8,128)S(1)}, u32[]{:S(2)}) copy-start(f32[512,1024]{1,0:T(8,128)S(1)} %get-tuple-element.66) | copy-start | bytes 6291460
  594.8 41.9 %collective-permute-start.7 = (bf16[512,256]{1,0:T(8,128)(2,1)S(1)}, bf16[512,256]{1,0:T(8,128)(2,1)S(1)}, u32[]{:S(2)}, u32[]{:S(2)}) collective-permute-start(bf16[512,256]{1,0:T(8,128)(2,1)S(1)} %get-tuple-element.75), channel_id=1, source_target_pairs={{0,1},{1,0},{2,3},{3,2},{4,5},{5,4},{6,7},{7,6},{8,9},{9,8},{10,11... | collective-permute-start | bytes 786440 | tf_op jit(solution)/shard_map/ppermute | solution.py:286
  596.3 32.7 %collective-permute-start.5 = (bf16[512,256]{1,0:T(8,128)(2,1)S(1)}, bf16[512,256]{1,0:T(8,128)(2,1)S(1)}, u32[]{:S(2)}, u32[]{:S(2)}) collective-permute-start(bf16[512,256]{1,0:T(8,128)(2,1)S(1)} %get-tuple-element.76), channel_id=1, source_target_pairs={{0,3},{1,2},{2,1},{3,0},{4,7},{5,6},{6,5},{7,4},{8,11},{9,10},{10,... | collective-permute-start | bytes 786440 | tf_op jit(solution)/shard_map/ppermute | solution.py:286
  598.5 22.8 %collective-permute-start.3 = (bf16[512,256]{1,0:T(8,128)(2,1)S(1)}, bf16[512,256]{1,0:T(8,128)(2,1)S(1)}, u32[]{:S(2)}, u32[]{:S(2)}) collective-permute-start(bf16[512,256]{1,0:T(8,128)(2,1)S(1)} %get-tuple-element.77), channel_id=1, source_target_pairs={{0,2},{1,3},{2,0},{3,1},{4,6},{5,7},{6,4},{7,5},{8,10},{9,11},{10,... | collective-permute-start | bytes 786440 | tf_op jit(solution)/shard_map/ppermute | solution.py:286
  609.7 11.6 %copy-start.7 = (bf16[4,512,512]{2,1,0:T(8,128)(2,1)S(1)}, bf16[4,512,512]{2,1,0:T(8,128)(2,1)}, u32[]{:S(2)}) copy-start(bf16[4,512,512]{2,1,0:T(8,128)(2,1)} %copy-done.6) | copy-start | bytes 6291460
  621.3 7.7 copy-start.5
  629.0 7.7 copy-start.3
  643.0 72.3 %collective-permute-start.8 = (bf16[512,768]{1,0:T(8,128)(2,1)S(1)}, bf16[512,768]{1,0:T(8,128)(2,1)}, u32[]{:S(2)}, u32[]{:S(2)}) collective-permute-start(bf16[512,768]{1,0:T(8,128)(2,1)S(1)} %get-tuple-element.43), channel_id=1, source_target_pairs={{0,1},{1,0},{2,3},{3,2},{4,5},{5,4},{6,7},{7,6},{8,9},{9,8},{10,11... | collective-permute-start | bytes 2359304 | tf_op jit(solution)/shard_map/ppermute | solution.py:286
  643.1 38.1 %collective-permute-start.6 = (bf16[512,768]{1,0:T(8,128)(2,1)S(1)}, bf16[512,768]{1,0:T(8,128)(2,1)}, u32[]{:S(2)}, u32[]{:S(2)}) collective-permute-start(bf16[512,768]{1,0:T(8,128)(2,1)S(1)} %get-tuple-element.40), channel_id=1, source_target_pairs={{0,3},{1,2},{2,1},{3,0},{4,7},{5,6},{6,5},{7,4},{8,11},{9,10},{10,... | collective-permute-start | bytes 2359304 | tf_op jit(solution)/shard_map/ppermute | solution.py:286
  645.8 67.2 %collective-permute-start.4 = (bf16[512,768]{1,0:T(8,128)(2,1)S(1)}, bf16[512,768]{1,0:T(8,128)(2,1)}, u32[]{:S(2)}, u32[]{:S(2)}) collective-permute-start(bf16[512,768]{1,0:T(8,128)(2,1)S(1)} %get-tuple-element.37), channel_id=1, source_target_pairs={{0,2},{1,3},{2,0},{3,1},{4,6},{5,7},{6,4},{7,5},{8,10},{9,11},{10,... | collective-permute-start | bytes 2359304 | tf_op jit(solution)/shard_map/ppermute | solution.py:286
  668.8 44.2 %copy-start.43 = (bf16[4096,768]{1,0:T(8,128)(2,1)S(1)}, bf16[4096,768]{1,0:T(8,128)(2,1)}, u32[]{:S(2)}) copy-start(bf16[4096,768]{1,0:T(8,128)(2,1)} %all-gather.5.cloned.1.call-done) | copy-start | bytes 18874372
  683.9 31.4 %copy-start.55 = (f32[1024]{0:T(1024)S(1)}, f32[1024]{0:T(1024)}, u32[]{:S(2)}) copy-start(f32[1024]{0:T(1024)} %param.21) | copy-start | bytes 12292
  683.9 31.4 %copy-start.61 = (f32[512]{0:T(512)S(1)}, f32[512]{0:T(512)}, u32[]{:S(2)}) copy-start(f32[512]{0:T(512)} %fusion.158) | copy-start | bytes 6148
  715.2 42.7 %copy-start.63 = (f32[512]{0:T(512)S(1)}, f32[512]{0:T(512)}, u32[]{:S(2)}) copy-start(f32[512]{0:T(512)} %copy-done.62) | copy-start | bytes 6148
  763.1 7.6 collective-permute-start.11
  764.8 7.2 collective-permute-start.10
  766.8 5.2 collective-permute-start.9
  767.6 16.7 %copy-start.1 = (bf16[256,1024]{1,0:T(8,128)(2,1)S(1)}, bf16[256,1024]{1,0:T(8,128)(2,1)}, u32[]{:S(2)}) copy-start(bf16[256,1024]{1,0:T(8,128)(2,1)} %param.25) | copy-start | bytes 1572868
  (49 other events, 151.8 us)
Sparse Core Ops, SparseCore 0:
  11.5 70.4 all-gather.2
  172.7 154.6 all-gather.4
  655.7 75.9 all-reduce.5

commit v2 on v1

--- a/solution.py
+++ b/solution.py
@@ -14,6 +14,9 @@
 BF = jnp.bfloat16
 F32 = jnp.float32
 VMEM_LIMIT = 48 << 20
+VMEM_MOST = 60 << 20
+GELU_A = 0.7978845608028654
+GELU_B = 0.044715
 
 
 def rms_norm(value, gain):
@@ -240,6 +243,497 @@
     )(seq, qkv, qkv, qkv, grad, probs, sums)
 
 
+def flipped(index, bits):
+    out, step = index, 1
+    while step <= bits:
+        if bits & step:
+            out = out + step * (1 - 2 * lax.rem(index // step, 2))
+        step *= 2
+    return out
+
+
+def greet(peers):
+    barrier = pltpu.get_barrier_semaphore()
+    for peer in peers:
+        pl.semaphore_signal(barrier, inc=1, device_id=peer, device_id_type=pl.DeviceIdType.MESH)
+    pl.semaphore_wait(barrier, len(peers))
+
+
+def remote(source, target, send_sem, recv_sem, peer):
+    return pltpu.make_async_remote_copy(
+        src_ref=source,
+        dst_ref=target,
+        send_sem=send_sem,
+        recv_sem=recv_sem,
+        device_id=peer,
+        device_id_type=pl.DeviceIdType.MESH,
+    )
+
+
+def attend_all_kernel(
+    groups,
+    replicas,
+    qkv_ref,
+    table_ref,
+    sent_ref,
+    out_ref,
+    probs_ref,
+    came_ref,
+    acc_ref,
+    block_ref,
+    hold_ref,
+    row_send,
+    row_recv,
+    hop_send,
+    hop_recv,
+    hold_sem,
+    own_sem,
+):
+    z, d = lax.axis_index("head"), lax.axis_index("dp")
+    heads, _, _ = table_ref.shape
+    length = block_ref.shape[1]
+    columns = block_ref.shape[2]
+    pairs = heads // 2
+    lanes = columns // pairs
+    half = lanes // 2
+    chunk = 2 * TILE
+    hops = range(1, replicas)
+    offs = [2, 4, 3, 5, 6, 7, 1]
+    greet([{"dp": flipped(d, o)} for o in offs] + [{"head": flipped(z, r)} for r in hops])
+    copies = []
+    for o in offs:
+        copies.append(
+            remote(
+                sent_ref.at[o],
+                came_ref.at[o],
+                row_send.at[o],
+                row_recv.at[o],
+                {"dp": flipped(d, o)},
+            )
+        )
+        copies[-1].start()
+    own = pltpu.make_async_copy(sent_ref.at[0], came_ref.at[0], own_sem.at[0])
+    own.start()
+
+    moves = []
+    for turn, r in enumerate(reversed(range(replicas))):
+        start = pl.multiple_of(flipped(z, r) * length, length)
+        slot = turn % 2
+        if turn >= 2:
+            moves[turn - 2].wait()
+
+        def pair_step(pair, carry, start=start, slot=slot, r=r):
+            def part_of(j):
+                at = pl.multiple_of(j * columns + pair * lanes, lanes)
+                return qkv_ref[pl.ds(start, length), pl.ds(at, lanes)]
+
+            key = part_of(1)
+            value_t = part_of(2).T
+            scaled = part_of(0) * SCALE
+            for part in range(2):
+                query = jnp.where(lanes_of((length, lanes), half, part), scaled, 0).astype(BF)
+                for c in range(length // chunk):
+                    cols = slice(c * chunk, (c + 1) * chunk)
+                    scores = contract(key, query[cols], 1, 1)
+                    pieces = []
+                    for kb in range(length // TILE):
+                        at = length - TILE * kb + chunk * c
+                        pieces.append(
+                            scores[kb * TILE : (kb + 1) * TILE]
+                            + table_ref[pair * 2 + part, :, at : at + chunk]
+                        )
+                    scores = jnp.concatenate(pieces, axis=0)
+                    top = jnp.max(scores, axis=0, keepdims=True)
+                    shifted = jnp.exp(scores - top)
+                    total = jnp.sum(shifted, axis=0, keepdims=True)
+                    probs = (shifted * (1.0 / total)).astype(BF)
+                    hold_ref[slot, pair * 2 + part, :, cols] = probs
+                    acc_ref[part * half : (part + 1) * half, cols] = jnp.dot(
+                        value_t[part * half : (part + 1) * half],
+                        probs,
+                        preferred_element_type=F32,
+                    )
+            at = pl.multiple_of(pair * lanes, lanes)
+            block_ref[r, :, pl.ds(at, lanes)] = acc_ref[...].T.astype(BF)
+            return carry
+
+        lax.fori_loop(0, pairs, pair_step, 0)
+        move = pltpu.make_async_copy(hold_ref.at[slot], probs_ref.at[r], hold_sem.at[slot])
+        move.start()
+        moves.append(move)
+        target = out_ref.at[:, pl.ds(r * columns, columns)]
+        if r:
+            hop = remote(
+                block_ref.at[r], target, hop_send.at[r], hop_recv.at[r], {"head": flipped(z, r)}
+            )
+            hop.start()
+            copies.append(hop)
+        else:
+            last = pltpu.make_async_copy(block_ref.at[0], target, own_sem.at[1])
+            last.start()
+    moves[-2].wait()
+    moves[-1].wait()
+    own.wait()
+    last.wait()
+    for copy in copies:
+        copy.wait()
+
+
+def attend_all(qkv, table, sent, length, replicas):
+    heads, _, width = table.shape
+    columns = qkv.shape[1] // 3
+    lanes = 2 * columns // heads
+    groups = sent.shape[0]
+    vmem = pl.BlockSpec(memory_space=pltpu.VMEM)
+    hbm = pl.BlockSpec(memory_space=pl.ANY)
+    return pl.pallas_call(
+        functools.partial(attend_all_kernel, groups, replicas),
+        out_shape=(
+            jax.ShapeDtypeStruct((length, replicas * columns), BF),
+            jax.ShapeDtypeStruct((replicas, heads, length, length), BF),
+            jax.ShapeDtypeStruct(sent.shape, BF),
+        ),
+        in_specs=[vmem, vmem, hbm],
+        out_specs=[hbm, hbm, hbm],
+        scratch_shapes=[
+            pltpu.VMEM((lanes, length), F32),
+            pltpu.VMEM((replicas, length, columns), BF),
+            pltpu.VMEM((2, heads, length, length), BF),
+            pltpu.SemaphoreType.DMA((groups,)),
+            pltpu.SemaphoreType.DMA((groups,)),
+            pltpu.SemaphoreType.DMA((replicas,)),
+            pltpu.SemaphoreType.DMA((replicas,)),
+            pltpu.SemaphoreType.DMA((2,)),
+            pltpu.SemaphoreType.DMA((2,)),
+        ],
+        compiler_params=pltpu.CompilerParams(
+            vmem_limit_bytes=VMEM_LIMIT, collective_id=1, has_side_effects=True
+        ),
+        cost_estimate=pl.CostEstimate(
+            flops=replicas * heads * 8 * length * length * lanes,
+            bytes_accessed=replicas * heads * length * length * 4,
+            transcendentals=replicas * heads * length * length,
+        ),
+        name="attend_all",
+    )(qkv, table, sent)
+
+
+def expert_tile(rows, scaled, gate_w, up_w, down_w):
+    gate = jnp.dot(rows, gate_w, preferred_element_type=F32)
+    up_part = jnp.dot(rows, up_w, preferred_element_type=F32)
+    grad_hidden = contract(scaled, down_w, 1, 1)
+    square = gate * gate
+    bend = jnp.tanh(gate * (GELU_A + GELU_A * GELU_B * square))
+    half = 0.5 + 0.5 * bend
+    active = gate * half
+    slope = half + 0.5 * gate * (1.0 - bend * bend) * (GELU_A + 3.0 * GELU_A * GELU_B * square)
+    hidden = (active * up_part).astype(BF)
+    grad_gate = (grad_hidden * up_part * slope).astype(BF)
+    grad_up = (grad_hidden * active).astype(BF)
+    return hidden, grad_gate, grad_up
+
+
+def scaled_rows(rows, extended, router, width):
+    logits = jnp.dot(rows, router, preferred_element_type=F32)
+    sign = extended[:, width:].astype(F32)
+    gap = jnp.sum(logits * sign, axis=1, keepdims=True)
+    return (extended[:, :width].astype(F32) * (1.0 / (1.0 + jnp.exp(gap)))).astype(BF)
+
+
+def expert_kernel(
+    width,
+    tile,
+    normed_ref,
+    both_ref,
+    cot_ref,
+    router_ref,
+    gate_hbm,
+    up_hbm,
+    down_hbm,
+    rows_out,
+    hidden_out,
+    grad_gate_out,
+    grad_up_out,
+    scaled_out,
+    back_out,
+    grad_back_out,
+    gate_w,
+    up_w,
+    down_w,
+    rows,
+    sends,
+    back,
+    grad_back,
+    hidden,
+    grad_gate,
+    grad_up,
+    scaled,
+    weight_sem,
+    row_send,
+    row_recv,
+    back_send,
+    back_recv,
+    grad_send,
+    grad_recv,
+    unit_sem,
+    keep_sem,
+):
+    d = lax.axis_index("dp")
+    groups, capacity, _ = rows.shape
+    units = gate_w.shape[1]
+    tiles = units // tile
+    count = 2 * capacity
+    offs = [2, 4, 3, 5, 6, 7, 1]
+
+    def weights_of(t):
+        at = pl.multiple_of(t * tile, tile)
+        return [
+            pltpu.make_async_copy(
+                gate_hbm.at[:, pl.ds(at, tile)], gate_w.at[:, pl.ds(at, tile)], weight_sem.at[0, t]
+            ),
+            pltpu.make_async_copy(
+                up_hbm.at[:, pl.ds(at, tile)], up_w.at[:, pl.ds(at, tile)], weight_sem.at[1, t]
+            ),
+            pltpu.make_async_copy(
+                down_hbm.at[pl.ds(at, tile), :], down_w.at[pl.ds(at, tile), :], weight_sem.at[2, t]
+            ),
+        ]
+
+    def start_weights(t, carry):
+        for copy in weights_of(t):
+            copy.start()
+        return carry
+
+    lax.fori_loop(0, tiles, start_weights, 0)
+    greet([{"dp": flipped(d, o)} for o in offs])
+    pending = []
+    arrivals = {}
+    for o in offs:
+        sends[o] = jnp.dot(
+            both_ref[o * capacity : (o + 1) * capacity],
+            normed_ref[...],
+            preferred_element_type=F32,
+        ).astype(BF)
+        arrivals[o] = remote(
+            sends.at[o], rows.at[o], row_send.at[o], row_recv.at[o], {"dp": flipped(d, o)}
+        )
+        arrivals[o].start()
+    rows[0] = jnp.dot(
+        both_ref[:capacity], normed_ref[...], preferred_element_type=F32
+    ).astype(BF)
+
+    unit_copies = {}
+    for j in range(groups // 2):
+        pair = (2 * j, 2 * j + 1)
+        slot = j % 2
+        for o in pair:
+            if o:
+                arrivals[o].wait_recv()
+        if j >= 2:
+            for copy in unit_copies[j - 2]:
+                copy.wait()
+        here = rows[2 * j : 2 * j + 2].reshape(count, width)
+        extended = cot_ref[2 * j : 2 * j + 2].reshape(count, cot_ref.shape[2])
+        scaled[2 * j : 2 * j + 2] = scaled_rows(here, extended, router_ref[...], width).reshape(
+            2, capacity, width
+        )
+
+        def tile_step(t, carry, j=j, slot=slot):
+            at = pl.multiple_of(t * tile, tile)
+            if j == 0:
+                for copy in weights_of(t):
+                    copy.wait()
+            values = expert_tile(
+                rows[2 * j : 2 * j + 2].reshape(count, width),
+                scaled[2 * j : 2 * j + 2].reshape(count, width),
+                gate_w[:, pl.ds(at, tile)],
+                up_w[:, pl.ds(at, tile)],
+                down_w[pl.ds(at, tile), :],
+            )
+            for ref, value in zip((hidden, grad_gate, grad_up), values):
+                ref[slot, :, pl.ds(at, tile)] = value
+            return carry
+
+        lax.fori_loop(0, tiles, tile_step, 0)
+        span = pl.ds(j * count, count)
+        unit_copies[j] = [
+            pltpu.make_async_copy(ref.at[slot], out.at[span], unit_sem.at[slot, i])
+            for i, (ref, out) in enumerate(
+                ((hidden, hidden_out), (grad_gate, grad_gate_out), (grad_up, grad_up_out))
+            )
+        ]
+        for copy in unit_copies[j]:
+            copy.start()
+
+        def back_step(t, carry, j=j, slot=slot):
+            at = pl.multiple_of(t * tile, tile)
+            value = jnp.dot(hidden[slot], down_w[:, pl.ds(at, tile)], preferred_element_type=F32)
+            back[2 * j : 2 * j + 2, :, pl.ds(at, tile)] = value.astype(BF).reshape(
+                2, capacity, tile
+            )
+            return carry
+
+        def grad_step(t, carry, j=j, slot=slot):
+            at = pl.multiple_of(t * tile, tile)
+            value = contract(grad_gate[slot], gate_w[pl.ds(at, tile), :], 1, 1) + contract(
+                grad_up[slot], up_w[pl.ds(at, tile), :], 1, 1
+            )
+            grad_back[2 * j : 2 * j + 2, :, pl.ds(at, tile)] = value.astype(BF).reshape(
+                2, capacity, tile
+            )
+            return carry
+
+        for step, buffer, out, send_sem, recv_sem in (
+            (back_step, back, back_out, back_send, back_recv),
+            (grad_step, grad_back, grad_back_out, grad_send, grad_recv),
+        ):
+            lax.fori_loop(0, width // tile, step, 0)
+            for o in pair:
+                if o:
+                    copy = remote(
+                        buffer.at[o],
+                        out.at[o],
+                        send_sem.at[o],
+                        recv_sem.at[o],
+                        {"dp": flipped(d, o)},
+                    )
+                else:
+                    copy = pltpu.make_async_copy(buffer.at[0], out.at[0], send_sem.at[0])
+                copy.start()
+                pending.append(copy)
+
+    keeps = [
+        pltpu.make_async_copy(rows, rows_out, keep_sem.at[0]),
+        pltpu.make_async_copy(scaled, scaled_out, keep_sem.at[1]),
+    ]
+    for copy in keeps:
+        copy.start()
+    for j in range(groups // 2 - 2, groups // 2):
+        for copy in unit_copies[j]:
+            copy.wait()
+    for o in offs:
+        arrivals[o].wait_send()
+    for copy in pending + keeps:
+        copy.wait()
+
+
+def expert_stage(normed2, both, cot, router, gate_w, up_w, down_w, groups, capacity, tile):
+    width, units = gate_w.shape
+    slots = groups * capacity
+    vmem = pl.BlockSpec(memory_space=pltpu.VMEM)
+    hbm = pl.BlockSpec(memory_space=pl.ANY)
+    row_shape = jax.ShapeDtypeStruct((groups, capacity, width), BF)
+    unit_shape = jax.ShapeDtypeStruct((slots, units), BF)
+    row_buffer = pltpu.VMEM((groups, capacity, width), BF)
+    unit_buffer = pltpu.VMEM((2, 2 * capacity, units), BF)
+    row_sem = pltpu.SemaphoreType.DMA((groups,))
+    return pl.pallas_call(
+        functools.partial(expert_kernel, width, tile),
+        out_shape=(row_shape,) + (unit_shape,) * 3 + (row_shape,) * 3,
+        in_specs=[vmem] * 4 + [hbm] * 3,
+        out_specs=[hbm] * 7,
+        scratch_shapes=[
+            pltpu.VMEM((width, units), BF),
+            pltpu.VMEM((width, units), BF),
+            pltpu.VMEM((units, width), BF),
+            row_buffer,
+            row_buffer,
+            row_buffer,
+            row_buffer,
+            unit_buffer,
+            unit_buffer,
+            unit_buffer,
+            row_buffer,
+            pltpu.SemaphoreType.DMA((3, units // tile)),
+            row_sem,
+            row_sem,
+            row_sem,
+            row_sem,
+            row_sem,
+            row_sem,
+            pltpu.SemaphoreType.DMA((2, 3)),
+            pltpu.SemaphoreType.DMA((2,)),
+        ],
+        compiler_params=pltpu.CompilerParams(
+            vmem_limit_bytes=VMEM_MOST, collective_id=2, has_side_effects=True
+        ),
+        cost_estimate=pl.CostEstimate(
+            flops=12 * slots * width * units,
+            bytes_accessed=6 * width * units + 6 * slots * units,
+            transcendentals=slots * units,
+        ),
+        name="expert_stage",
+    )(normed2, both, cot, router, gate_w, up_w, down_w)
+
+
+def far_kernel(
+    width,
+    rows_ref,
+    cot_ref,
+    router_ref,
+    gate_w,
+    up_w,
+    down_w,
+    hidden_out,
+    grad_gate_out,
+    grad_up_out,
+    scaled_out,
+):
+    slots = rows_ref.shape[0]
+    count = slots // 4
+
+    @pl.when(pl.program_id(0) == 0)
+    def _():
+        for i in range(4):
+            span = slice(i * count, (i + 1) * count)
+            scaled_out[span] = scaled_rows(
+                rows_ref[span], cot_ref[span], router_ref[...], width
+            )
+
+    def step(i, carry):
+        span = pl.ds(pl.multiple_of(i * count, count), count)
+        values = expert_tile(
+            rows_ref[span], scaled_out[span], gate_w[...], up_w[...], down_w[...]
+        )
+        for ref, value in zip((hidden_out, grad_gate_out, grad_up_out), values):
+            ref[span] = value
+        return carry
+
+    lax.fori_loop(0, 4, step, 0)
+
+
+def far_stage(rows, cot, router, gate_w, up_w, down_w, tile):
+    width, units = gate_w.shape
+    slots = rows.shape[0]
+
+    def whole(shape):
+        return pl.BlockSpec(shape, lambda t: (0, 0))
+
+    unit_shape = jax.ShapeDtypeStruct((slots, units), BF)
+    unit_spec = pl.BlockSpec((slots, tile), lambda t: (0, t))
+    return pl.pallas_call(
+        functools.partial(far_kernel, width),
+        out_shape=(unit_shape,) * 3 + (jax.ShapeDtypeStruct((slots, width), BF),),
+        grid=(units // tile,),
+        in_specs=[
+            whole(rows.shape),
+            whole(cot.shape),
+            whole(router.shape),
+            pl.BlockSpec((width, tile), lambda t: (0, t)),
+            pl.BlockSpec((width, tile), lambda t: (0, t)),
+            pl.BlockSpec((tile, width), lambda t: (t, 0)),
+        ],
+        out_specs=[unit_spec] * 3 + [whole((slots, width))],
+        compiler_params=pltpu.CompilerParams(vmem_limit_bytes=VMEM_LIMIT),
+        cost_estimate=pl.CostEstimate(
+            flops=6 * slots * width * units,
+            bytes_accessed=6 * width * units + 6 * slots * units,
+            transcendentals=slots * units,
+        ),
+        name="far_stage",
+    )(rows, cot, router, gate_w, up_w, down_w)
+
+
 def expert_forward(rows, gate_w, up_w, grad_unscaled, slot_gates):
     gate_pre = jnp.dot(rows, gate_w, preferred_element_type=F32)
     up_pre = jnp.dot(rows, up_w, preferred_element_type=F32)
@@ -248,7 +742,7 @@
     return hidden.astype(BF), grad_gate_pre.astype(BF), grad_up_pre.astype(BF)
 
 
-def body(
+def body_plain(
     block_input,
     cotangent,
     expert_ids,
@@ -498,6 +992,237 @@
     )
 
 
+def body(*args):
+    block_input, cotangent, rel_bucket, pos_bias, w_gate, w_router = (
+        args[0],
+        args[1],
+        args[4],
+        args[10],
+        args[13],
+        args[12],
+    )
+    own_rows = cotangent.shape[0]
+    length = (rel_bucket.shape[0] + 1) // 2
+    replicas, groups = lax.axis_size("head"), lax.axis_size("dp")
+    experts = w_router.shape[1]
+    capacity = 5 * 2 * own_rows // (4 * experts)
+    stepwise = (
+        own_rows == length
+        and block_input.shape[0] == replicas * length
+        and replicas == 4
+        and groups == 8
+        and experts == groups
+        and capacity % 16 == 0
+        and pos_bias.shape[1] % 2 == 0
+        and w_gate.shape[2] % 256 == 0
+    )
+    return body_steps(*args) if stepwise else body_plain(*args)
+
+
+def body_steps(
+    block_input,
+    cotangent,
+    expert_ids,
+    priority,
+    rel_bucket,
+    norm1_gain,
+    w_query,
+    w_key,
+    w_value,
+    w_out,
+    pos_bias,
+    norm2_gain,
+    w_router,
+    w_gate,
+    w_up,
+    w_down,
+):
+    group_rows, width = block_input.shape
+    own_rows = cotangent.shape[0]
+    buckets, heads_here = pos_bias.shape
+    head_cols = w_query.shape[1]
+    length = (rel_bucket.shape[0] + 1) // 2
+    experts = w_router.shape[1]
+    capacity = 5 * 2 * own_rows // (4 * experts)
+    slot_count = experts * capacity
+    replicas, groups = lax.axis_size("head"), lax.axis_size("dp")
+    me, dp_at = lax.axis_index("head"), lax.axis_index("dp")
+    far = replicas // 2
+    far_perm = [(i, i ^ far) for i in range(replicas)]
+
+    def hop(value, r):
+        return lax.ppermute(value, "head", [(i, i ^ r) for i in range(replicas)])
+
+    dest = route_slots(expert_ids, priority[0], experts, capacity)
+    mixed_dest = jnp.where(
+        dest < slot_count,
+        ((dest // capacity) ^ dp_at) * capacity + dest % capacity,
+        slot_count,
+    )
+    routing_far = hop(jnp.concatenate([dest, expert_ids], axis=1), far)
+    slot_row = jnp.arange(slot_count, dtype=jnp.int32)[None, :]
+    slot_col = jnp.arange(slot_count, dtype=jnp.int32)[:, None]
+    expert_range = jnp.arange(experts, dtype=jnp.int32)
+    lane_range = jnp.arange(TILE, dtype=jnp.int32)[None, :]
+
+    def dispatch_of(places, ids):
+        first = (slot_col == places[:, 0][None, :]).astype(BF)
+        second = (slot_col == places[:, 1][None, :]).astype(BF)
+        signs = (ids[:, 1:2] == lane_range).astype(BF) - (ids[:, 0:1] == lane_range).astype(BF)
+        return first + second, contract(first - second, signs, 1, 0).astype(BF)
+
+    both, signs = dispatch_of(mixed_dest, expert_ids)
+    picks = [(mixed_dest[:, k : k + 1] == slot_row).astype(BF) for k in range(2)]
+    router_wide = jnp.pad(w_router, ((0, 0), (0, TILE - experts)))
+    cot_sent = jnp.concatenate([contract(both, cotangent, 1, 0).astype(BF), signs], axis=1)
+    cot_sent = cot_sent.reshape(experts, capacity, width + TILE)
+    cot_far_own = hop(cotangent, far)
+
+    out_rows = head_cols // groups
+    piece = lax.dynamic_slice_in_dim(w_out, dp_at * out_rows, out_rows, 0)
+    w_out_all = lax.all_gather(piece, ("head", "dp"), axis=0, tiled=True)
+    w_qkv = jnp.concatenate([w_query, w_key, w_value], axis=1)
+    order = [me ^ r for r in range(replicas)]
+    w_out_all = w_out_all.reshape(replicas, head_cols, width)
+    w_out_cat = jnp.concatenate(
+        [lax.dynamic_index_in_dim(w_out_all, o, 0, keepdims=False) for o in order], axis=0
+    )
+
+    inputs_all = block_input.astype(F32)
+    normed = rms_norm(inputs_all, norm1_gain).astype(BF)
+    qkv = jnp.dot(normed, w_qkv, preferred_element_type=F32).astype(BF)
+    line = (rel_bucket[::-1][None, :] == jnp.arange(buckets, dtype=jnp.int32)[:, None]).astype(F32)
+    line = jnp.pad(line, ((0, 0), (1, 0)))
+    table = skew(contract(pos_bias, line, 0, 0, HIGH))
+    attended, probs, cot_here = attend_all(qkv, table, cot_sent, length, replicas)
+
+    branch = jnp.dot(attended, w_out_cat, preferred_element_type=F32)
+    inputs_own = lax.dynamic_slice_in_dim(block_input, me * own_rows, own_rows, 0).astype(F32)
+    mixed = inputs_own + branch
+    normed2_full, norm2_pull = jax.vjp(rms_norm, mixed, norm2_gain)
+    normed2 = normed2_full.astype(BF)
+
+    gate_w, up_w, down_w = w_gate[0], w_up[0], w_down[0]
+    normed2_far = hop(normed2, far)
+    tile = 256
+    (rows_here, hidden_here, ggp_here, gup_here, scaled_here, came_back, grad_back) = expert_stage(
+        normed2, both, cot_here, router_wide, gate_w, up_w, down_w, groups, capacity, tile
+    )
+    rows_here = rows_here.reshape(slot_count, width)
+    scaled_here = scaled_here.reshape(slot_count, width)
+    came_back = came_back.reshape(slot_count, width)
+    grad_back = grad_back.reshape(slot_count, width)
+
+    both_far, signs_far = dispatch_of(routing_far[:, :2], routing_far[:, 2:])
+    far_own = jnp.concatenate([normed2_far, cot_far_own], axis=1)
+    far_sent = jnp.concatenate([contract(both_far, far_own, 1, 0).astype(BF), signs_far], axis=1)
+    far_sent, grad_back = lax.optimization_barrier((far_sent, grad_back))
+    far_came = lax.all_to_all(
+        far_sent.reshape(experts, capacity, 2 * width + TILE),
+        "dp",
+        split_axis=0,
+        concat_axis=0,
+        tiled=True,
+    ).reshape(slot_count, 2 * width + TILE)
+    rows_far = far_came[:, :width]
+    hidden_far, ggp_far, gup_far, scaled_far = far_stage(
+        rows_far, far_came[:, width:], router_wide, gate_w, up_w, down_w, tile
+    )
+
+    low, high = me % far, me // far
+
+    def part(lefts, rights, at):
+        rows = lefts[0].shape[1] // replicas
+        return sum(
+            contract(lax.dynamic_slice_in_dim(left, at * rows, rows, 1), right, 0, 0)
+            for left, right in zip(lefts, rights)
+        )
+
+    def sent(lefts, rights):
+        return hop(part(lefts, rights, high * far + (1 - low)).astype(BF), 1)
+
+    weight_args = (
+        ((rows_here, rows_far), (ggp_here, ggp_far)),
+        ((rows_here, rows_far), (gup_here, gup_far)),
+        ((hidden_here, hidden_far), (scaled_here, scaled_far)),
+    )
+    came = [sent(*a) for a in weight_args]
+
+    logits = jnp.dot(normed2, w_router, preferred_element_type=F32)
+    chosen = (expert_ids[:, :, None] == expert_range[None, None, :]).astype(F32)
+    gates = jax.nn.softmax(jnp.sum(chosen * logits[:, None, :], axis=2), axis=-1)
+    chosen_rows = [jnp.dot(pick, came_back, preferred_element_type=F32) for pick in picks]
+    output = mixed + sum(gates[:, k : k + 1] * chosen_rows[k] for k in range(2))
+    grad_output = cotangent.astype(F32)
+    grad_gates = jnp.stack([jnp.sum(grad_output * rows, axis=1) for rows in chosen_rows], axis=1)
+    grad_normed2 = jnp.dot(picks[0] + picks[1], grad_back, preferred_element_type=F32)
+    grad_picked = gates * (grad_gates - jnp.sum(gates * grad_gates, axis=1, keepdims=True))
+    grad_logits = jnp.sum(chosen * grad_picked[:, :, None], axis=1)
+    grad_normed2 = grad_normed2 + contract(grad_logits, w_router.astype(F32), 1, 1, HIGH)
+    grad_router = contract(normed2.astype(F32), grad_logits, 0, 0, HIGH)
+    grad_mixed, grad_norm2 = norm2_pull(grad_normed2)
+    grad_mixed = grad_mixed + grad_output
+    grad_branch = grad_mixed.astype(BF)
+
+    grad_wout = contract(attended, grad_branch, 0, 0).astype(BF)
+    grad_wout = grad_wout.reshape(replicas, groups, out_rows, width)
+    grad_wout = lax.psum_scatter(grad_wout, "dp", scatter_dimension=1, tiled=True)[:, 0]
+    grad_wout = sum(
+        (hop(grad_wout[r], r) if r else grad_wout[r]).astype(F32) for r in range(replicas)
+    ).astype(BF)
+    grad_out_proj = lax.all_gather(grad_wout, "dp", axis=0, tiled=True).astype(F32)
+
+    qkv_rows = width // groups
+    piece = lax.dynamic_slice_in_dim(w_qkv, dp_at * qkv_rows, qkv_rows, 0)
+    piece, _ = lax.optimization_barrier((piece, w_out_cat))
+    w_qkv_all = lax.all_gather(piece, ("head", "dp"), axis=0, tiled=True)
+    w_qkv_all = w_qkv_all.reshape(replicas, width, 3 * head_cols)
+    grad_heads = contract(grad_branch, w_out_cat, 1, 1).astype(BF)
+    sums = jnp.zeros((heads_here, TILE, 2 * length), F32)
+    grad_blocks = [grad_heads[:, i * head_cols : (i + 1) * head_cols] for i in range(replicas)]
+    grad_normed = None
+    weight_terms = []
+    arrived = [hop(grad_blocks[r], r) if r else grad_blocks[0] for r in range(replicas)]
+    for r in (0, 2, 3, 1):
+        grad_qkv, sums = attend_bwd(order[r].reshape(1), qkv, arrived[r], probs[r], sums, length)
+        normed_seq = lax.dynamic_slice_in_dim(normed, order[r] * length, length, 0)
+        weight_terms.append(contract(normed_seq, grad_qkv, 0, 0))
+        mine = hop(grad_qkv, r) if r else grad_qkv
+        weight = lax.dynamic_index_in_dim(w_qkv_all, order[r], 0, keepdims=False)
+        term = contract(mine, weight, 1, 1)
+        grad_normed = term if grad_normed is None else grad_normed + term
+    grad_qkv_w = sum(weight_terms)
+
+    _, norm1_pull = jax.vjp(rms_norm, inputs_own, norm1_gain)
+    grad_first, grad_norm1 = norm1_pull(grad_normed)
+    grad_input = grad_mixed + grad_first
+    grad_bias = contract(unskew(sums), line, 1, 1, HIGH)
+    grad_qkv_w, grad_bias = lax.psum((grad_qkv_w.astype(BF), grad_bias), "dp")
+    grad_qkv_w = grad_qkv_w.astype(F32)
+    grad_norm1, grad_norm2, grad_router = lax.psum(
+        (grad_norm1, grad_norm2, grad_router), ("dp", "head")
+    )
+    came, _ = lax.optimization_barrier((came, grad_normed))
+    grad_gate_w, grad_up_w, grad_down_w = (
+        (part(*a, me) + piece.astype(F32))[None] for a, piece in zip(weight_args, came)
+    )
+    return (
+        output,
+        grad_input,
+        grad_norm1,
+        grad_qkv_w[:, :head_cols],
+        grad_qkv_w[:, head_cols : 2 * head_cols],
+        grad_qkv_w[:, 2 * head_cols :],
+        grad_out_proj,
+        jnp.transpose(grad_bias),
+        grad_norm2,
+        grad_router,
+        grad_gate_w,
+        grad_up_w,
+        grad_down_w,
+    )
+
+
 def solution(mesh):
     placed = (
         P("dp", None),

time: 796 us -> 682 us (0.86)
  Pallas kernels: 54.4 us -> 230 us
  waiting for transfers between devices: 259 us -> 104 us
  matrix products: 265 us -> 114 us
  starting transfers between devices: 55.2 us -> 30.4 us
  other arithmetic: 18.1 us -> 35.9 us
  local copies, waits for them, and re-layouts: 26.9 us -> 40.4 us
    pallas_call x4 -> x3, Pallas kernels: 22.2 us -> 197 us  [the longest x1 109 us: expert_stage(): pl.pallas_call(functools.partial(expert_kernel, width, tile), out_shape=(...]
    dot_general x11 -> x6, matrix products: 101 us -> 17.8 us  [the longest x2 6.52 us: body_steps(): jnp.dot(pick, came_back, preferred_element_type=F32)]
    ppermute x4 -> x0, waiting for transfers between devices: 69.3 us -> none  [the longest x1 65.9 us: body(): dest_far = lax.ppermute(dest, 'head', far_perm)]
    dot_general x34 -> x30, matrix products: 163 us -> 95.8 us  [contract(): lax.dot_general(left, right, (((left_dim,), (right_dim,)), ((), ())), pre...]
    ppermute x15, waiting for transfers between devices: 123 us -> 70.5 us  [hop(): return lax.ppermute(value, 'head', [(i, i ^ r) for i in range(replicas)])]
    all_to_all x7 -> x1, waiting for transfers between devices: 51.3 us -> 0.01 us  [body_steps(): lax.all_to_all(far_sent.reshape(experts, capacity, 2 * width + TILE), 'dp...]
    psum x2, blocking collectives: 52.5 us -> 93.6 us  [the longest x1 53.3 us: body_steps(): grad_qkv_w, grad_bias = lax.psum((grad_qkv_w.astype(BF), grad_bias), 'dp')]
    all_to_all x1 -> x0, blocking collectives: 34.9 us -> none  [exchange(): lax.all_to_all(parts, 'dp', split_axis=0, concat_axis=0, tiled=True)]
  transfers between devices with their start and end apart: 29 -> 19, of which waited for: 15 -> 5; matrix products, arithmetic and copies ran while one was open for 31% -> 22% of each run, Pallas kernels for 7% -> 33%
where the time goes in v2:
time: 682 us; the launch traced here: 672 us
  Pallas kernels  230 us (34%)
  matrix products  114 us (17%)
  waiting for transfers between devices  104 us (15%)
  blocking collectives  103 us (15%)
  local copies, waits for them, and re-layouts  40.4 us (6%)
  other arithmetic  35.9 us (5%)
  starting transfers between devices  30.4 us (4%)
  between operations  15.1 us (2%)
    pallas_call x1, Pallas kernels, expert_stage(): pl.pallas_call(functools.partial(expert_kernel, width, tile), out_shape=(...  109 us
    dot_general x30, matrix products, contract(): lax.dot_general(left, right, (((left_dim,), (right_dim,)), ((), ())), pre...  95.8 us
    ppermute x15, waiting for transfers between devices, hop(): return lax.ppermute(value, 'head', [(i, i ^ r) for i in range(replicas)])  70.5 us
    psum x1, blocking collectives, body_steps(): grad_qkv_w, grad_bias = lax.psum((grad_qkv_w.astype(BF), grad_bias), 'dp')  53.3 us
    pallas_call x1, Pallas kernels, attend_all(): pl.pallas_call(functools.partial(attend_all_kernel, groups, replicas), ou...  51.3 us
    psum x1, blocking collectives, body_steps(): lax.psum((grad_norm1, grad_norm2, grad_router), ('dp', 'head'))  40.3 us
    pallas_call x1, Pallas kernels, far_stage(): pl.pallas_call(functools.partial(far_kernel, width), out_shape=(unit_shap...  35.9 us
    pallas_call x4, Pallas kernels, attend_bwd(): pl.pallas_call(attend_bwd_kernel, out_shape=(jax.ShapeDtypeStruct((length...  26.3 us
  transfers between devices with their start and end apart: 19, of which 5 were waited for; matrix products, arithmetic and copies ran while one was open for 22% of the time, Pallas kernels for 33%

profile of v2, /device:TPU:0, one launch (start us, length us, event | category | flops | bytes accessed | tf_op | source)
XLA Modules:
  0.0 672.3 jit_solution(6090416239627132974)
XLA Ops:
  12.9 4.1 collective-permute-start
  24.4 3.7 skew.1.table_ref
  28.1 5.5 copy.46
  34.5 3.6 fusion
  39.6 4.7 convolution_convert_fusion.2.qkv_ref.q_ref.k_ref.v_ref
  44.3 51.3 %attend_all.1 = (bf16[512,1024]{1,0:T(8,128)(2,1)S(1)}, bf16[4,4,512,512]{3,2,1,0:T(8,128)(2,1)}, bf16[8,160,1152]{2,1,0:T(8,128)(2,1)S(1)}) custom-call(bf16[2048,768]{1,0:T(8,128)(2,1)} %convolution_convert_fusion.2.qkv_ref.q_ref.k_ref.v_ref, f32[4,128,1024]{2,1,0:T(8,128)S(1)} %skew.1.table_ref, bf16[8,160,1152]{2,1,0:T(8,128)(2,1)} %bitcast.138), custom_call_target="tpu_custom_call" | custom-call | flops 4294967296 | bytes 16777216 | tf_op jit(solution)/shard_map/attend_all/pallas_call | solution.py:389
  97.3 1.9 fusion.34.both_ref
  99.2 5.8 slice_bitcast_fusion
  108.6 3.3 multiply_reduce_fusion.2
  114.5 109.5 %expert_stage.1 = (bf16[8,160,1024]{2,1,0:T(8,128)(2,1)}, bf16[1280,2816]{1,0:T(8,128)(2,1)}, bf16[1280,2816]{1,0:T(8,128)(2,1)}, bf16[1280,2816]{1,0:T(8,128)(2...) custom-call(bf16[512,1024]{1,0:T(8,128)(2,1)} %multiply_convert_fusion.normed_ref, ...), custom_call_target="tpu_custom_call" | custom-call | flops 44291850240 | bytes 38928384 | tf_op jit(solution)/shard_map/expert_stage/pallas_call | solution.py:630
  224.0 3.4 fusion.6
  227.5 3.1 fusion.13
  232.3 4.8 convolution_convert_fusion
  237.2 3.0 pad_maximum_fusion
  244.3 2.2 convert_add_fusion.1
  247.8 2.7 convolution_convert_fusion.5
  251.7 3.2 collective-permute-start.5
  256.6 6.3 attend_bwd.4
  262.9 2.7 fusion.76
  265.7 11.4 %collective-permute-done.3.grad_ref = bf16[512,256]{1,0:T(8,128)(2,1)S(1)} collective-permute-done((bf16[512,256]{1,0:T(8,128)(2,1)S(1)}, bf16[512,256]{1,0:T(8,128)(2,1)S(1)}, u32[]{:S(2)}, u32[]{:S(2)}) %collective-permute-start.3) | collective-permute-done | bytes 262176 | tf_op jit(solution)/shard_map/ppermute | solution.py:1054
  277.1 6.5 attend_bwd.5
  284.9 7.3 %attend_bwd.6 = (bf16[512,768]{1,0:T(8,128)(2,1)}, f32[4,128,1024]{2,1,0:T(8,128)S(1)}) custom-call(s32[1]{0:T(128)} %bitcast.34.seq_ref, bf16[2048,768]{1,0:T(8,128)(2,1)} %convolution_convert_fusion.2.qkv_ref.q_ref.k_ref.v_ref, bf16[2048,768]{1,0:T(8,128)(2,1)} %convolution_convert_fusion.2.qkv_ref.q_ref.k_ref.v_ref, ...), custom_call_target="tpu_custom_call" | custom-call | flops 2147483648 | bytes 4194304 | tf_op jit(solution)/shard_map/attend_bwd/pallas_call | solution.py:218
  292.2 4.3 fusion.72
  296.5 2.7 fusion.74
  299.2 6.3 attend_bwd.7
  305.5 6.0 add_convert_fusion
  313.3 5.2 all-to-all-start
  322.4 6.4 fusion.25
  328.9 6.9 %fusion.88 = f32[256,2816]{1,0:T(8,128)} fusion(bf16[1280,2816]{1,0:T(8,128)(2,1)} %get-tuple-element.57, bf16[1280,1024]{1,0:T(8,128)(2,1)S(1)} %bitcast.139, s32[]{:T(128)S(6)} %select_n.101), kind=kOutput, calls=%fused_computation.127 | convolution fusion | flops 1845493760 | bytes 10747908 | tf_op jit(solution)/shard_map/dot_general | solution.py:31
  335.8 3.7 fusion.82
  339.5 3.7 fusion.80
  343.2 3.7 fusion.86
  346.9 2.6 collective-permute-start.6
  349.5 3.1 unskew.1
  352.8 53.3 %psum.37 = f32[32,4]{0,1:T(4,128)} all-reduce(f32[32,4]{0,1:T(4,128)S(1)} %fusion.111), channel_id=1, replica_groups=mesh['dp'=8,'head'=4] {'dp'}, use_global_device_ids=true, to_apply=%region_17.18 | all-reduce | flops 128 | bytes 1024 | tf_op jit(solution)/shard_map/psum | solution.py:1200
  406.1 21.7 %all-reduce.7.cloned.1.call-done = (bf16[1024,768]{1,0:T(8,128)(2,1)}, bf16[4,8,32,1024]{3,2,1,0:T(8,128)(2,1)}) async-done(((bf16[1024,768]{1,0:T(8,128)(2,1)}, bf16[4,8,32,1024]{3,2,1,0:T(8,128)(2,1)}), (bf16[1024,768]{1,0:T(8,128)(2,1)}, bf16[4,8,32,1024]{3,2,1,0:T(8,128)(2,1)})) %all-reduce.7.cloned.1.call-update) | async-done | bytes 3670032 | tf_op jit(solution)/shard_map/psum | solution.py:1200
  429.4 3.4 collective-permute-start.11
  433.8 3.2 fusion.144
  437.0 2.1 collective-permute-start.4
  440.6 9.8 %all_gather.11 = bf16[256,1024]{1,0:T(8,128)(2,1)S(1)} all-gather(bf16[32,1024]{1,0:T(8,128)(2,1)S(1)} %fusion.105), channel_id=1, replica_groups=mesh['dp'=8,'head'=4] {'dp'}, dimensions={0}, use_global_device_ids=true | all-gather | bytes 589824 | tf_op jit(solution)/shard_map/all_gather | solution.py:1173
  451.5 2.0 slice.145.rows_ref
  453.5 3.8 slice.146.cot_ref
  457.3 35.9 %far_stage.1 = (bf16[1280,2816]{1,0:T(8,128)(2,1)}, bf16[1280,2816]{1,0:T(8,128)(2,1)}, bf16[1280,2816]{1,0:T(8,128)(2,1)}, bf16[1280,1024]{1,0:T(8,128)(2,1)S(1)}) custom-call(bf16[1280,1024]{1,0:T(8,128)(2,1)S(1)} %slice.145.rows_ref, bf16[1280,1152]{1,0:T(8,128)(2,1)} %slice.146.cot_ref, bf16[1024,128]{1,0:T(8,128)(2,1)S(1)} %copy-done.10, ...), custom_call_target="tpu_custom_call" | custom-call | flops 22145925120 | bytes 38928384 | tf_op jit(solution)/shard_map/far_stage/pallas_call | solution.py:714
  493.2 7.3 %fusion.3 = bf16[256,2816]{1,0:T(8,128)(2,1)} fusion(f32[256,2816]{1,0:T(8,128)} %fusion.82, bf16[1280,2816]{1,0:T(8,128)(2,1)} %get-tuple-element.59, bf16[1280,1024]{1,0:T(8,128)(2,1)S(1)} %slice.145.rows_ref, s32[]{:T(128)S(6)} %select_n.104), kind=kOutput, calls=%fused_computation.17 | convolution fusion | flops 1846935552 | bytes 12189700 | tf_op jit(solution)/shard_map/dot_general | solution.py:31
  500.5 1.8 collective-permute-start.12
  502.3 3.2 fusion.4
  505.7 3.8 fusion.23
  509.6 2.3 fusion.27
  512.3 3.7 convolution_add_fusion.3
  516.0 3.9 convolution_add_fusion
  519.9 5.1 add_convert_fusion.1
  525.0 11.5 %all-gather.5.cloned.1.call-done = bf16[4096,768]{1,0:T(8,128)(2,1)} async-done(((bf16[128,768]{1,0:T(8,128)(2,1)}), bf16[4096,768]{1,0:T(8,128)(2,1)}) %all-gather.5.cloned.1.call-update) | async-done | bytes 6291472 | tf_op jit(solution)/shard_map/all_gather | solution.py:1178
  536.5 2.6 fusion.41
  539.1 5.3 collective-permute-start.14
  544.4 2.7 fusion.37
  547.1 2.3 fusion.39
  549.5 2.8 fusion.19
  552.3 1.9 fusion.15
  554.2 28.7 %collective-permute-done.13 = bf16[256,2816]{1,0:T(8,128)(2,1)} collective-permute-done((bf16[256,2816]{1,0:T(8,128)(2,1)}, bf16[256,2816]{1,0:T(8,128)(2,1)}, u32[]{:S(2)}, u32[]{:S(2)}) %collective-permute-start.13) | collective-permute-done | bytes 1441824 | tf_op jit(solution)/shard_map/ppermute | solution.py:1054
  582.9 30.3 %collective-permute-done.14 = bf16[704,1024]{1,0:T(8,128)(2,1)S(1)} collective-permute-done((bf16[704,1024]{1,0:T(8,128)(2,1)S(1)}, bf16[704,1024]{1,0:T(8,128)(2,1)S(1)}, u32[]{:S(2)}, u32[]{:S(2)}) %collective-permute-start.14) | collective-permute-done | bytes 1441824 | tf_op jit(solution)/shard_map/ppermute | solution.py:1054
  613.2 3.8 add_bitcast_fusion.2
  617.0 3.4 add_bitcast_fusion.1
  620.4 40.3 %all-reduce.3 = (f32[1024]{0:T(1024)}, f32[1024]{0:T(1024)}, f32[1024,8]{0,1:T(8,128)}) all-reduce(f32[1024]{0:T(1024)S(1)} %get-tuple-element.69, f32[1024]{0:T(1024)S(1)} %get-tuple-element.71, f32[1024,8]{0,1:T(8,128)S(1)} %fusion.152), channel_id=1, replica_groups=mesh['dp'=8,'head'=4] {'dp','head'}, use_global_device_ids=true, to_apply=%region_14.15 | all-reduce | flops 10240 | bytes 81920 | tf_op jit(solution)/shard_map/psum | solution.py:1202
  660.7 4.6 add_bitcast_fusion
  (239 shorter events, 46.3 us)
Async XLA Ops:
  7.2 99.6 %all-gather.3.cloned.1.call-start = ((), (), s32[]{:S(2)}) async-start(), calls=%async_computation.1 | async-start | bytes 2162688 | tf_op jit(solution)/shard_map/all_gather | solution.py:1083
  8.9 418.9 %all-reduce.7.cloned.1.call-start = ((), (), s32[]{:S(2)}) async-start(), calls=%async_computation.3 | async-start | bytes 7340032 | tf_op jit(solution)/shard_map/psum | solution.py:1200
  8.9 9.1 %copy-start.37 = (bf16[512,1024]{1,0:T(8,128)(2,1)S(1)}, bf16[512,1024]{1,0:T(8,128)(2,1)}, u32[]{:S(2)}) copy-start(bf16[512,1024]{1,0:T(8,128)(2,1)} %param.17) | copy-start | bytes 3145732
  12.9 93.0 %collective-permute-start = (s32[512,4]{0,1:T(4,128)S(1)}, s32[512,4]{0,1:T(4,128)S(1)}, u32[]{:S(2)}, u32[]{:S(2)}) collective-permute-start(s32[512,4]{0,1:T(4,128)S(1)} %pad_add_fusion), channel_id=1, source_target_pairs={{0,2},{1,3},{2,0},{3,1},{4,6},{5,7},{6,4},{7,5},{8,10},{9,11},{10,... | collective-permute-start | bytes 24584 | tf_op jit(solution)/shard_map/ppermute | solution.py:1054
  17.0 215.3 %collective-permute-start.2 = (bf16[512,1024]{1,0:T(8,128)(2,1)}, bf16[512,1024]{1,0:T(8,128)(2,1)}, u32[]{:S(2)}, u32[]{:S(2)}) collective-permute-start(bf16[512,1024]{1,0:T(8,128)(2,1)} %param.17), channel_id=1, source_target_pairs={{0,2},{1,3},{2,0},{3,1},{4,6},{5,7},{6,4},{7,5},{8,10},{9,11},{10,... | collective-permute-start | bytes 3145736 | tf_op jit(solution)/shard_map/ppermute | solution.py:1054
  18.0 3.4 copy-start.61
  28.1 5.5 copy-start.42
  33.6 4.6 copy-start.16
  33.6 4.6 copy-start.57
  39.6 4.7 copy-start.28
  99.2 5.8 copy-start.55
  108.5 3.4 copy-start.43
  108.5 3.4 copy-start.45
  108.5 4.7 copy-start.59
  114.5 117.9 %collective-permute-start.1 = (bf16[512,1024]{1,0:T(8,128)(2,1)}, bf16[512,1024]{1,0:T(8,128)(2,1)}, u32[]{:S(2)}, u32[]{:S(2)}) collective-permute-start(bf16[512,1024]{1,0:T(8,128)(2,1)} %multiply_convert_fusion.normed_ref), channel_id=1, source_target_pairs={{0,2},{1,3},{2,0},{3,1},{4,6},{5,7},{6,4},{7,5},{8,10},{9,11},{10,... | collective-permute-start | bytes 3145736 | tf_op jit(solution)/shard_map/ppermute | solution.py:1054
  223.9 3.5 copy-start.38
  223.9 3.5 copy-start.64
  227.4 4.7 copy-start.56
  250.5 6.1 copy-start.4
  250.5 48.7 %collective-permute-start.7 = (bf16[512,256]{1,0:T(8,128)(2,1)S(1)}, bf16[512,256]{1,0:T(8,128)(2,1)S(1)}, u32[]{:S(2)}, u32[]{:S(2)}) collective-permute-start(bf16[512,256]{1,0:T(8,128)(2,1)S(1)} %get-tuple-element.98), channel_id=1, source_target_pairs={{0,1},{1,0},{2,3},{3,2},{4,5},{5,4},{6,7},{7,6},{8,9},{9,8},{10,11... | collective-permute-start | bytes 786440 | tf_op jit(solution)/shard_map/ppermute | solution.py:1054
  251.7 33.2 %collective-permute-start.5 = (bf16[512,256]{1,0:T(8,128)(2,1)S(1)}, bf16[512,256]{1,0:T(8,128)(2,1)S(1)}, u32[]{:S(2)}, u32[]{:S(2)}) collective-permute-start(bf16[512,256]{1,0:T(8,128)(2,1)S(1)} %get-tuple-element.99), channel_id=1, source_target_pairs={{0,3},{1,2},{2,1},{3,0},{4,7},{5,6},{6,5},{7,4},{8,11},{9,10},{10,... | collective-permute-start | bytes 786440 | tf_op jit(solution)/shard_map/ppermute | solution.py:1054
  255.0 22.1 %collective-permute-start.3 = (bf16[512,256]{1,0:T(8,128)(2,1)S(1)}, bf16[512,256]{1,0:T(8,128)(2,1)S(1)}, u32[]{:S(2)}, u32[]{:S(2)}) collective-permute-start(bf16[512,256]{1,0:T(8,128)(2,1)S(1)} %get-tuple-element.100), channel_id=1, source_target_pairs={{0,2},{1,3},{2,0},{3,1},{4,6},{5,7},{6,4},{7,5},{8,10},{9,11},{10,... | collective-permute-start | bytes 786440 | tf_op jit(solution)/shard_map/ppermute | solution.py:1054
  256.6 6.3 copy-start.29
  262.9 14.2 %copy-start.3 = (bf16[4,512,512]{2,1,0:T(8,128)(2,1)S(1)}, bf16[4,512,512]{2,1,0:T(8,128)(2,1)}, u32[]{:S(2)}) copy-start(bf16[4,512,512]{2,1,0:T(8,128)(2,1)} %get-tuple-element.84.probs_ref) | copy-start | bytes 6291460
  277.1 7.8 %copy-start.2 = (bf16[4,512,512]{2,1,0:T(8,128)(2,1)S(1)}, bf16[4,512,512]{2,1,0:T(8,128)(2,1)}, u32[]{:S(2)}) copy-start(bf16[4,512,512]{2,1,0:T(8,128)(2,1)} %get-tuple-element.83.probs_ref) | copy-start | bytes 6291460
  284.9 11.6 %copy-start.13 = (bf16[512,768]{1,0:T(8,128)(2,1)}, bf16[512,768]{1,0:T(8,128)(2,1)S(1)}, u32[]{:S(2)}) copy-start(bf16[512,768]{1,0:T(8,128)(2,1)S(1)} %get-tuple-element.50) | copy-start | bytes 2359300
  292.2 4.3 copy-start.7
  299.2 6.3 copy-start.30
  305.5 6.1 copy-start.5
  311.6 224.9 %all-gather.5.cloned.1.call-start = ((), (), s32[]{:S(2)}) async-start(), calls=%async_computation.2 | async-start | bytes 6488064 | tf_op jit(solution)/shard_map/all_gather | solution.py:1178
  313.3 5.3 copy-start.65
  313.3 138.2 %all-to-all-start = ((bf16[8,160,2176]{2,1,0:T(8,128)(2,1)}), bf16[8,160,2176]{2,1,0:T(8,128)(2,1)}, u32[]{:S(2)}, u32[]{:S(2)}) async-start(bf16[8,160,2176]{2,1,0:T(8,128)(2,1)} %bitcast.137), calls=%async_computation | async-start | bytes 11141120 | tf_op jit(solution)/shard_map/all_to_all | solution.py:1120
  322.4 6.4 copy-start.31
  322.4 13.4 %slice-start.2 = ((s8[7208960]{0:T(1024)(128)(4,1)}), s8[4194304]{0:T(1024)(128)(4,1)S(1)}, s32[]{:S(2)}) async-start(s8[7208960]{0:T(1024)(128)(4,1)} %bitcast.131), calls=%async_computation.6 | async-start | bytes 8388608
  328.9 7.0 %slice-start.3 = ((s8[7208960]{0:T(1024)(128)(4,1)}), s8[3014656]{0:T(1024)(128)(4,1)S(1)}, s32[]{:S(2)}) async-start(s8[7208960]{0:T(1024)(128)(4,1)} %bitcast.131), calls=%async_computation.7 | async-start | bytes 6029312
  328.9 10.7 %slice-start = ((s8[7208960]{0:T(1024)(128)(4,1)}), s8[4194304]{0:T(1024)(128)(4,1)S(1)}, s32[]{:S(2)}) async-start(s8[7208960]{0:T(1024)(128)(4,1)} %bitcast.129), calls=%async_computation.4 | async-start | bytes 8388608
  335.8 3.7 slice-start.1
  343.2 6.3 copy-start.6
  343.2 9.4 %copy-start.54 = (pred[32,1023]{1,0:T(32,128)(4,1)S(1)}, pred[32,1023]{1,0:T(32,128)(4,1)}, u32[]{:S(2)}) copy-start(pred[32,1023]{1,0:T(32,128)(4,1)} %copy-done.53) | copy-start | bytes 98212
  346.9 202.5 %collective-permute-start.8 = (bf16[512,768]{1,0:T(8,128)(2,1)S(1)}, bf16[512,768]{1,0:T(8,128)(2,1)}, u32[]{:S(2)}, u32[]{:S(2)}) collective-permute-start(bf16[512,768]{1,0:T(8,128)(2,1)S(1)} %get-tuple-element.54), channel_id=1, source_target_pairs={{0,1},{1,0},{2,3},{3,2},{4,5},{5,4},{6,7},{7,6},{8,9},{9,8},{10,11... | collective-permute-start | bytes 2359304 | tf_op jit(solution)/shard_map/ppermute | solution.py:1054
  346.9 192.2 %collective-permute-start.6 = (bf16[512,768]{1,0:T(8,128)(2,1)}, bf16[512,768]{1,0:T(8,128)(2,1)}, u32[]{:S(2)}, u32[]{:S(2)}) collective-permute-start(bf16[512,768]{1,0:T(8,128)(2,1)} %get-tuple-element.52), channel_id=1, source_target_pairs={{0,3},{1,2},{2,1},{3,0},{4,7},{5,6},{6,5},{7,4},{8,11},{9,10},{10,... | collective-permute-start | bytes 2359304 | tf_op jit(solution)/shard_map/ppermute | solution.py:1054
  429.4 7.6 %collective-permute-start.11 = (bf16[32,1024]{1,0:T(8,128)(2,1)S(1)}, bf16[32,1024]{1,0:T(8,128)(2,1)S(1)}, u32[]{:S(2)}, u32[]{:S(2)}) collective-permute-start(bf16[32,1024]{1,0:T(8,128)(2,1)S(1)} %get-tuple-element.88), channel_id=1, source_target_pairs={{0,3},{1,2},{2,1},{3,0},{4,7},{5,6},{6,5},{7,4},{8,11},{9,10},{10,... | collective-permute-start | bytes 196616 | tf_op jit(solution)/shard_map/ppermute | solution.py:1054
  432.8 6.3 collective-permute-start.10
  432.8 6.3 collective-permute-start.9
  437.0 110.0 %collective-permute-start.4 = (bf16[512,768]{1,0:T(8,128)(2,1)S(1)}, bf16[512,768]{1,0:T(8,128)(2,1)}, u32[]{:S(2)}, u32[]{:S(2)}) collective-permute-start(bf16[512,768]{1,0:T(8,128)(2,1)S(1)} %copy-done.14), channel_id=1, source_target_pairs={{0,2},{1,3},{2,0},{3,1},{4,6},{5,7},{6,4},{7,5},{8,10},{9,11},{10,... | collective-permute-start | bytes 2359304 | tf_op jit(solution)/shard_map/ppermute | solution.py:1054
  453.5 3.8 copy-start.10
  493.1 9.2 %slice-start.4 = ((s8[7208960]{0:T(1024)(128)(4,1)}), s8[4194304]{0:T(1024)(128)(4,1)S(1)}, s32[]{:S(2)}) async-start(s8[7208960]{0:T(1024)(128)(4,1)} %bitcast.133), calls=%async_computation.8 | async-start | bytes 8388608
  493.1 9.2 %slice-start.5 = ((s8[7208960]{0:T(1024)(128)(4,1)}), s8[3014656]{0:T(1024)(128)(4,1)S(1)}, s32[]{:S(2)}) async-start(s8[7208960]{0:T(1024)(128)(4,1)} %bitcast.133), calls=%async_computation.9 | async-start | bytes 6029312
  493.1 9.2 %copy-start.21 = (f32[256,2816]{1,0:T(8,128)S(1)}, f32[256,2816]{1,0:T(8,128)}, u32[]{:S(2)}) copy-start(f32[256,2816]{1,0:T(8,128)} %fusion.80) | copy-start | bytes 8650756
  493.1 12.6 %slice-start.8 = ((s8[7208960]{0:T(1024)(128)(4,1)}), s8[4194304]{0:T(1024)(128)(4,1)S(1)}, s32[]{:S(2)}) async-start(s8[7208960]{0:T(1024)(128)(4,1)} %bitcast.145), calls=%async_computation.12 | async-start | bytes 8388608
  500.5 53.7 %collective-permute-start.12 = (bf16[256,2816]{1,0:T(8,128)(2,1)}, bf16[256,2816]{1,0:T(8,128)(2,1)}, u32[]{:S(2)}, u32[]{:S(2)}) collective-permute-start(bf16[256,2816]{1,0:T(8,128)(2,1)} %fusion.3), channel_id=1, source_target_pairs={{0,1},{1,0},{2,3},{3,2},{4,5},{5,4},{6,7},{7,6},{8,9},{9,8},{10,11... | collective-permute-start | bytes 4325384 | tf_op jit(solution)/shard_map/ppermute | solution.py:1054
  502.3 3.4 slice-start.9
  505.5 77.4 %collective-permute-start.13 = (bf16[256,2816]{1,0:T(8,128)(2,1)}, bf16[256,2816]{1,0:T(8,128)(2,1)}, u32[]{:S(2)}, u32[]{:S(2)}) collective-permute-start(bf16[256,2816]{1,0:T(8,128)(2,1)} %fusion.4), channel_id=1, source_target_pairs={{0,1},{1,0},{2,3},{3,2},{4,5},{5,4},{6,7},{7,6},{8,9},{9,8},{10,11... | collective-permute-start | bytes 4325384 | tf_op jit(solution)/shard_map/ppermute | solution.py:1054
  505.7 6.1 slice-start.6
  512.3 3.7 copy-start.25
  516.0 3.9 copy-start.32
  519.9 16.6 %copy-start.12 = (bf16[512,768]{1,0:T(8,128)(2,1)S(1)}, bf16[512,768]{1,0:T(8,128)(2,1)}, u32[]{:S(2)}) copy-start(bf16[512,768]{1,0:T(8,128)(2,1)} %copy-done.11) | copy-start | bytes 2359300
  536.5 10.6 %copy-start.51 = (bf16[4096,768]{1,0:T(8,128)(2,1)S(1)}, bf16[4096,768]{1,0:T(8,128)(2,1)}, u32[]{:S(2)}) copy-start(bf16[4096,768]{1,0:T(8,128)(2,1)} %all-gather.5.cloned.1.call-done) | copy-start | bytes 18874372
  539.1 74.2 %collective-permute-start.14 = (bf16[704,1024]{1,0:T(8,128)(2,1)S(1)}, bf16[704,1024]{1,0:T(8,128)(2,1)S(1)}, u32[]{:S(2)}, u32[]{:S(2)}) collective-permute-start(bf16[704,1024]{1,0:T(8,128)(2,1)S(1)} %copy-done.62), channel_id=1, source_target_pairs={{0,1},{1,0},{2,3},{3,2},{4,5},{5,4},{6,7},{7,6},{8,9},{9,8},{10,11... | collective-permute-start | bytes 4325384 | tf_op jit(solution)/shard_map/ppermute | solution.py:1054
  552.3 60.9 %copy-start.22 = (f32[256,2816]{1,0:T(8,128)S(1)}, f32[256,2816]{1,0:T(8,128)}, u32[]{:S(2)}) copy-start(f32[256,2816]{1,0:T(8,128)} %convolution_add_fusion.3) | copy-start | bytes 8650756
  554.2 62.8 %copy-start.23 = (f32[256,2816]{1,0:T(8,128)S(1)}, f32[256,2816]{1,0:T(8,128)}, u32[]{:S(2)}) copy-start(f32[256,2816]{1,0:T(8,128)} %convolution_add_fusion) | copy-start | bytes 8650756
  613.2 3.8 copy-start.36
  617.0 43.7 %copy-start.20 = (f32[704,1024]{1,0:T(8,128)S(1)}, f32[704,1024]{1,0:T(8,128)}, u32[]{:S(2)}) copy-start(f32[704,1024]{1,0:T(8,128)} %fusion.25) | copy-start | bytes 8650756
  620.4 45.0 %copy-start.1 = (bf16[256,1024]{1,0:T(8,128)(2,1)S(1)}, bf16[256,1024]{1,0:T(8,128)(2,1)}, u32[]{:S(2)}) copy-start(bf16[256,1024]{1,0:T(8,128)(2,1)} %param.25) | copy-start | bytes 1572868
  (31 other events, 68.6 us)
Sparse Core Ops, SparseCore 0:
  11.5 91.0 all-gather.2
  311.7 116.0 all-reduce.6
  431.1 105.3 all-gather.4

commit v3 on v2

--- a/solution.py
+++ b/solution.py
@@ -17,6 +17,7 @@
 VMEM_MOST = 60 << 20
 GELU_A = 0.7978845608028654
 GELU_B = 0.044715
+PEERS = [2, 4, 3, 5, 6, 7, 1]
 
 
 def rms_norm(value, gain):
@@ -271,17 +272,23 @@
 
 
 def attend_all_kernel(
-    groups,
-    replicas,
-    qkv_ref,
+    input_ref,
+    gain_ref,
+    query_ref,
+    key_ref,
+    value_ref,
     table_ref,
     sent_ref,
     out_ref,
     probs_ref,
     came_ref,
+    normed_out,
+    qkv_out,
     acc_ref,
     block_ref,
     hold_ref,
+    normed_ref,
+    qkv_ref,
     row_send,
     row_recv,
     hop_send,
@@ -291,17 +298,15 @@
 ):
     z, d = lax.axis_index("head"), lax.axis_index("dp")
     heads, _, _ = table_ref.shape
-    length = block_ref.shape[1]
-    columns = block_ref.shape[2]
+    replicas, length, columns = block_ref.shape
     pairs = heads // 2
     lanes = columns // pairs
     half = lanes // 2
     chunk = 2 * TILE
     hops = range(1, replicas)
-    offs = [2, 4, 3, 5, 6, 7, 1]
-    greet([{"dp": flipped(d, o)} for o in offs] + [{"head": flipped(z, r)} for r in hops])
+    greet([{"dp": flipped(d, o)} for o in PEERS] + [{"head": flipped(z, r)} for r in hops])
     copies = []
-    for o in offs:
+    for o in PEERS:
         copies.append(
             remote(
                 sent_ref.at[o],
@@ -317,15 +322,29 @@
 
     moves = []
     for turn, r in enumerate(reversed(range(replicas))):
-        start = pl.multiple_of(flipped(z, r) * length, length)
+        start = flipped(z, r) * length
         slot = turn % 2
         if turn >= 2:
-            moves[turn - 2].wait()
-
-        def pair_step(pair, carry, start=start, slot=slot, r=r):
+            for move in moves[turn - 2]:
+                move.wait()
+
+        def norm_step(i, carry, start=start, slot=slot):
+            rows = pl.multiple_of(start + i * TILE, TILE)
+            value = input_ref[pl.ds(rows, TILE), :].astype(F32)
+            value = rms_norm(value, gain_ref[...])
+            normed_ref[slot, pl.ds(pl.multiple_of(i * TILE, TILE), TILE), :] = value.astype(BF)
+            return carry
+
+        lax.fori_loop(0, length // TILE, norm_step, 0)
+        for i, weight in enumerate((query_ref, key_ref, value_ref)):
+            qkv_ref[slot, :, i * columns : (i + 1) * columns] = jnp.dot(
+                normed_ref[slot], weight[...], preferred_element_type=F32
+            ).astype(BF)
+
+        def pair_step(pair, carry, slot=slot, r=r):
             def part_of(j):
                 at = pl.multiple_of(j * columns + pair * lanes, lanes)
-                return qkv_ref[pl.ds(start, length), pl.ds(at, lanes)]
+                return qkv_ref[slot, :, pl.ds(at, lanes)]
 
             key = part_of(1)
             value_t = part_of(2).T
@@ -358,9 +377,16 @@
             return carry
 
         lax.fori_loop(0, pairs, pair_step, 0)
-        move = pltpu.make_async_copy(hold_ref.at[slot], probs_ref.at[r], hold_sem.at[slot])
-        move.start()
-        moves.append(move)
+        moves.append(
+            [
+                pltpu.make_async_copy(ref.at[slot], out.at[r], hold_sem.at[i, slot])
+                for i, (ref, out) in enumerate(
+                    ((hold_ref, probs_ref), (normed_ref, normed_out), (qkv_ref, qkv_out))
+                )
+            ]
+        )
+        for move in moves[-1]:
+            move.start()
         target = out_ref.at[:, pl.ds(r * columns, columns)]
         if r:
             hop = remote(
@@ -371,39 +397,44 @@
         else:
             last = pltpu.make_async_copy(block_ref.at[0], target, own_sem.at[1])
             last.start()
-    moves[-2].wait()
-    moves[-1].wait()
+    for move in moves[-2] + moves[-1]:
+        move.wait()
     own.wait()
     last.wait()
     for copy in copies:
         copy.wait()
 
 
-def attend_all(qkv, table, sent, length, replicas):
-    heads, _, width = table.shape
-    columns = qkv.shape[1] // 3
+def attend_all(inputs, gain, weights, table, sent, length, replicas):
+    heads, _, _ = table.shape
+    width = inputs.shape[1]
+    columns = weights[0].shape[1]
     lanes = 2 * columns // heads
     groups = sent.shape[0]
     vmem = pl.BlockSpec(memory_space=pltpu.VMEM)
     hbm = pl.BlockSpec(memory_space=pl.ANY)
     return pl.pallas_call(
-        functools.partial(attend_all_kernel, groups, replicas),
+        attend_all_kernel,
         out_shape=(
             jax.ShapeDtypeStruct((length, replicas * columns), BF),
             jax.ShapeDtypeStruct((replicas, heads, length, length), BF),
             jax.ShapeDtypeStruct(sent.shape, BF),
+            jax.ShapeDtypeStruct((replicas, length, width), BF),
+            jax.ShapeDtypeStruct((replicas, length, 3 * columns), BF),
         ),
-        in_specs=[vmem, vmem, hbm],
-        out_specs=[hbm, hbm, hbm],
+        in_specs=[vmem] * 6 + [hbm],
+        out_specs=[hbm] * 5,
         scratch_shapes=[
             pltpu.VMEM((lanes, length), F32),
             pltpu.VMEM((replicas, length, columns), BF),
             pltpu.VMEM((2, heads, length, length), BF),
+            pltpu.VMEM((2, length, width), BF),
+            pltpu.VMEM((2, length, 3 * columns), BF),
             pltpu.SemaphoreType.DMA((groups,)),
             pltpu.SemaphoreType.DMA((groups,)),
             pltpu.SemaphoreType.DMA((replicas,)),
             pltpu.SemaphoreType.DMA((replicas,)),
-            pltpu.SemaphoreType.DMA((2,)),
+            pltpu.SemaphoreType.DMA((3, 2)),
             pltpu.SemaphoreType.DMA((2,)),
         ],
         compiler_params=pltpu.CompilerParams(
@@ -415,7 +446,7 @@
             transcendentals=replicas * heads * length * length,
         ),
         name="attend_all",
-    )(qkv, table, sent)
+    )(inputs, gain, *weights, table, sent)
 
 
 def expert_tile(rows, scaled, gate_w, up_w, down_w):
@@ -483,7 +514,6 @@
     units = gate_w.shape[1]
     tiles = units // tile
     count = 2 * capacity
-    offs = [2, 4, 3, 5, 6, 7, 1]
 
     def weights_of(t):
         at = pl.multiple_of(t * tile, tile)
@@ -505,10 +535,10 @@
         return carry
 
     lax.fori_loop(0, tiles, start_weights, 0)
-    greet([{"dp": flipped(d, o)} for o in offs])
+    greet([{"dp": flipped(d, o)} for o in PEERS])
     pending = []
     arrivals = {}
-    for o in offs:
+    for o in PEERS:
         sends[o] = jnp.dot(
             both_ref[o * capacity : (o + 1) * capacity],
             normed_ref[...],
@@ -611,7 +641,7 @@
     for j in range(groups // 2 - 2, groups // 2):
         for copy in unit_copies[j]:
             copy.wait()
-    for o in offs:
+    for o in PEERS:
         arrivals[o].wait_send()
     for copy in pending + keeps:
         copy.wait()
@@ -666,72 +696,581 @@
     )(normed2, both, cot, router, gate_w, up_w, down_w)
 
 
-def far_kernel(
-    width,
-    rows_ref,
-    cot_ref,
+def attend_back_kernel(
+    far_ref,
+    both_ref,
+    signs_ref,
+    grad_ref,
+    qkv_hbm,
+    probs_hbm,
+    query_w,
+    key_w,
+    value_w,
+    far_out,
+    grad_qkv_out,
+    grad_normed_out,
+    sums_ref,
+    acc_ref,
+    sends,
+    grads,
+    qkv_ref,
+    probs_ref,
+    grad_qkv_ref,
+    parts,
+    landed,
+    far_send,
+    far_recv,
+    hop_send,
+    hop_recv,
+    part_send,
+    part_recv,
+    load_sem,
+    store_sem,
+    own_sem,
+):
+    z, d = lax.axis_index("head"), lax.axis_index("dp")
+    replicas, length, columns = grads.shape
+    groups, capacity, extent = sends.shape
+    heads, _, width = sums_ref.shape
+    pairs = heads // 2
+    lanes = columns // pairs
+    half = lanes // 2
+    chunk = 2 * TILE
+    hops = range(1, replicas)
+    order = [0, 3, 2, 1]
+
+    def loads(turn):
+        r, slot = order[turn], turn % 2
+        return [
+            pltpu.make_async_copy(qkv_hbm.at[r], qkv_ref.at[slot], load_sem.at[0, slot]),
+            pltpu.make_async_copy(probs_hbm.at[r], probs_ref.at[slot], load_sem.at[1, slot]),
+        ]
+
+    for copy in loads(0):
+        copy.start()
+    greet([{"dp": flipped(d, o)} for o in PEERS] + [{"head": flipped(z, r)} for r in hops])
+    copies = []
+    arrivals = {}
+    for r in order[1:]:
+        arrivals[r] = remote(
+            grad_ref.at[:, pl.ds(r * columns, columns)],
+            grads.at[r],
+            hop_send.at[r],
+            hop_recv.at[r],
+            {"head": flipped(z, r)},
+        )
+        arrivals[r].start()
+    model = extent - TILE
+    for o in PEERS + [0]:
+        span = slice(o * capacity, (o + 1) * capacity)
+        sends[o, :, :model] = jnp.dot(
+            both_ref[span], far_ref[...], preferred_element_type=F32
+        ).astype(BF)
+        sends[o, :, model:] = signs_ref[span]
+        if o:
+            copy = remote(
+                sends.at[o],
+                far_out.at[o],
+                far_send.at[o],
+                far_recv.at[o],
+                {"dp": flipped(d, o)},
+            )
+        else:
+            copy = pltpu.make_async_copy(sends.at[0], far_out.at[0], own_sem)
+        copy.start()
+        copies.append(copy)
+    sums_ref[...] = jnp.zeros_like(sums_ref)
+    grads[0] = grad_ref[:, :columns]
+
+    stores = []
+    for turn, r in enumerate(order):
+        slot = turn % 2
+        if turn + 1 < replicas:
+            for copy in loads(turn + 1):
+                copy.start()
+        for copy in loads(turn):
+            copy.wait()
+        if r:
+            arrivals[r].wait_recv()
+        if turn >= 2:
+            stores[turn - 2].wait()
+
+        def pair_step(pair, carry, slot=slot, r=r):
+            def part_of(j):
+                at = pl.multiple_of(j * columns + pair * lanes, lanes)
+                return qkv_ref[slot, :, pl.ds(at, lanes)]
+
+            at = pl.multiple_of(pair * lanes, lanes)
+            query, value = part_of(0), part_of(2)
+            key_t = part_of(1).T
+            grad_all = grads[r, :, pl.ds(at, lanes)]
+            grad_keys, grad_values = [], []
+            for part in range(2):
+                mask = lanes_of((length, lanes), half, part)
+                grad = jnp.where(mask, grad_all, 0).astype(BF)
+                grad_key = jnp.zeros((length, lanes), F32)
+                grad_value = jnp.zeros((length, lanes), F32)
+                for c in range(length // chunk):
+                    cols = slice(c * chunk, (c + 1) * chunk)
+                    grad_probs = contract(value, grad[cols], 1, 1)
+                    probs_low = probs_ref[slot, pair * 2 + part, :, cols]
+                    probs = probs_low.astype(F32)
+                    delta = jnp.sum(probs * grad_probs, axis=0, keepdims=True)
+                    grad_scores = (probs * (grad_probs - delta)).astype(BF)
+                    grad_value += jnp.dot(probs_low, grad_all[cols], preferred_element_type=F32)
+                    grad_key += jnp.dot(grad_scores, query[cols], preferred_element_type=F32)
+                    acc_ref[part * half : (part + 1) * half, cols] = jnp.dot(
+                        key_t[part * half : (part + 1) * half],
+                        grad_scores,
+                        preferred_element_type=F32,
+                    )
+                    for kb in range(length // TILE):
+                        to = length - TILE * kb + chunk * c
+                        sums_ref[pair * 2 + part, :, to : to + chunk] += grad_scores[
+                            kb * TILE : (kb + 1) * TILE
+                        ].astype(F32)
+                grad_keys.append(grad_key)
+                grad_values.append(grad_value)
+            first = lanes_of((length, lanes), half, 0)
+            results = (
+                acc_ref[...].T * SCALE,
+                jnp.where(first, *grad_keys) * SCALE,
+                jnp.where(first, *grad_values),
+            )
+            for j, result in enumerate(results):
+                to = pl.multiple_of(j * columns + pair * lanes, lanes)
+                grad_qkv_ref[slot, :, pl.ds(to, lanes)] = result.astype(BF)
+            return carry
+
+        lax.fori_loop(0, pairs, pair_step, 0)
+        stores.append(
+            pltpu.make_async_copy(grad_qkv_ref.at[slot], grad_qkv_out.at[r], store_sem.at[slot])
+        )
+        stores[-1].start()
+
+        def part_step(i, carry, slot=slot, r=r):
+            span = pl.ds(pl.multiple_of(i * TILE, TILE), TILE)
+            total = sum(
+                contract(
+                    grad_qkv_ref[slot, :, j * columns : (j + 1) * columns], weight[span, :], 1, 1
+                )
+                for j, weight in enumerate((query_w, key_w, value_w))
+            )
+            parts[r, :, span] = total.astype(BF)
+            return carry
+
+        lax.fori_loop(0, parts.shape[2] // TILE, part_step, 0)
+        if r:
+            copy = remote(
+                parts.at[r], landed.at[r], part_send.at[r], part_recv.at[r], {"head": flipped(z, r)}
+            )
+            copy.start()
+            copies.append(copy)
+
+    for r in order[1:]:
+        arrivals[r].wait_send()
+    stores[-2].wait()
+    stores[-1].wait()
+    for copy in copies:
+        copy.wait()
+    grad_normed_out[...] = parts[0].astype(F32) + sum(landed[r].astype(F32) for r in hops)
+
+
+def attend_back(far_own, both_far, signs_far, grad_heads, qkv, probs, weights, groups):
+    replicas, length, triple = qkv.shape
+    heads = probs.shape[1]
+    columns = triple // 3
+    width = weights[0].shape[0]
+    lanes = 2 * columns // heads
+    capacity = both_far.shape[0] // groups
+    extent = far_own.shape[1] + TILE
+    vmem = pl.BlockSpec(memory_space=pltpu.VMEM)
+    hbm = pl.BlockSpec(memory_space=pl.ANY)
+    hop_sem = pltpu.SemaphoreType.DMA((replicas,))
+    return pl.pallas_call(
+        attend_back_kernel,
+        out_shape=(
+            jax.ShapeDtypeStruct((groups, capacity, extent), BF),
+            jax.ShapeDtypeStruct((replicas, length, triple), BF),
+            jax.ShapeDtypeStruct((length, width), F32),
+            jax.ShapeDtypeStruct((heads, TILE, 2 * length), F32),
+        ),
+        in_specs=[vmem] * 4 + [hbm] * 2 + [vmem] * 3,
+        out_specs=[hbm, hbm, vmem, vmem],
+        scratch_shapes=[
+            pltpu.VMEM((lanes, length), F32),
+            pltpu.VMEM((groups, capacity, extent), BF),
+            pltpu.VMEM((replicas, length, columns), BF),
+            pltpu.VMEM((2, length, triple), BF),
+            pltpu.VMEM((2, heads, length, length), BF),
+            pltpu.VMEM((2, length, triple), BF),
+            pltpu.VMEM((replicas, length, width), BF),
+            pltpu.VMEM((replicas, length, width), BF),
+            pltpu.SemaphoreType.DMA((groups,)),
+            pltpu.SemaphoreType.DMA((groups,)),
+            hop_sem,
+            hop_sem,
+            hop_sem,
+            hop_sem,
+            pltpu.SemaphoreType.DMA((2, 2)),
+            pltpu.SemaphoreType.DMA((2,)),
+            pltpu.SemaphoreType.DMA,
+        ],
+        compiler_params=pltpu.CompilerParams(
+            vmem_limit_bytes=VMEM_LIMIT, collective_id=3, has_side_effects=True
+        ),
+        cost_estimate=pl.CostEstimate(
+            flops=replicas * heads * 16 * length * length * lanes,
+            bytes_accessed=replicas * heads * length * length * 4,
+            transcendentals=0,
+        ),
+        name="attend_back",
+    )(far_own, both_far, signs_far, grad_heads, qkv, probs, *weights)
+
+
+def last_kernel(
+    tile,
+    far_ref,
+    rows_here,
+    scaled_here,
     router_ref,
-    gate_w,
-    up_w,
-    down_w,
-    hidden_out,
-    grad_gate_out,
-    grad_up_out,
-    scaled_out,
+    gate_hbm,
+    up_hbm,
+    down_hbm,
+    grad_gate_hbm,
+    grad_up_hbm,
+    hidden_hbm,
+    qkv_w_hbm,
+    out_w_hbm,
+    small_ref,
+    gate_out,
+    up_out,
+    down_out,
+    qkv_w_out,
+    out_w_out,
+    small_out,
+    scaled,
+    left,
+    weights,
+    downs,
+    units,
+    hidden,
+    hidden_here,
+    send_wide,
+    came_wide,
+    send_tall,
+    came_tall,
+    qkv_land,
+    qkv_sum,
+    out_land,
+    out_sum,
+    out_hop,
+    out_last,
+    small_land,
+    small_sum,
+    small_hop,
+    stream_sem,
+    hidden_sem,
+    wide_send,
+    wide_recv,
+    tall_sem,
+    first_send,
+    first_recv,
+    hop_send,
+    hop_recv,
+    third_send,
+    third_recv,
+    own_sem,
 ):
-    slots = rows_ref.shape[0]
-    count = slots // 4
-
-    @pl.when(pl.program_id(0) == 0)
-    def _():
-        for i in range(4):
-            span = slice(i * count, (i + 1) * count)
-            scaled_out[span] = scaled_rows(
-                rows_ref[span], cot_ref[span], router_ref[...], width
-            )
-
-    def step(i, carry):
-        span = pl.ds(pl.multiple_of(i * count, count), count)
-        values = expert_tile(
-            rows_ref[span], scaled_out[span], gate_w[...], up_w[...], down_w[...]
+    z, d = lax.axis_index("head"), lax.axis_index("dp")
+    groups, capacity, _ = far_ref.shape
+    slots, width = scaled_here.shape
+    rows, total_units = gate_out.shape
+    half_units = hidden_here.shape[1]
+    tiles = total_units // tile
+    low, high = lax.rem(z, 2), z // 2
+    keep_at = pl.multiple_of(low * rows, rows)
+    send_at = pl.multiple_of((1 - low) * rows, rows)
+    near = {"head": flipped(z, 1)}
+    count = 2 * capacity
+    hops = [3, 2, 1]
+
+    def streams(t):
+        slot = lax.rem(t, 2)
+        at = pl.multiple_of(t * tile, tile)
+        cols = pl.ds(at, tile)
+        return [
+            pltpu.make_async_copy(gate_hbm.at[:, cols], weights.at[slot, 0], stream_sem.at[0, slot]),
+            pltpu.make_async_copy(up_hbm.at[:, cols], weights.at[slot, 1], stream_sem.at[1, slot]),
+            pltpu.make_async_copy(down_hbm.at[cols, :], downs.at[slot], stream_sem.at[2, slot]),
+            pltpu.make_async_copy(
+                grad_gate_hbm.at[:, cols], units.at[slot, 0], stream_sem.at[3, slot]
+            ),
+            pltpu.make_async_copy(
+                grad_up_hbm.at[:, cols], units.at[slot, 1], stream_sem.at[4, slot]
+            ),
+        ]
+
+    for copy in streams(0):
+        copy.start()
+    half_copy = pltpu.make_async_copy(
+        hidden_hbm.at[:, pl.ds(pl.multiple_of(high * half_units, TILE), half_units)],
+        hidden_here,
+        hidden_sem,
+    )
+    half_copy.start()
+    greet([{"dp": flipped(d, o)} for o in PEERS] + [{"head": flipped(z, r)} for r in hops])
+
+    first = []
+    for o in PEERS:
+        peer = flipped(d, o)
+        for i, (source, target) in enumerate(
+            (
+                (qkv_w_hbm.at[peer], qkv_land.at[o]),
+                (out_w_hbm.at[:, peer], out_land.at[o]),
+                (small_ref, small_land.at[o]),
+            )
+        ):
+            copy = remote(source, target, first_send.at[i, o], first_recv.at[i, o], {"dp": peer})
+            copy.start()
+            first.append(copy)
+    own = [
+        pltpu.make_async_copy(qkv_w_hbm.at[d], qkv_land.at[0], own_sem.at[0]),
+        pltpu.make_async_copy(out_w_hbm.at[:, d], out_land.at[0], own_sem.at[1]),
+    ]
+    for copy in own:
+        copy.start()
+
+    for j in range(groups // 2):
+        span = slice(j * count, (j + 1) * count)
+        here = far_ref[2 * j : 2 * j + 2, :, :width].reshape(count, width)
+        extended = far_ref[2 * j : 2 * j + 2, :, width:].reshape(count, width + TILE)
+        scaled[span] = scaled_rows(here, extended, router_ref[...], width)
+
+    wide = 2 * rows
+    columns = pl.ds(pl.multiple_of(high * wide, wide), wide)
+
+    def left_step(i, carry):
+        at = pl.multiple_of(i * capacity, capacity)
+        left[0, pl.ds(at, capacity), :] = rows_here[pl.ds(at, capacity), columns]
+        left[1, pl.ds(at, capacity), :] = far_ref[i, :, columns]
+        return carry
+
+    lax.fori_loop(0, groups, left_step, 0)
+
+    def wide_copy(i, t):
+        at = pl.multiple_of(t * tile, tile)
+        return remote(
+            send_wide.at[i, :, pl.ds(at, tile)],
+            came_wide.at[i, :, pl.ds(at, tile)],
+            wide_send.at[i, t],
+            wide_recv.at[i, t],
+            near,
         )
-        for ref, value in zip((hidden_out, grad_gate_out, grad_up_out), values):
-            ref[span] = value
+
+    def tile_step(t, carry):
+        slot = lax.rem(t, 2)
+        at = pl.multiple_of(t * tile, tile)
+
+        @pl.when(t + 1 < tiles)
+        def _():
+            for copy in streams(t + 1):
+                copy.start()
+
+        for copy in streams(t):
+            copy.wait()
+
+        def chunk_step(j, inner):
+            span = pl.ds(pl.multiple_of(j * count, count), count)
+            here = far_ref[pl.ds(2 * j, 2), :, :width].reshape(count, width)
+            values = expert_tile(
+                here, scaled[span], weights[slot, 0], weights[slot, 1], downs[slot]
+            )
+            hidden[span, pl.ds(at, tile)] = values[0]
+            units[slot, 2, span, :] = values[1]
+            units[slot, 3, span, :] = values[2]
+            return inner
+
+        lax.fori_loop(0, groups // 2, chunk_step, 0)
+        for i, out in enumerate((gate_out, up_out)):
+            value = contract(left[0], units[slot, i], 0, 0) + contract(
+                left[1], units[slot, 2 + i], 0, 0
+            )
+            upper = low == 1
+            send_wide[i, :, pl.ds(at, tile)] = jnp.where(
+                upper, value[:rows], value[rows:]
+            ).astype(BF)
+            out[:, pl.ds(at, tile)] = jnp.where(upper, value[rows:], value[:rows])
+            wide_copy(i, t).start()
         return carry
 
-    lax.fori_loop(0, 4, step, 0)
-
-
-def far_stage(rows, cot, router, gate_w, up_w, down_w, tile):
+    middle = tiles // 2
+    lax.fori_loop(0, middle, tile_step, 0)
+
+    for copy in first:
+        copy.wait()
+    for copy in own:
+        copy.wait()
+    small_land[0] = small_ref[...]
+    qkv_sum[...] = sum(qkv_land[o].astype(F32) for o in range(groups)).astype(BF)
+    out_sum[...] = sum(out_land[o].astype(F32) for o in range(groups)).astype(BF)
+    small_sum[...] = sum(small_land[o] for o in range(groups))
+    second = []
+    for o in PEERS:
+        copy = remote(
+            qkv_sum, qkv_w_out.at[d], third_send.at[0, o], third_recv.at[0, o], {"dp": flipped(d, o)}
+        )
+        copy.start()
+        second.append(copy)
+    mine = [pltpu.make_async_copy(qkv_sum, qkv_w_out.at[d], own_sem.at[0])]
+    mine[0].start()
+    over = []
+    for r in hops:
+        for i, (source, target) in enumerate(
+            ((out_sum.at[r], out_hop.at[r]), (small_sum, small_hop.at[r]))
+        ):
+            copy = remote(
+                source, target, hop_send.at[i, r], hop_recv.at[i, r], {"head": flipped(z, r)}
+            )
+            copy.start()
+            over.append(copy)
+
+    lax.fori_loop(middle, tiles, tile_step, 0)
+
+    for copy in over:
+        copy.wait()
+    out_last[...] = (
+        out_sum[0].astype(F32) + sum(out_hop[r].astype(F32) for r in hops)
+    ).astype(BF)
+    small_out[0] = small_sum[...]
+    small_out[1] = small_sum[...] + sum(small_hop[r] for r in hops)
+    for o in PEERS:
+        copy = remote(
+            out_last,
+            out_w_out.at[d],
+            third_send.at[1, o],
+            third_recv.at[1, o],
+            {"dp": flipped(d, o)},
+        )
+        copy.start()
+        second.append(copy)
+    mine.append(pltpu.make_async_copy(out_last, out_w_out.at[d], own_sem.at[1]))
+    mine[1].start()
+
+    half_copy.wait()
+    share = half_units // 2
+    halves = pl.ds(pl.multiple_of(high * half_units, TILE), half_units)
+
+    def tall_step(i, carry):
+        cols = pl.ds(pl.multiple_of(i * tile, tile), tile)
+        value = contract(hidden_here[...], scaled_here[:, cols], 0, 0) + contract(
+            hidden[:, halves], scaled[:, cols], 0, 0
+        )
+        upper = low == 1
+        send_tall[:, cols] = jnp.where(upper, value[:share], value[share:]).astype(BF)
+        down_out[:, cols] = jnp.where(upper, value[share:], value[:share])
+        return carry
+
+    lax.fori_loop(0, width // tile, tall_step, 0)
+    tall = remote(send_tall, came_tall, tall_sem.at[0], tall_sem.at[1], near)
+    tall.start()
+
+    def wide_end(t, carry):
+        at = pl.multiple_of(t * tile, tile)
+        for i, out in enumerate((gate_out, up_out)):
+            wide_copy(i, t).wait()
+            out[:, pl.ds(at, tile)] += came_wide[i, :, pl.ds(at, tile)].astype(F32)
+        return carry
+
+    lax.fori_loop(0, tiles, wide_end, 0)
+    for copy in second + mine:
+        copy.wait()
+    tall.wait()
+    down_out[...] += came_tall[...].astype(F32)
+
+
+def last_stage(
+    far, rows_here, scaled_here, router, weights, grads_here, hidden_here, qkv_w, out_w, small, tile
+):
+    gate_w, up_w, down_w = weights
     width, units = gate_w.shape
-    slots = rows.shape[0]
-
-    def whole(shape):
-        return pl.BlockSpec(shape, lambda t: (0, 0))
-
-    unit_shape = jax.ShapeDtypeStruct((slots, units), BF)
-    unit_spec = pl.BlockSpec((slots, tile), lambda t: (0, t))
+    groups, capacity, extent = far.shape
+    replicas, _, part_rows, _ = out_w.shape
+    slots = groups * capacity
+    vmem = pl.BlockSpec(memory_space=pltpu.VMEM)
+    hbm = pl.BlockSpec(memory_space=pl.ANY)
+    rows, share = width // replicas, units // replicas
+    plane_sem = pltpu.SemaphoreType.DMA((3, groups))
+    hop_sem = pltpu.SemaphoreType.DMA((2, replicas))
     return pl.pallas_call(
-        functools.partial(far_kernel, width),
-        out_shape=(unit_shape,) * 3 + (jax.ShapeDtypeStruct((slots, width), BF),),
-        grid=(units // tile,),
-        in_specs=[
-            whole(rows.shape),
-            whole(cot.shape),
-            whole(router.shape),
-            pl.BlockSpec((width, tile), lambda t: (0, t)),
-            pl.BlockSpec((width, tile), lambda t: (0, t)),
-            pl.BlockSpec((tile, width), lambda t: (t, 0)),
+        functools.partial(last_kernel, tile),
+        out_shape=(
+            jax.ShapeDtypeStruct((rows, units), F32),
+            jax.ShapeDtypeStruct((rows, units), F32),
+            jax.ShapeDtypeStruct((share, width), F32),
+            jax.ShapeDtypeStruct(qkv_w.shape, BF),
+            jax.ShapeDtypeStruct(out_w.shape[1:], BF),
+            jax.ShapeDtypeStruct((2,) + small.shape, F32),
+        ),
+        in_specs=[vmem] * 4 + [hbm] * 8 + [vmem],
+        out_specs=[vmem, vmem, vmem, hbm, hbm, vmem],
+        scratch_shapes=[
+            pltpu.VMEM((slots, width), BF),
+            pltpu.VMEM((2, slots, 2 * rows), BF),
+            pltpu.VMEM((2, 2, width, tile), BF),
+            pltpu.VMEM((2, tile, width), BF),
+            pltpu.VMEM((2, 4, slots, tile), BF),
+            pltpu.VMEM((slots, units), BF),
+            pltpu.VMEM((slots, units // 2), BF),
+            pltpu.VMEM((2, rows, units), BF),
+            pltpu.VMEM((2, rows, units), BF),
+            pltpu.VMEM((share, width), BF),
+            pltpu.VMEM((share, width), BF),
+            pltpu.VMEM(qkv_w.shape, BF),
+            pltpu.VMEM(qkv_w.shape[1:], BF),
+            pltpu.VMEM((groups, replicas, part_rows, width), BF),
+            pltpu.VMEM((replicas, part_rows, width), BF),
+            pltpu.VMEM((replicas, part_rows, width), BF),
+            pltpu.VMEM((part_rows, width), BF),
+            pltpu.VMEM((groups,) + small.shape, F32),
+            pltpu.VMEM(small.shape, F32),
+            pltpu.VMEM((replicas,) + small.shape, F32),
+            pltpu.SemaphoreType.DMA((5, 2)),
+            pltpu.SemaphoreType.DMA,
+            pltpu.SemaphoreType.DMA((2, units // tile)),
+            pltpu.SemaphoreType.DMA((2, units // tile)),
+            pltpu.SemaphoreType.DMA((2,)),
+            plane_sem,
+            plane_sem,
+            hop_sem,
+            hop_sem,
+            plane_sem,
+            plane_sem,
+            pltpu.SemaphoreType.DMA((2,)),
         ],
-        out_specs=[unit_spec] * 3 + [whole((slots, width))],
-        compiler_params=pltpu.CompilerParams(vmem_limit_bytes=VMEM_LIMIT),
+        compiler_params=pltpu.CompilerParams(
+            vmem_limit_bytes=VMEM_MOST, collective_id=4, has_side_effects=True
+        ),
         cost_estimate=pl.CostEstimate(
-            flops=6 * slots * width * units,
+            flops=12 * slots * width * units,
             bytes_accessed=6 * width * units + 6 * slots * units,
             transcendentals=slots * units,
         ),
-        name="far_stage",
-    )(rows, cot, router, gate_w, up_w, down_w)
+        name="last_stage",
+    )(
+        far,
+        rows_here,
+        scaled_here,
+        router,
+        gate_w,
+        up_w,
+        down_w,
+        *grads_here,
+        hidden_here,
+        qkv_w,
+        out_w,
+        small,
+    )
 
 
 def expert_forward(rows, gate_w, up_w, grad_unscaled, slot_gates):
@@ -1059,7 +1598,7 @@
         ((dest // capacity) ^ dp_at) * capacity + dest % capacity,
         slot_count,
     )
-    routing_far = hop(jnp.concatenate([dest, expert_ids], axis=1), far)
+    routing_far = hop(jnp.concatenate([mixed_dest, expert_ids], axis=1), far)
     slot_row = jnp.arange(slot_count, dtype=jnp.int32)[None, :]
     slot_col = jnp.arange(slot_count, dtype=jnp.int32)[:, None]
     expert_range = jnp.arange(experts, dtype=jnp.int32)
@@ -1072,6 +1611,7 @@
         return first + second, contract(first - second, signs, 1, 0).astype(BF)
 
     both, signs = dispatch_of(mixed_dest, expert_ids)
+    both_far, signs_far = dispatch_of(routing_far[:, :2], routing_far[:, 2:])
     picks = [(mixed_dest[:, k : k + 1] == slot_row).astype(BF) for k in range(2)]
     router_wide = jnp.pad(w_router, ((0, 0), (0, TILE - experts)))
     cot_sent = jnp.concatenate([contract(both, cotangent, 1, 0).astype(BF), signs], axis=1)
@@ -1081,20 +1621,19 @@
     out_rows = head_cols // groups
     piece = lax.dynamic_slice_in_dim(w_out, dp_at * out_rows, out_rows, 0)
     w_out_all = lax.all_gather(piece, ("head", "dp"), axis=0, tiled=True)
-    w_qkv = jnp.concatenate([w_query, w_key, w_value], axis=1)
     order = [me ^ r for r in range(replicas)]
     w_out_all = w_out_all.reshape(replicas, head_cols, width)
     w_out_cat = jnp.concatenate(
         [lax.dynamic_index_in_dim(w_out_all, o, 0, keepdims=False) for o in order], axis=0
     )
 
-    inputs_all = block_input.astype(F32)
-    normed = rms_norm(inputs_all, norm1_gain).astype(BF)
-    qkv = jnp.dot(normed, w_qkv, preferred_element_type=F32).astype(BF)
     line = (rel_bucket[::-1][None, :] == jnp.arange(buckets, dtype=jnp.int32)[:, None]).astype(F32)
     line = jnp.pad(line, ((0, 0), (1, 0)))
     table = skew(contract(pos_bias, line, 0, 0, HIGH))
-    attended, probs, cot_here = attend_all(qkv, table, cot_sent, length, replicas)
+    input_weights = (w_query, w_key, w_value)
+    attended, probs, cot_here, normed, qkv = attend_all(
+        block_input, norm1_gain[None, :], input_weights, table, cot_sent, length, replicas
+    )
 
     branch = jnp.dot(attended, w_out_cat, preferred_element_type=F32)
     inputs_own = lax.dynamic_slice_in_dim(block_input, me * own_rows, own_rows, 0).astype(F32)
@@ -1112,41 +1651,6 @@
     scaled_here = scaled_here.reshape(slot_count, width)
     came_back = came_back.reshape(slot_count, width)
     grad_back = grad_back.reshape(slot_count, width)
-
-    both_far, signs_far = dispatch_of(routing_far[:, :2], routing_far[:, 2:])
-    far_own = jnp.concatenate([normed2_far, cot_far_own], axis=1)
-    far_sent = jnp.concatenate([contract(both_far, far_own, 1, 0).astype(BF), signs_far], axis=1)
-    far_sent, grad_back = lax.optimization_barrier((far_sent, grad_back))
-    far_came = lax.all_to_all(
-        far_sent.reshape(experts, capacity, 2 * width + TILE),
-        "dp",
-        split_axis=0,
-        concat_axis=0,
-        tiled=True,
-    ).reshape(slot_count, 2 * width + TILE)
-    rows_far = far_came[:, :width]
-    hidden_far, ggp_far, gup_far, scaled_far = far_stage(
-        rows_far, far_came[:, width:], router_wide, gate_w, up_w, down_w, tile
-    )
-
-    low, high = me % far, me // far
-
-    def part(lefts, rights, at):
-        rows = lefts[0].shape[1] // replicas
-        return sum(
-            contract(lax.dynamic_slice_in_dim(left, at * rows, rows, 1), right, 0, 0)
-            for left, right in zip(lefts, rights)
-        )
-
-    def sent(lefts, rights):
-        return hop(part(lefts, rights, high * far + (1 - low)).astype(BF), 1)
-
-    weight_args = (
-        ((rows_here, rows_far), (ggp_here, ggp_far)),
-        ((rows_here, rows_far), (gup_here, gup_far)),
-        ((hidden_here, hidden_far), (scaled_here, scaled_far)),
-    )
-    came = [sent(*a) for a in weight_args]
 
     logits = jnp.dot(normed2, w_router, preferred_element_type=F32)
     chosen = (expert_ids[:, :, None] == expert_range[None, None, :]).astype(F32)
@@ -1163,63 +1667,59 @@
     grad_mixed, grad_norm2 = norm2_pull(grad_normed2)
     grad_mixed = grad_mixed + grad_output
     grad_branch = grad_mixed.astype(BF)
-
     grad_wout = contract(attended, grad_branch, 0, 0).astype(BF)
-    grad_wout = grad_wout.reshape(replicas, groups, out_rows, width)
-    grad_wout = lax.psum_scatter(grad_wout, "dp", scatter_dimension=1, tiled=True)[:, 0]
-    grad_wout = sum(
-        (hop(grad_wout[r], r) if r else grad_wout[r]).astype(F32) for r in range(replicas)
+    grad_heads = contract(grad_branch, w_out_cat, 1, 1).astype(BF)
+
+    far_own = jnp.concatenate([normed2_far, cot_far_own], axis=1)
+    far_came, grad_qkv, grad_normed, sums = attend_back(
+        far_own, both_far, signs_far, grad_heads, qkv, probs, input_weights, groups
+    )
+    grad_qkv_w = lax.dot_general(
+        normed, grad_qkv, (((0, 1), (0, 1)), ((), ())), preferred_element_type=F32
     ).astype(BF)
-    grad_out_proj = lax.all_gather(grad_wout, "dp", axis=0, tiled=True).astype(F32)
-
-    qkv_rows = width // groups
-    piece = lax.dynamic_slice_in_dim(w_qkv, dp_at * qkv_rows, qkv_rows, 0)
-    piece, _ = lax.optimization_barrier((piece, w_out_cat))
-    w_qkv_all = lax.all_gather(piece, ("head", "dp"), axis=0, tiled=True)
-    w_qkv_all = w_qkv_all.reshape(replicas, width, 3 * head_cols)
-    grad_heads = contract(grad_branch, w_out_cat, 1, 1).astype(BF)
-    sums = jnp.zeros((heads_here, TILE, 2 * length), F32)
-    grad_blocks = [grad_heads[:, i * head_cols : (i + 1) * head_cols] for i in range(replicas)]
-    grad_normed = None
-    weight_terms = []
-    arrived = [hop(grad_blocks[r], r) if r else grad_blocks[0] for r in range(replicas)]
-    for r in (0, 2, 3, 1):
-        grad_qkv, sums = attend_bwd(order[r].reshape(1), qkv, arrived[r], probs[r], sums, length)
-        normed_seq = lax.dynamic_slice_in_dim(normed, order[r] * length, length, 0)
-        weight_terms.append(contract(normed_seq, grad_qkv, 0, 0))
-        mine = hop(grad_qkv, r) if r else grad_qkv
-        weight = lax.dynamic_index_in_dim(w_qkv_all, order[r], 0, keepdims=False)
-        term = contract(mine, weight, 1, 1)
-        grad_normed = term if grad_normed is None else grad_normed + term
-    grad_qkv_w = sum(weight_terms)
-
     _, norm1_pull = jax.vjp(rms_norm, inputs_own, norm1_gain)
     grad_first, grad_norm1 = norm1_pull(grad_normed)
     grad_input = grad_mixed + grad_first
-    grad_bias = contract(unskew(sums), line, 1, 1, HIGH)
-    grad_qkv_w, grad_bias = lax.psum((grad_qkv_w.astype(BF), grad_bias), "dp")
-    grad_qkv_w = grad_qkv_w.astype(F32)
-    grad_norm1, grad_norm2, grad_router = lax.psum(
-        (grad_norm1, grad_norm2, grad_router), ("dp", "head")
-    )
-    came, _ = lax.optimization_barrier((came, grad_normed))
-    grad_gate_w, grad_up_w, grad_down_w = (
-        (part(*a, me) + piece.astype(F32))[None] for a, piece in zip(weight_args, came)
-    )
+    grad_bias = contract(line, unskew(sums), 1, 1, HIGH)
+
+    flat = jnp.concatenate(
+        [grad_norm1, grad_norm2, grad_router.reshape(-1), grad_bias.reshape(-1)]
+    )
+    small_rows = -(-flat.shape[0] // (8 * TILE)) * 8
+    small = jnp.pad(flat, (0, small_rows * TILE - flat.shape[0])).reshape(small_rows, TILE)
+
+    grad_gate_w, grad_up_w, grad_down_w, grad_qkv_w, grad_out_proj, summed = last_stage(
+        far_came,
+        rows_here,
+        scaled_here,
+        router_wide,
+        (gate_w, up_w, down_w),
+        (ggp_here, gup_here),
+        hidden_here,
+        grad_qkv_w.reshape(groups, width // groups, 3 * head_cols),
+        grad_wout.reshape(replicas, groups, out_rows, width),
+        small,
+        tile,
+    )
+    grad_qkv_w = grad_qkv_w.reshape(width, 3 * head_cols).astype(F32)
+    grad_out_proj = grad_out_proj.reshape(head_cols, width).astype(F32)
+    summed = summed.reshape(2, -1)
+    ends = [width, 2 * width, 2 * width + width * experts]
+    grad_bias = summed[0, ends[2] : ends[2] + buckets * heads_here].reshape(buckets, heads_here)
     return (
         output,
         grad_input,
-        grad_norm1,
+        summed[1, : ends[0]],
         grad_qkv_w[:, :head_cols],
         grad_qkv_w[:, head_cols : 2 * head_cols],
         grad_qkv_w[:, 2 * head_cols :],
         grad_out_proj,
-        jnp.transpose(grad_bias),
-        grad_norm2,
-        grad_router,
-        grad_gate_w,
-        grad_up_w,
-        grad_down_w,
+        grad_bias,
+        summed[1, ends[0] : ends[1]],
+        summed[1, ends[1] : ends[2]].reshape(width, experts),
+        grad_gate_w[None],
+        grad_up_w[None],
+        grad_down_w[None],
     )
 
 

time: 682 us -> 555 us (0.81)
  Pallas kernels: 230 us -> 426 us
  blocking collectives: 103 us -> 0 us
  waiting for transfers between devices: 104 us -> 13.5 us
  matrix products: 114 us -> 35.7 us
  starting transfers between devices: 30.4 us -> 4.99 us
  local copies, waits for them, and re-layouts: 40.4 us -> 26.1 us
  other arithmetic: 35.9 us -> 24.5 us
    pallas_call x6 -> x3, Pallas kernels: 113 us -> 311 us  [the longest x1 133 us: last_stage(): pl.pallas_call(functools.partial(last_kernel, tile), out_shape=(jax.Shape...]
    psum x2 -> x0, blocking collectives: 93.6 us -> none  [the longest x1 53.3 us: body_steps(): grad_qkv_w, grad_bias = lax.psum((grad_qkv_w.astype(BF), grad_bias), 'dp')]
    dot_general x30 -> x9, matrix products: 95.8 us -> 13.9 us  [contract(): lax.dot_general(left, right, (((left_dim,), (right_dim,)), ((), ())), pre...]
    ppermute x15 -> x3, waiting for transfers between devices: 70.5 us -> 0.01 us  [hop(): return lax.ppermute(value, 'head', [(i, i ^ r) for i in range(replicas)])]
    psum x1 -> x0, waiting for transfers between devices: 21.7 us -> none  [body_steps(): grad_qkv_w, grad_bias = lax.psum((grad_qkv_w.astype(BF), grad_bias), 'dp')]
    ppermute x15 -> x3, starting transfers between devices: 25.1 us -> 4.95 us  [hop(): return lax.ppermute(value, 'head', [(i, i ^ r) for i in range(replicas)])]
    all_gather x1, waiting for transfers between devices: 0.02 us -> 13.5 us  [body_steps(): w_out_all = lax.all_gather(piece, ('head', 'dp'), axis=0, tiled=True)]
    broadcast_in_dim x3 -> x0, other arithmetic: 11.8 us -> none  [body_steps(): (part(*a, me) + piece.astype(F32))[None]]
  transfers between devices with their start and end apart: 19 -> 4, of which waited for: 5 -> 1; matrix products, arithmetic and copies ran while one was open for 22% -> 9% of each run, Pallas kernels for 33% -> 31%
where the time goes in v3:
time: 555 us; the launch traced here: 546 us
  Pallas kernels  426 us (77%)
  matrix products  35.7 us (6%)
  local copies, waits for them, and re-layouts  26.1 us (5%)
  other arithmetic  24.5 us (4%)
  between operations  15.2 us (3%)
  waiting for transfers between devices  13.5 us (2%)
    pallas_call x1, Pallas kernels, last_stage(): pl.pallas_call(functools.partial(last_kernel, tile), out_shape=(jax.Shape...  133 us
    pallas_call x1, Pallas kernels, attend_back(): pl.pallas_call(attend_back_kernel, out_shape=(jax.ShapeDtypeStruct((group...  121 us
    pallas_call x1, Pallas kernels, expert_stage(): pl.pallas_call(functools.partial(expert_kernel, width, tile), out_shape=(...  109 us
    pallas_call x1, Pallas kernels, attend_all(): pl.pallas_call(attend_all_kernel, out_shape=(jax.ShapeDtypeStruct((length...  56.4 us
    unnamed x91, local copies, waits for them, and re-layouts  15.6 us
    dot_general x9, matrix products, contract(): lax.dot_general(left, right, (((left_dim,), (right_dim,)), ((), ())), pre...  13.9 us
    all_gather x1, waiting for transfers between devices, body_steps(): w_out_all = lax.all_gather(piece, ('head', 'dp'), axis=0, tiled=True)  13.5 us
  transfers between devices with their start and end apart: 4, of which 1 were waited for; matrix products, arithmetic and copies ran while one was open for 9% of the time, Pallas kernels for 31%

profile of v3, /device:TPU:0, one launch (start us, length us, event | category | flops | bytes accessed | tf_op | source)
XLA Modules:
  0.0 546.3 jit_solution(3115442449556863093)
XLA Ops:
  7.3 1.0 copy-done
  8.2 0.6 constant_dynamic-slice_fusion
  8.9 4.1 collective-permute-start.1
  13.0 0.8 fusion.72
  13.8 0.7 broadcast_add_fusion
  14.4 0.7 pad_add_fusion.1
  15.1 1.0 convert_reduce_fusion
  16.2 0.7 pad_add_fusion
  17.0 0.9 convolution_convert_fusion.2
  17.9 1.6 convolution_convert_fusion
  19.5 0.2 pad_maximum_fusion
  19.7 3.4 copy.46
  23.3 0.2 convolution_bitcast_fusion
  23.6 3.7 skew.1.table_ref
  27.3 1.5 fusion.11
  28.8 1.0 copy-done.6
  29.9 56.4 %attend_all.1 = (bf16[512,1024]{1,0:T(8,128)(2,1)S(1)}, bf16[4,4,512,512]{3,2,1,0:T(8,128)(2,1)}, bf16[8,160,1152]{2,1,0:T(8,128)(2,1)}, bf16[4,512,1024]{2,1,0:T(8,128)(2,1)}, bf16[4,512,768]{2,1,0:T(8,128)(2,1)}) custom-call(bf16[2048,1024]{1,0:T(8,128)(2,1)} %input_ref.1, f32[1,1024]{1,0:T(1,128)S(1)} %bitcast.75, bf16[1024,256]{1,0:T(8,128)(2,1)S(1)} %copy-done.4, ...), custom_call_target="tpu_custom_call" | custom-call | flops 4294967296 | bytes 16777216 | tf_op jit(solution)/shard_map/attend_all/pallas_call | solution.py:416
  86.3 1.0 copy-done.8
  87.2 1.9 fusion.18.both_ref
  89.1 0.2 copy.47
  89.3 0.8 pad.17.router_ref
  90.1 0.8 convolution_convert_fusion.1.signs_ref
  90.9 0.8 fusion.16.both_ref
  91.8 13.5 %all-gather.2.cloned.1.call-done = bf16[1024,1024]{1,0:T(8,128)(2,1)} async-done(((bf16[32,1024]{1,0:T(8,128)(2,1)}), bf16[1024,1024]{1,0:T(8,128)(2,1)}) %all-gather.2.cloned.1.call-update) | async-done | bytes 2097168 | tf_op jit(solution)/shard_map/all_gather | solution.py:1623
  105.2 1.8 dynamic-slice_bitcast_fusion.3
  107.1 3.3 multiply_reduce_fusion.2
  110.5 1.4 multiply_convert_fusion.normed_ref
  111.9 1.6 fusion.73
  113.5 0.8 collective-permute-start
  114.3 108.8 %expert_stage.1 = (bf16[8,160,1024]{2,1,0:T(8,128)(2,1)}, bf16[1280,2816]{1,0:T(8,128)(2,1)}, bf16[1280,2816]{1,0:T(8,128)(2,1)}, bf16[1280,2816]{1,0:T(8,128)(2...) custom-call(bf16[512,1024]{1,0:T(8,128)(2,1)} %multiply_convert_fusion.normed_ref, ...), custom_call_target="tpu_custom_call" | custom-call | flops 44291850240 | bytes 38928384 | tf_op jit(solution)/shard_map/expert_stage/pallas_call | solution.py:660
  223.2 3.4 fusion.1
  226.7 3.1 fusion.8
  229.9 3.5 fusion.22
  233.4 1.7 multiply_reduce_fusion
  235.2 0.5 copy-done.19
  235.6 0.3 copy-done.22
  235.9 2.8 convert_add_fusion.1
  238.7 2.4 fusion.74
  241.2 0.3 reshape.193
  241.5 4.7 convolution_convert_fusion.3
  246.2 1.3 convolution_convert_fusion.4.grad_ref
  247.5 3.1 pad_maximum_fusion.2.far_ref
  250.6 121.1 %attend_back.1 = (bf16[8,160,2176]{2,1,0:T(8,128)(2,1)}, bf16[4,512,768]{2,1,0:T(8,128)(2,1)}, f32[512,1024]{1,0:T(8,128)}, f32[4,128,1024]{2,1,0:T(8,128)}) custom-call(bf16[512,2048]{1,0:T(8,128)(2,1)} %pad_maximum_fusion.2.far_ref, bf16[1280,512]{1,0:T(8,128)(2,1)S(1)} %fusion.16.both_ref, bf16[1280,128]{1,0:T(8,128)(2,1)S(1)} %convolution_convert_fusion.1.signs_ref, ...), custom_call_target="tpu_custom_call" | custom-call | flops 8589934592 | bytes 16777216 | tf_op jit(solution)/shard_map/attend_back/pallas_call | solution.py:890
  371.7 1.6 copy-done.2
  373.3 2.9 unskew.1
  376.2 0.2 fusion.51
  376.6 2.1 fusion.14
  378.8 6.9 %bitcast_convert_fusion = bf16[1024,768]{1,0:T(8,128)(2,1)} fusion(bf16[4,512,1024]{2,1,0:T(8,128)(2,1)} %get-tuple-element.48, bf16[4,512,768]{2,1,0:T(8,128)(2,1)S(1)} %copy-done.40), kind=kOutput, calls=%fused_computation.7 | convolution fusion | flops 3222011904 | bytes 8912896 | tf_op jit(solution)/shard_map/dot_general | solution.py:1677
  385.7 0.6 fusion.53.small_ref
  386.3 133.5 %last_stage.1 = (f32[256,2816]{1,0:T(8,128)}, f32[256,2816]{1,0:T(8,128)}, f32[704,1024]{1,0:T(8,128)}, bf16[8,128,768]{2,1,0:T(8,128)(2,1)}, bf16[8,32,1024]{2,1,0:T(8,128)(2,1)}, /*index=5*/f32[2,88,128]{2,1,0:T(8,128)}) custom-call(bf16[8,160,2176]{2,1,0:T(8,128)(2,1)} %get-tuple-element.42.far_ref, bf16[1280,1024]{1,0:T(8,128)(2,1)} %bitcast.126, ...), custom_call_target="tpu_custom_call" | custom-call | flops 44291850240 | bytes 38928384 | tf_op jit(solution)/shard_map/last_stage/pallas_call | solution.py:1205
  519.8 0.9 copy.63
  520.9 0.6 fusion.67
  521.5 1.6 bitcast_convert_fusion.1
  523.1 1.7 fusion.66
  524.9 1.1 bitcast_convert_fusion.2
  526.0 0.3 reshape_squeeze.7
  526.3 0.8 copy.52
  527.2 0.7 copy.51
  527.8 3.9 fusion.10
  531.7 1.6 copy.70
  533.3 1.3 copy-done.15
  534.6 1.6 copy.71
  536.1 1.3 copy-done.14
  537.4 1.6 copy.72
  (104 shorter events, 1.1 us)
Async XLA Ops:
  7.2 1.1 copy-start
  7.2 10.7 %copy-start.20 = (bf16[512,1024]{1,0:T(8,128)(2,1)S(1)}, bf16[512,1024]{1,0:T(8,128)(2,1)}, u32[]{:S(2)}) copy-start(bf16[512,1024]{1,0:T(8,128)(2,1)} %param.17) | copy-start | bytes 3145732
  7.2 98.0 %all-gather.2.cloned.1.call-start = ((), (), s32[]{:S(2)}) async-start(), calls=%async_computation | async-start | bytes 2162688 | tf_op jit(solution)/shard_map/all_gather | solution.py:1623
  8.9 238.6 %collective-permute-start.1 = (bf16[512,1024]{1,0:T(8,128)(2,1)}, bf16[512,1024]{1,0:T(8,128)(2,1)}, u32[]{:S(2)}, u32[]{:S(2)}) collective-permute-start(bf16[512,1024]{1,0:T(8,128)(2,1)} %param.17), channel_id=1, source_target_pairs={{0,2},{1,3},{2,0},{3,1},{4,6},{5,7},{6,4},{7,5},{8,10},{9,11},{10,... | collective-permute-start | bytes 3145736 | tf_op jit(solution)/shard_map/ppermute | solution.py:1593
  16.9 73.2 %collective-permute-start.2 = (s32[512,4]{0,1:T(4,128)S(1)}, s32[512,4]{0,1:T(4,128)S(1)}, u32[]{:S(2)}, u32[]{:S(2)}) collective-permute-start(s32[512,4]{0,1:T(4,128)S(1)} %pad_add_fusion), channel_id=1, source_target_pairs={{0,2},{1,3},{2,0},{3,1},{4,6},{5,7},{6,4},{7,5},{8,10},{9,11},{10,... | collective-permute-start | bytes 24584 | tf_op jit(solution)/shard_map/ppermute | solution.py:1593
  17.0 69.3 %copy-start.35 = (s32[512,1]{0,1:T(1,128)}, s32[512,1]{0,1:T(1,128)S(1)}, u32[]{:S(2)}) copy-start(s32[512,1]{0,1:T(1,128)S(1)} %get-tuple-element.122) | copy-start | bytes 6148
  19.7 3.4 copy-start.37
  19.7 3.6 copy-start.38
  23.1 5.7 %copy-start.3 = (f32[1024]{0:T(1024)S(1)}, f32[1024]{0:T(1024)}, u32[]{:S(2)}) copy-start(f32[1024]{0:T(1024)} %param.21) | copy-start | bytes 12292
  23.1 5.7 %copy-start.4 = (bf16[1024,256]{1,0:T(8,128)(2,1)S(1)}, bf16[1024,256]{1,0:T(8,128)(2,1)}, u32[]{:S(2)}) copy-start(bf16[1024,256]{1,0:T(8,128)(2,1)} %query_w.1) | copy-start | bytes 1572868
  23.1 5.7 %copy-start.5 = (bf16[1024,256]{1,0:T(8,128)(2,1)S(1)}, bf16[1024,256]{1,0:T(8,128)(2,1)}, u32[]{:S(2)}) copy-start(bf16[1024,256]{1,0:T(8,128)(2,1)} %key_w.1) | copy-start | bytes 1572868
  28.8 1.0 copy-start.6
  29.9 59.3 %copy-start.32 = (bf16[1024,8]{0,1:T(8,128)(2,1)S(1)}, bf16[1024,8]{0,1:T(8,128)(2,1)}, u32[]{:S(2)}) copy-start(bf16[1024,8]{0,1:T(8,128)(2,1)} %param.28) | copy-start | bytes 49156
  86.3 1.0 copy-start.8
  105.2 1.9 copy-start.9
  107.0 3.4 copy-start.24
  107.0 3.4 copy-start.26
  107.0 3.4 copy-start.28
  107.0 3.4 copy-start.30
  107.1 3.4 copy-start.34
  110.4 3.1 copy-start.10
  113.5 134.0 %collective-permute-start = (bf16[512,1024]{1,0:T(8,128)(2,1)}, bf16[512,1024]{1,0:T(8,128)(2,1)}, u32[]{:S(2)}, u32[]{:S(2)}) collective-permute-start(bf16[512,1024]{1,0:T(8,128)(2,1)} %multiply_convert_fusion.normed_ref), channel_id=1, source_target_pairs={{0,2},{1,3},{2,0},{3,1},{4,6},{5,7},{6,4},{7,5},{8,10},{9,11},{10,... | collective-permute-start | bytes 3145736 | tf_op jit(solution)/shard_map/ppermute | solution.py:1593
  114.3 108.8 %copy-start.36 = (s32[512,1]{0,1:T(1,128)S(1)}, s32[512,1]{0,1:T(1,128)}, u32[]{:S(2)}) copy-start(s32[512,1]{0,1:T(1,128)} %copy-done.35) | copy-start | bytes 6148
  223.2 3.5 copy-start.21
  223.2 3.5 copy-start.39
  226.7 3.1 copy-start.17
  226.7 3.1 copy-start.33
  229.9 3.5 copy-start.11
  233.4 1.7 copy-start.18
  233.4 2.2 copy-start.19
  233.4 2.5 copy-start.22
  241.4 4.7 copy-start.13
  241.4 4.7 copy-start.25
  241.4 4.7 copy-start.27
  241.4 4.7 copy-start.29
  241.5 4.7 copy-start.31
  247.5 3.2 copy-start.7
  371.7 1.6 copy-start.2
  373.3 3.3 copy-start.12
  376.6 2.2 copy-start.40
  523.1 1.7 copy-start.23
  527.8 3.9 copy-start.16
  531.7 2.9 copy-start.15
  534.6 2.9 copy-start.14
  534.6 4.4 copy-start.1
Sparse Core Ops, SparseCore 0:
  11.5 93.7 all-gather.1

commit v4 on v3

--- a/solution.py
+++ b/solution.py
@@ -18,6 +18,7 @@
 GELU_A = 0.7978845608028654
 GELU_B = 0.044715
 PEERS = [2, 4, 3, 5, 6, 7, 1]
+ROW_PEERS = [6, 7, 2, 3, 4, 5, 1]
 
 
 def rms_norm(value, gain):
@@ -277,48 +278,89 @@
     query_ref,
     key_ref,
     value_ref,
-    table_ref,
-    sent_ref,
-    out_ref,
-    probs_ref,
-    came_ref,
+    line_ref,
+    both_ref,
+    signs_ref,
+    cot_ref,
+    routing_hbm,
+    w_out_ref,
+    gain2_ref,
+    attended_out,
+    probs_out,
+    came_out,
     normed_out,
     qkv_out,
+    w_cat_out,
+    cot_far_out,
+    routing_far_out,
+    mixed_ref,
+    normed2_ref,
+    table_ref,
+    sends,
     acc_ref,
     block_ref,
     hold_ref,
     normed_ref,
     qkv_ref,
+    attended_ref,
+    w_cat,
+    w_land,
     row_send,
     row_recv,
     hop_send,
     hop_recv,
+    w_send,
+    w_recv,
+    plane_send,
+    plane_recv,
+    far_send,
+    far_recv,
     hold_sem,
     own_sem,
 ):
     z, d = lax.axis_index("head"), lax.axis_index("dp")
     heads, _, _ = table_ref.shape
     replicas, length, columns = block_ref.shape
+    groups, capacity, _ = sends.shape
+    width = input_ref.shape[1]
+    part_rows = w_land.shape[1]
     pairs = heads // 2
     lanes = columns // pairs
     half = lanes // 2
     chunk = 2 * TILE
-    hops = range(1, replicas)
+    hops = [3, 2, 1]
     greet([{"dp": flipped(d, o)} for o in PEERS] + [{"head": flipped(z, r)} for r in hops])
     copies = []
-    for o in PEERS:
-        copies.append(
-            remote(
-                sent_ref.at[o],
-                came_ref.at[o],
-                row_send.at[o],
-                row_recv.at[o],
-                {"dp": flipped(d, o)},
+
+    def launch(*what):
+        copy = remote(*what)
+        copy.start()
+        copies.append(copy)
+        return copy
+
+    piece = w_out_ref.at[pl.ds(pl.multiple_of(d * part_rows, part_rows), part_rows), :]
+    w_hops = {}
+    for r in hops:
+        w_hops[r] = remote(piece, w_land.at[r], w_send.at[r], w_recv.at[r], {"head": flipped(z, r)})
+        w_hops[r].start()
+    for o in PEERS + [0]:
+        span = slice(o * capacity, (o + 1) * capacity)
+        sends[o, :, :width] = jnp.dot(
+            both_ref[span], cot_ref[...], preferred_element_type=F32
+        ).astype(BF)
+        sends[o, :, width:] = signs_ref[span]
+        if o:
+            launch(
+                sends.at[o], came_out.at[o], row_send.at[o], row_recv.at[o], {"dp": flipped(d, o)}
             )
-        )
-        copies[-1].start()
-    own = pltpu.make_async_copy(sent_ref.at[0], came_ref.at[0], own_sem.at[0])
+    own = pltpu.make_async_copy(sends.at[0], came_out.at[0], own_sem.at[0])
     own.start()
+    far = {"head": flipped(z, 2)}
+    launch(routing_hbm, routing_far_out, far_send.at[0], far_recv.at[0], far)
+    early = pl.ds(0, length // 2)
+    launch(cot_ref.at[early], cot_far_out, far_send.at[1], far_recv.at[1], far)
+    skew_kernel(line_ref, table_ref)
+    w_cat[:columns, :] = w_out_ref[...]
 
     moves = []
     for turn, r in enumerate(reversed(range(replicas))):
@@ -381,61 +423,122 @@
             [
                 pltpu.make_async_copy(ref.at[slot], out.at[r], hold_sem.at[i, slot])
                 for i, (ref, out) in enumerate(
-                    ((hold_ref, probs_ref), (normed_ref, normed_out), (qkv_ref, qkv_out))
+                    ((hold_ref, probs_out), (normed_ref, normed_out), (qkv_ref, qkv_out))
                 )
             ]
         )
         for move in moves[-1]:
             move.start()
-        target = out_ref.at[:, pl.ds(r * columns, columns)]
         if r:
-            hop = remote(
-                block_ref.at[r], target, hop_send.at[r], hop_recv.at[r], {"head": flipped(z, r)}
+            launch(
+                block_ref.at[r],
+                attended_ref.at[:, pl.ds(r * columns, columns)],
+                hop_send.at[r],
+                hop_recv.at[r],
+                {"head": flipped(z, r)},
             )
-            hop.start()
-            copies.append(hop)
         else:
-            last = pltpu.make_async_copy(block_ref.at[0], target, own_sem.at[1])
-            last.start()
-    for move in moves[-2] + moves[-1]:
-        move.wait()
-    own.wait()
-    last.wait()
+            attended_ref[:, :columns] = block_ref[0]
+        if turn == 0:
+            for s in hops:
+                w_hops[s].wait()
+                at = pl.multiple_of(s * columns + d * part_rows, part_rows)
+                w_cat[pl.ds(at, part_rows), :] = w_land[s]
+                for o in PEERS:
+                    launch(
+                        w_land.at[s],
+                        w_cat.at[pl.ds(at, part_rows), :],
+                        plane_send.at[s, o],
+                        plane_recv.at[s, o],
+                        {"dp": flipped(d, o)},
+                    )
     for copy in copies:
         copy.wait()
-
-
-def attend_all(inputs, gain, weights, table, sent, length, replicas):
-    heads, _, _ = table.shape
+    outs = [
+        pltpu.make_async_copy(attended_ref, attended_out, own_sem.at[1]),
+        pltpu.make_async_copy(w_cat, w_cat_out, own_sem.at[2]),
+    ]
+    for copy in outs:
+        copy.start()
+
+    def branch_step(i, carry):
+        cols = pl.ds(pl.multiple_of(i * chunk, chunk), chunk)
+        mixed_ref[:, cols] = jnp.dot(
+            attended_ref[...], w_cat[:, cols], preferred_element_type=F32
+        )
+        return carry
+
+    lax.fori_loop(0, width // chunk, branch_step, 0)
+
+    def mixed_step(i, carry):
+        at = pl.multiple_of(i * TILE, TILE)
+        span = pl.ds(at, TILE)
+        rows = pl.multiple_of(z * length + at, TILE)
+        value = mixed_ref[span, :] + input_ref[pl.ds(rows, TILE), :].astype(F32)
+        mixed_ref[span, :] = value
+        normed2_ref[span, :] = rms_norm(value, gain2_ref[...]).astype(BF)
+        return carry
+
+    lax.fori_loop(0, length // TILE, mixed_step, 0)
+    for move in moves[-2] + moves[-1] + outs + [own]:
+        move.wait()
+
+
+def attend_all(inputs, gain, weights, line, both, signs, cot, routing, w_out, gain2, groups):
+    heads, _, table_width = line.shape
     width = inputs.shape[1]
+    length = cot.shape[0]
+    replicas = inputs.shape[0] // length
     columns = weights[0].shape[1]
     lanes = 2 * columns // heads
-    groups = sent.shape[0]
+    capacity = both.shape[0] // groups
+    part_rows = columns // groups
     vmem = pl.BlockSpec(memory_space=pltpu.VMEM)
     hbm = pl.BlockSpec(memory_space=pl.ANY)
+    came_shape = (groups, capacity, width + TILE)
+    plane_sem = pltpu.SemaphoreType.DMA((groups,))
+    hop_sem = pltpu.SemaphoreType.DMA((replicas,))
+    both_sem = pltpu.SemaphoreType.DMA((replicas, groups))
+    two_sem = pltpu.SemaphoreType.DMA((2,))
     return pl.pallas_call(
         attend_all_kernel,
         out_shape=(
             jax.ShapeDtypeStruct((length, replicas * columns), BF),
             jax.ShapeDtypeStruct((replicas, heads, length, length), BF),
-            jax.ShapeDtypeStruct(sent.shape, BF),
+            jax.ShapeDtypeStruct(came_shape, BF),
             jax.ShapeDtypeStruct((replicas, length, width), BF),
             jax.ShapeDtypeStruct((replicas, length, 3 * columns), BF),
+            jax.ShapeDtypeStruct((replicas * columns, width), BF),
+            jax.ShapeDtypeStruct((length // 2, width), BF),
+            jax.ShapeDtypeStruct(routing.shape, routing.dtype),
+            jax.ShapeDtypeStruct((length, width), F32),
+            jax.ShapeDtypeStruct((length, width), BF),
         ),
-        in_specs=[vmem] * 6 + [hbm],
-        out_specs=[hbm] * 5,
+        in_specs=[vmem] * 9 + [hbm] + [vmem] * 2,
+        out_specs=[hbm] * 8 + [vmem] * 2,
         scratch_shapes=[
+            pltpu.VMEM((heads, TILE, table_width), F32),
+            pltpu.VMEM(came_shape, BF),
             pltpu.VMEM((lanes, length), F32),
             pltpu.VMEM((replicas, length, columns), BF),
             pltpu.VMEM((2, heads, length, length), BF),
             pltpu.VMEM((2, length, width), BF),
             pltpu.VMEM((2, length, 3 * columns), BF),
-            pltpu.SemaphoreType.DMA((groups,)),
-            pltpu.SemaphoreType.DMA((groups,)),
-            pltpu.SemaphoreType.DMA((replicas,)),
-            pltpu.SemaphoreType.DMA((replicas,)),
+            pltpu.VMEM((length, replicas * columns), BF),
+            pltpu.VMEM((replicas * columns, width), BF),
+            pltpu.VMEM((replicas, part_rows, width), BF),
+            plane_sem,
+            plane_sem,
+            hop_sem,
+            hop_sem,
+            hop_sem,
+            hop_sem,
+            both_sem,
+            both_sem,
+            two_sem,
+            two_sem,
             pltpu.SemaphoreType.DMA((3, 2)),
-            pltpu.SemaphoreType.DMA((2,)),
+            pltpu.SemaphoreType.DMA((3,)),
         ],
         compiler_params=pltpu.CompilerParams(
             vmem_limit_bytes=VMEM_LIMIT, collective_id=1, has_side_effects=True
@@ -446,7 +549,7 @@
             transcendentals=replicas * heads * length * length,
         ),
         name="attend_all",
-    )(inputs, gain, *weights, table, sent)
+    )(inputs, gain, *weights, line, both, signs, cot, routing, w_out, gain2)
 
 
 def expert_tile(rows, scaled, gate_w, up_w, down_w):
@@ -481,6 +584,7 @@
     gate_hbm,
     up_hbm,
     down_hbm,
+    cot_hbm,
     rows_out,
     hidden_out,
     grad_gate_out,
@@ -488,6 +592,8 @@
     scaled_out,
     back_out,
     grad_back_out,
+    far_out,
+    cot_far_out,
     gate_w,
     up_w,
     down_w,
@@ -508,8 +614,10 @@
     grad_recv,
     unit_sem,
     keep_sem,
+    far_sem,
 ):
-    d = lax.axis_index("dp")
+    z, d = lax.axis_index("head"), lax.axis_index("dp")
+    far = {"head": flipped(z, 2)}
     groups, capacity, _ = rows.shape
     units = gate_w.shape[1]
     tiles = units // tile
@@ -535,10 +643,10 @@
         return carry
 
     lax.fori_loop(0, tiles, start_weights, 0)
-    greet([{"dp": flipped(d, o)} for o in PEERS])
+    greet([{"dp": flipped(d, o)} for o in ROW_PEERS] + [far])
     pending = []
     arrivals = {}
-    for o in PEERS:
+    for o in ROW_PEERS:
         sends[o] = jnp.dot(
             both_ref[o * capacity : (o + 1) * capacity],
             normed_ref[...],
@@ -548,19 +656,32 @@
             sends.at[o], rows.at[o], row_send.at[o], row_recv.at[o], {"dp": flipped(d, o)}
         )
         arrivals[o].start()
+    over = [
+        remote(normed_ref, far_out, far_sem.at[0, 0], far_sem.at[0, 1], far),
+        remote(
+            cot_hbm.at[pl.ds(cot_far_out.shape[0], cot_far_out.shape[0])],
+            cot_far_out,
+            far_sem.at[1, 0],
+            far_sem.at[1, 1],
+            far,
+        ),
+    ]
+    for copy in over:
+        copy.start()
     rows[0] = jnp.dot(
         both_ref[:capacity], normed_ref[...], preferred_element_type=F32
     ).astype(BF)
 
     unit_copies = {}
-    for j in range(groups // 2):
+    order = [0, 3, 1, 2]
+    for turn, j in enumerate(order):
         pair = (2 * j, 2 * j + 1)
-        slot = j % 2
+        slot = turn % 2
         for o in pair:
             if o:
                 arrivals[o].wait_recv()
-        if j >= 2:
-            for copy in unit_copies[j - 2]:
+        if turn >= 2:
+            for copy in unit_copies[order[turn - 2]]:
                 copy.wait()
         here = rows[2 * j : 2 * j + 2].reshape(count, width)
         extended = cot_ref[2 * j : 2 * j + 2].reshape(count, cot_ref.shape[2])
@@ -638,16 +759,18 @@
     ]
     for copy in keeps:
         copy.start()
-    for j in range(groups // 2 - 2, groups // 2):
+    for j in order[-2:]:
         for copy in unit_copies[j]:
             copy.wait()
-    for o in PEERS:
+    for o in ROW_PEERS:
         arrivals[o].wait_send()
-    for copy in pending + keeps:
+    for copy in pending + keeps + over:
         copy.wait()
 
 
-def expert_stage(normed2, both, cot, router, gate_w, up_w, down_w, groups, capacity, tile):
+def expert_stage(
+    normed2, both, cot, router, gate_w, up_w, down_w, cot_own, groups, capacity, tile
+):
     width, units = gate_w.shape
     slots = groups * capacity
     vmem = pl.BlockSpec(memory_space=pltpu.VMEM)
@@ -659,9 +782,15 @@
     row_sem = pltpu.SemaphoreType.DMA((groups,))
     return pl.pallas_call(
         functools.partial(expert_kernel, width, tile),
-        out_shape=(row_shape,) + (unit_shape,) * 3 + (row_shape,) * 3,
-        in_specs=[vmem] * 4 + [hbm] * 3,
-        out_specs=[hbm] * 7,
+        out_shape=(row_shape,)
+        + (unit_shape,) * 3
+        + (row_shape,) * 3
+        + (
+            jax.ShapeDtypeStruct(normed2.shape, BF),
+            jax.ShapeDtypeStruct((normed2.shape[0] // 2, width), BF),
+        ),
+        in_specs=[vmem] * 4 + [hbm] * 4,
+        out_specs=[hbm] * 9,
         scratch_shapes=[
             pltpu.VMEM((width, units), BF),
             pltpu.VMEM((width, units), BF),
@@ -683,6 +812,7 @@
             row_sem,
             pltpu.SemaphoreType.DMA((2, 3)),
             pltpu.SemaphoreType.DMA((2,)),
+            pltpu.SemaphoreType.DMA((2, 2)),
         ],
         compiler_params=pltpu.CompilerParams(
             vmem_limit_bytes=VMEM_MOST, collective_id=2, has_side_effects=True
@@ -693,29 +823,150 @@
             transcendentals=slots * units,
         ),
         name="expert_stage",
-    )(normed2, both, cot, router, gate_w, up_w, down_w)
+    )(normed2, both, cot, router, gate_w, up_w, down_w, cot_own)
+
+
+def split_parts(value):
+    first = value.astype(BF)
+    rest = value - first.astype(F32)
+    second = rest.astype(BF)
+    return first, second, (rest - second.astype(F32)).astype(BF)
+
+
+def combine_kernel(
+    back_ref,
+    grad_back_ref,
+    first_ref,
+    second_ref,
+    mixed_ref,
+    normed2_ref,
+    cot_ref,
+    signs_ref,
+    router_ref,
+    gain_ref,
+    w_cat_ref,
+    output_ref,
+    grad_mixed_ref,
+    grad_branch_ref,
+    grad_heads_ref,
+    grad_router_ref,
+    grad_norm2_ref,
+    picked,
+    slopes,
+):
+    length, width = mixed_ref.shape
+    chunk = 2 * TILE
+
+    def pick_step(i, carry):
+        cols = pl.ds(pl.multiple_of(i * chunk, chunk), chunk)
+        for k, (pick, source) in enumerate(((first_ref, back_ref), (second_ref, back_ref))):
+            picked[k, :, cols] = jnp.dot(pick[...], source[:, cols], preferred_element_type=F32)
+        picked[2, :, cols] = jnp.dot(
+            first_ref[...] + second_ref[...], grad_back_ref[:, cols], preferred_element_type=F32
+        )
+        return carry
+
+    lax.fori_loop(0, width // chunk, pick_step, 0)
+
+    def row_step(i, total):
+        span = pl.ds(pl.multiple_of(i * TILE, TILE), TILE)
+        sign = signs_ref[span, :].astype(F32)
+        logits = jnp.dot(normed2_ref[span, :], router_ref[...], preferred_element_type=F32)
+        gap = jnp.sum(logits * sign, axis=1, keepdims=True)
+        gate0, gate1 = 1.0 / (1.0 + jnp.exp(gap)), 1.0 / (1.0 + jnp.exp(-gap))
+        cot = cot_ref[span, :].astype(F32)
+        mixed = mixed_ref[span, :]
+        row0, row1 = picked[0, span, :], picked[1, span, :]
+        output_ref[span, :] = mixed + (gate0 * row0 + gate1 * row1)
+        grad_gap = jnp.sum(cot * (row1 - row0), axis=1, keepdims=True)
+        slope = gate0 * gate1 * grad_gap * sign
+        slopes[span, :] = slope
+        grad_normed2 = picked[2, span, :] + sum(
+            contract(part, router_ref[...], 1, 1) for part in split_parts(slope)
+        )
+        scale = lax.rsqrt(jnp.mean(mixed * mixed, axis=1, keepdims=True) + EPS)
+        inner = grad_normed2 * gain_ref[...]
+        mean = jnp.mean(inner * mixed, axis=1, keepdims=True)
+        grad_mixed = cot + scale * inner - mixed * (scale * scale * scale * mean)
+        grad_mixed_ref[span, :] = grad_mixed
+        grad_branch_ref[span, :] = grad_mixed.astype(BF)
+        return total + jnp.sum(grad_normed2 * mixed * scale, axis=0, keepdims=True)
+
+    grad_norm2_ref[...] = lax.fori_loop(
+        0, length // TILE, row_step, jnp.zeros((1, width), F32)
+    )
+
+    def head_step(i, carry):
+        cols = pl.ds(pl.multiple_of(i * chunk, chunk), chunk)
+        grad_heads_ref[:, cols] = contract(grad_branch_ref[...], w_cat_ref[cols, :], 1, 1).astype(BF)
+        return carry
+
+    lax.fori_loop(0, w_cat_ref.shape[0] // chunk, head_step, 0)
+    experts = grad_router_ref.shape[0]
+    grad_router_ref[...] = sum(
+        contract(part, normed2_ref[...], 0, 0) for part in split_parts(slopes[...])
+    )[:experts]
+
+
+def combine(back, grad_back, picks, mixed, normed2, cot, signs, router, gain, w_cat, experts):
+    length, width = mixed.shape
+    vmem = pl.BlockSpec(memory_space=pltpu.VMEM)
+    return pl.pallas_call(
+        combine_kernel,
+        out_shape=(
+            jax.ShapeDtypeStruct((length, width), F32),
+            jax.ShapeDtypeStruct((length, width), F32),
+            jax.ShapeDtypeStruct((length, width), BF),
+            jax.ShapeDtypeStruct((length, w_cat.shape[0]), BF),
+            jax.ShapeDtypeStruct((experts, width), F32),
+            jax.ShapeDtypeStruct((1, width), F32),
+        ),
+        in_specs=[vmem] * 11,
+        out_specs=[vmem] * 6,
+        scratch_shapes=[pltpu.VMEM((3, length, width), F32), pltpu.VMEM((length, TILE), F32)],
+        compiler_params=pltpu.CompilerParams(vmem_limit_bytes=VMEM_LIMIT),
+        cost_estimate=pl.CostEstimate(
+            flops=6 * length * back.shape[0] * width,
+            bytes_accessed=4 * back.shape[0] * width,
+            transcendentals=0,
+        ),
+        name="combine",
+    )(back, grad_back, *picks, mixed, normed2, cot, signs, router, gain, w_cat)
 
 
 def attend_back_kernel(
-    far_ref,
+    normed2_far,
+    cot_far,
+    cot_rest,
     both_ref,
     signs_ref,
     grad_ref,
     qkv_hbm,
     probs_hbm,
+    normed_hbm,
     query_w,
     key_w,
     value_w,
+    attended_ref,
+    grad_branch_ref,
+    grad_mixed_ref,
+    input_ref,
+    gain_ref,
     far_out,
-    grad_qkv_out,
-    grad_normed_out,
+    qkv_w_ref,
+    out_w_ref,
+    grad_input_ref,
+    norm1_ref,
+    lines_ref,
     sums_ref,
     acc_ref,
     sends,
     grads,
     qkv_ref,
     probs_ref,
+    normed_ref,
     grad_qkv_ref,
+    weight_sum,
     parts,
     landed,
     far_send,
@@ -725,25 +976,27 @@
     part_send,
     part_recv,
     load_sem,
-    store_sem,
     own_sem,
 ):
     z, d = lax.axis_index("head"), lax.axis_index("dp")
     replicas, length, columns = grads.shape
     groups, capacity, extent = sends.shape
-    heads, _, width = sums_ref.shape
+    width = input_ref.shape[1]
+    heads = sums_ref.shape[0]
     pairs = heads // 2
     lanes = columns // pairs
     half = lanes // 2
     chunk = 2 * TILE
-    hops = range(1, replicas)
+    hops = [3, 2, 1]
     order = [0, 3, 2, 1]
 
     def loads(turn):
         r, slot = order[turn], turn % 2
         return [
-            pltpu.make_async_copy(qkv_hbm.at[r], qkv_ref.at[slot], load_sem.at[0, slot]),
-            pltpu.make_async_copy(probs_hbm.at[r], probs_ref.at[slot], load_sem.at[1, slot]),
+            pltpu.make_async_copy(source.at[r], target.at[slot], load_sem.at[i, slot])
+            for i, (source, target) in enumerate(
+                ((qkv_hbm, qkv_ref), (probs_hbm, probs_ref), (normed_hbm, normed_ref))
+            )
         ]
 
     for copy in loads(0):
@@ -751,7 +1004,7 @@
     greet([{"dp": flipped(d, o)} for o in PEERS] + [{"head": flipped(z, r)} for r in hops])
     copies = []
     arrivals = {}
-    for r in order[1:]:
+    for r in hops:
         arrivals[r] = remote(
             grad_ref.at[:, pl.ds(r * columns, columns)],
             grads.at[r],
@@ -760,13 +1013,17 @@
             {"head": flipped(z, r)},
         )
         arrivals[r].start()
-    model = extent - TILE
     for o in PEERS + [0]:
         span = slice(o * capacity, (o + 1) * capacity)
-        sends[o, :, :model] = jnp.dot(
-            both_ref[span], far_ref[...], preferred_element_type=F32
+        sends[o, :, :width] = jnp.dot(
+            both_ref[span], normed2_far[...], preferred_element_type=F32
         ).astype(BF)
-        sends[o, :, model:] = signs_ref[span]
+        early = cot_far.shape[0]
+        sends[o, :, width : 2 * width] = (
+            jnp.dot(both_ref[span, :early], cot_far[...], preferred_element_type=F32)
+            + jnp.dot(both_ref[span, early:], cot_rest[...], preferred_element_type=F32)
+        ).astype(BF)
+        sends[o, :, 2 * width :] = signs_ref[span]
         if o:
             copy = remote(
                 sends.at[o],
@@ -782,7 +1039,19 @@
     sums_ref[...] = jnp.zeros_like(sums_ref)
     grads[0] = grad_ref[:, :columns]
 
-    stores = []
+    near, over = {"head": flipped(z, 1)}, {"head": flipped(z, 2)}
+    steps = length // 2
+
+    def half_copy(i, source, target, h, peer):
+        span = pl.ds(h * steps, steps)
+        return remote(
+            parts.at[source, span], landed.at[target, span], part_send.at[i, h], part_recv.at[i, h], peer
+        )
+
+    inner = [half_copy(0, 3, 2, h, near) for h in range(2)]
+    outer = [half_copy(1, 2, 0, h, over) for h in range(2)]
+    direct = [half_copy(2, 1, 1, h, near) for h in range(2)]
+
     for turn, r in enumerate(order):
         slot = turn % 2
         if turn + 1 < replicas:
@@ -792,8 +1061,6 @@
             copy.wait()
         if r:
             arrivals[r].wait_recv()
-        if turn >= 2:
-            stores[turn - 2].wait()
 
         def pair_step(pair, carry, slot=slot, r=r):
             def part_of(j):
@@ -843,13 +1110,9 @@
             return carry
 
         lax.fori_loop(0, pairs, pair_step, 0)
-        stores.append(
-            pltpu.make_async_copy(grad_qkv_ref.at[slot], grad_qkv_out.at[r], store_sem.at[slot])
-        )
-        stores[-1].start()
 
         def part_step(i, carry, slot=slot, r=r):
-            span = pl.ds(pl.multiple_of(i * TILE, TILE), TILE)
+            span = pl.ds(pl.multiple_of(i * chunk, chunk), chunk)
             total = sum(
                 contract(
                     grad_qkv_ref[slot, :, j * columns : (j + 1) * columns], weight[span, :], 1, 1
@@ -859,65 +1122,139 @@
             parts[r, :, span] = total.astype(BF)
             return carry
 
-        lax.fori_loop(0, parts.shape[2] // TILE, part_step, 0)
-        if r:
-            copy = remote(
-                parts.at[r], landed.at[r], part_send.at[r], part_recv.at[r], {"head": flipped(z, r)}
-            )
-            copy.start()
-            copies.append(copy)
-
-    for r in order[1:]:
+        lax.fori_loop(0, width // chunk, part_step, 0)
+        if r == 3:
+            for copy in inner:
+                copy.start()
+        if r == 1:
+            for copy in direct:
+                copy.start()
+
+        def weight_step(i, carry, slot=slot, turn=turn):
+            cols = pl.ds(pl.multiple_of(i * chunk, chunk), chunk)
+            value = contract(normed_ref[slot, :, cols], grad_qkv_ref[slot], 0, 0)
+            if turn:
+                value = value + weight_sum[cols, :]
+            if turn + 1 < replicas:
+                weight_sum[cols, :] = value
+            else:
+                qkv_w_ref[cols, :] = value.astype(BF)
+            return carry
+
+        def relay(h):
+            inner[h].wait_recv()
+            span = slice(h * steps, (h + 1) * steps)
+            parts[2, span, :] = (
+                parts[2, span, :].astype(F32) + landed[2, span, :].astype(F32)
+            ).astype(BF)
+            outer[h].start()
+
+        if turn == replicas - 1:
+            relay(0)
+        lax.fori_loop(0, width // chunk, weight_step, 0)
+    relay(1)
+
+    def wout_step(i, carry):
+        rows = pl.ds(pl.multiple_of(i * chunk, chunk), chunk)
+        out_w_ref[rows, :] = contract(attended_ref[:, rows], grad_branch_ref[...], 0, 0).astype(BF)
+        return carry
+
+    lax.fori_loop(0, out_w_ref.shape[0] // chunk, wout_step, 0)
+    unskew_kernel(sums_ref, lines_ref)
+
+    for copy in direct + outer:
+        copy.wait()
+
+    def end_step(i, total):
+        span = pl.ds(pl.multiple_of(i * TILE, TILE), TILE)
+        grad_normed = (
+            parts[0, span, :].astype(F32)
+            + landed[0, span, :].astype(F32)
+            + landed[1, span, :].astype(F32)
+        )
+        value = input_ref[span, :].astype(F32)
+        scale = lax.rsqrt(jnp.mean(value * value, axis=1, keepdims=True) + EPS)
+        inner_grad = grad_normed * gain_ref[...]
+        mean = jnp.mean(inner_grad * value, axis=1, keepdims=True)
+        grad_input_ref[span, :] = (
+            grad_mixed_ref[span, :] + scale * inner_grad - value * (scale * scale * scale * mean)
+        )
+        return total + jnp.sum(grad_normed * value * scale, axis=0, keepdims=True)
+
+    norm1_ref[...] = lax.fori_loop(0, length // TILE, end_step, jnp.zeros((1, width), F32))
+    for r in hops:
         arrivals[r].wait_send()
-    stores[-2].wait()
-    stores[-1].wait()
+    for copy in inner:
+        copy.wait_send()
     for copy in copies:
         copy.wait()
-    grad_normed_out[...] = parts[0].astype(F32) + sum(landed[r].astype(F32) for r in hops)
-
-
-def attend_back(far_own, both_far, signs_far, grad_heads, qkv, probs, weights, groups):
+
+
+def attend_back(
+    normed2_far,
+    cot_far,
+    cot_rest,
+    both_far,
+    signs_far,
+    grad_heads,
+    qkv,
+    probs,
+    normed,
+    weights,
+    attended,
+    grad_branch,
+    grad_mixed,
+    inputs,
+    gain,
+    groups,
+):
     replicas, length, triple = qkv.shape
     heads = probs.shape[1]
     columns = triple // 3
-    width = weights[0].shape[0]
+    width = inputs.shape[1]
     lanes = 2 * columns // heads
     capacity = both_far.shape[0] // groups
-    extent = far_own.shape[1] + TILE
+    extent = 2 * width + TILE
     vmem = pl.BlockSpec(memory_space=pltpu.VMEM)
     hbm = pl.BlockSpec(memory_space=pl.ANY)
     hop_sem = pltpu.SemaphoreType.DMA((replicas,))
+    plane_sem = pltpu.SemaphoreType.DMA((groups,))
+    part_sem = pltpu.SemaphoreType.DMA((3, 2))
     return pl.pallas_call(
         attend_back_kernel,
         out_shape=(
             jax.ShapeDtypeStruct((groups, capacity, extent), BF),
-            jax.ShapeDtypeStruct((replicas, length, triple), BF),
+            jax.ShapeDtypeStruct((width, triple), BF),
+            jax.ShapeDtypeStruct((replicas * columns, width), BF),
             jax.ShapeDtypeStruct((length, width), F32),
-            jax.ShapeDtypeStruct((heads, TILE, 2 * length), F32),
+            jax.ShapeDtypeStruct((1, width), F32),
+            jax.ShapeDtypeStruct((heads, 1, 2 * length), F32),
         ),
-        in_specs=[vmem] * 4 + [hbm] * 2 + [vmem] * 3,
-        out_specs=[hbm, hbm, vmem, vmem],
+        in_specs=[vmem] * 6 + [hbm] * 3 + [vmem] * 8,
+        out_specs=[hbm] + [vmem] * 5,
         scratch_shapes=[
+            pltpu.VMEM((heads, TILE, 2 * length), F32),
             pltpu.VMEM((lanes, length), F32),
             pltpu.VMEM((groups, capacity, extent), BF),
             pltpu.VMEM((replicas, length, columns), BF),
             pltpu.VMEM((2, length, triple), BF),
             pltpu.VMEM((2, heads, length, length), BF),
+            pltpu.VMEM((2, length, width), BF),
             pltpu.VMEM((2, length, triple), BF),
+            pltpu.VMEM((width, triple), F32),
             pltpu.VMEM((replicas, length, width), BF),
-            pltpu.VMEM((replicas, length, width), BF),
-            pltpu.SemaphoreType.DMA((groups,)),
-            pltpu.SemaphoreType.DMA((groups,)),
+            pltpu.VMEM((3, length, width), BF),
+            plane_sem,
+            plane_sem,
             hop_sem,
             hop_sem,
-            hop_sem,
-            hop_sem,
-            pltpu.SemaphoreType.DMA((2, 2)),
-            pltpu.SemaphoreType.DMA((2,)),
+            part_sem,
+            part_sem,
+            pltpu.SemaphoreType.DMA((3, 2)),
             pltpu.SemaphoreType.DMA,
         ],
         compiler_params=pltpu.CompilerParams(
-            vmem_limit_bytes=VMEM_LIMIT, collective_id=3, has_side_effects=True
+            vmem_limit_bytes=VMEM_MOST, collective_id=3, has_side_effects=True
         ),
         cost_estimate=pl.CostEstimate(
             flops=replicas * heads * 16 * length * length * lanes,
@@ -925,7 +1262,23 @@
             transcendentals=0,
         ),
         name="attend_back",
-    )(far_own, both_far, signs_far, grad_heads, qkv, probs, *weights)
+    )(
+        normed2_far,
+        cot_far,
+        cot_rest,
+        both_far,
+        signs_far,
+        grad_heads,
+        qkv,
+        probs,
+        normed,
+        *weights,
+        attended,
+        grad_branch,
+        grad_mixed,
+        inputs,
+        gain,
+    )
 
 
 def last_kernel(
@@ -942,7 +1295,10 @@
     hidden_hbm,
     qkv_w_hbm,
     out_w_hbm,
-    small_ref,
+    norm1_ref,
+    norm2_ref,
+    router_grad_ref,
+    lines_ref,
     gate_out,
     up_out,
     down_out,
@@ -966,6 +1322,7 @@
     out_sum,
     out_hop,
     out_last,
+    small_own,
     small_land,
     small_sum,
     small_hop,
@@ -1021,6 +1378,14 @@
     half_copy.start()
     greet([{"dp": flipped(d, o)} for o in PEERS] + [{"head": flipped(z, r)} for r in hops])
 
+    heads = lines_ref.shape[0]
+    small_own[...] = jnp.zeros_like(small_own)
+    small_own[0:1] = norm1_ref[...]
+    small_own[1:2] = norm2_ref[...]
+    for h in range(heads):
+        small_own[2 + h : 3 + h] = lines_ref[h]
+    small_own[8:] = router_grad_ref[...]
+
     first = []
     for o in PEERS:
         peer = flipped(d, o)
@@ -1028,7 +1393,7 @@
             (
                 (qkv_w_hbm.at[peer], qkv_land.at[o]),
                 (out_w_hbm.at[:, peer], out_land.at[o]),
-                (small_ref, small_land.at[o]),
+                (small_own, small_land.at[o]),
             )
         ):
             copy = remote(source, target, first_send.at[i, o], first_recv.at[i, o], {"dp": peer})
@@ -1104,14 +1469,13 @@
             wide_copy(i, t).start()
         return carry
 
-    middle = tiles // 2
-    lax.fori_loop(0, middle, tile_step, 0)
+    lax.fori_loop(0, tiles, tile_step, 0)
 
     for copy in first:
         copy.wait()
     for copy in own:
         copy.wait()
-    small_land[0] = small_ref[...]
+    small_land[0] = small_own[...]
     qkv_sum[...] = sum(qkv_land[o].astype(F32) for o in range(groups)).astype(BF)
     out_sum[...] = sum(out_land[o].astype(F32) for o in range(groups)).astype(BF)
     small_sum[...] = sum(small_land[o] for o in range(groups))
@@ -1135,7 +1499,23 @@
             copy.start()
             over.append(copy)
 
-    lax.fori_loop(middle, tiles, tile_step, 0)
+    half_copy.wait()
+    share = half_units // 2
+    halves = pl.ds(pl.multiple_of(high * half_units, TILE), half_units)
+
+    def tall_step(i, carry):
+        cols = pl.ds(pl.multiple_of(i * tile, tile), tile)
+        value = contract(hidden_here[...], scaled_here[:, cols], 0, 0) + contract(
+            hidden[:, halves], scaled[:, cols], 0, 0
+        )
+        upper = low == 1
+        send_tall[:, cols] = jnp.where(upper, value[:share], value[share:]).astype(BF)
+        down_out[:, cols] = jnp.where(upper, value[share:], value[:share])
+        return carry
+
+    lax.fori_loop(0, width // tile, tall_step, 0)
+    tall = remote(send_tall, came_tall, tall_sem.at[0], tall_sem.at[1], near)
+    tall.start()
 
     for copy in over:
         copy.wait()
@@ -1157,24 +1537,6 @@
     mine.append(pltpu.make_async_copy(out_last, out_w_out.at[d], own_sem.at[1]))
     mine[1].start()
 
-    half_copy.wait()
-    share = half_units // 2
-    halves = pl.ds(pl.multiple_of(high * half_units, TILE), half_units)
-
-    def tall_step(i, carry):
-        cols = pl.ds(pl.multiple_of(i * tile, tile), tile)
-        value = contract(hidden_here[...], scaled_here[:, cols], 0, 0) + contract(
-            hidden[:, halves], scaled[:, cols], 0, 0
-        )
-        upper = low == 1
-        send_tall[:, cols] = jnp.where(upper, value[:share], value[share:]).astype(BF)
-        down_out[:, cols] = jnp.where(upper, value[share:], value[:share])
-        return carry
-
-    lax.fori_loop(0, width // tile, tall_step, 0)
-    tall = remote(send_tall, came_tall, tall_sem.at[0], tall_sem.at[1], near)
-    tall.start()
-
     def wide_end(t, carry):
         at = pl.multiple_of(t * tile, tile)
         for i, out in enumerate((gate_out, up_out)):
@@ -1200,6 +1562,7 @@
     vmem = pl.BlockSpec(memory_space=pltpu.VMEM)
     hbm = pl.BlockSpec(memory_space=pl.ANY)
     rows, share = width // replicas, units // replicas
+    small_shape = (8 + groups, width)
     plane_sem = pltpu.SemaphoreType.DMA((3, groups))
     hop_sem = pltpu.SemaphoreType.DMA((2, replicas))
     return pl.pallas_call(
@@ -1210,9 +1573,9 @@
             jax.ShapeDtypeStruct((share, width), F32),
             jax.ShapeDtypeStruct(qkv_w.shape, BF),
             jax.ShapeDtypeStruct(out_w.shape[1:], BF),
-            jax.ShapeDtypeStruct((2,) + small.shape, F32),
+            jax.ShapeDtypeStruct((2,) + small_shape, F32),
         ),
-        in_specs=[vmem] * 4 + [hbm] * 8 + [vmem],
+        in_specs=[vmem] * 4 + [hbm] * 8 + [vmem] * 4,
         out_specs=[vmem, vmem, vmem, hbm, hbm, vmem],
         scratch_shapes=[
             pltpu.VMEM((slots, width), BF),
@@ -1232,9 +1595,10 @@
             pltpu.VMEM((replicas, part_rows, width), BF),
             pltpu.VMEM((replicas, part_rows, width), BF),
             pltpu.VMEM((part_rows, width), BF),
-            pltpu.VMEM((groups,) + small.shape, F32),
-            pltpu.VMEM(small.shape, F32),
-            pltpu.VMEM((replicas,) + small.shape, F32),
+            pltpu.VMEM(small_shape, F32),
+            pltpu.VMEM((groups,) + small_shape, F32),
+            pltpu.VMEM(small_shape, F32),
+            pltpu.VMEM((replicas,) + small_shape, F32),
             pltpu.SemaphoreType.DMA((5, 2)),
             pltpu.SemaphoreType.DMA,
             pltpu.SemaphoreType.DMA((2, units // tile)),
@@ -1269,7 +1633,7 @@
         hidden_here,
         qkv_w,
         out_w,
-        small,
+        *small,
     )
 
 
@@ -1552,7 +1916,7 @@
         and groups == 8
         and experts == groups
         and capacity % 16 == 0
-        and pos_bias.shape[1] % 2 == 0
+        and pos_bias.shape[1] in (2, 4, 6)
         and w_gate.shape[2] % 256 == 0
     )
     return body_steps(*args) if stepwise else body_plain(*args)
@@ -1586,11 +1950,6 @@
     slot_count = experts * capacity
     replicas, groups = lax.axis_size("head"), lax.axis_size("dp")
     me, dp_at = lax.axis_index("head"), lax.axis_index("dp")
-    far = replicas // 2
-    far_perm = [(i, i ^ far) for i in range(replicas)]
-
-    def hop(value, r):
-        return lax.ppermute(value, "head", [(i, i ^ r) for i in range(replicas)])
 
     dest = route_slots(expert_ids, priority[0], experts, capacity)
     mixed_dest = jnp.where(
@@ -1598,95 +1957,112 @@
         ((dest // capacity) ^ dp_at) * capacity + dest % capacity,
         slot_count,
     )
-    routing_far = hop(jnp.concatenate([mixed_dest, expert_ids], axis=1), far)
+    routing = jnp.concatenate([mixed_dest, expert_ids], axis=1)
     slot_row = jnp.arange(slot_count, dtype=jnp.int32)[None, :]
     slot_col = jnp.arange(slot_count, dtype=jnp.int32)[:, None]
-    expert_range = jnp.arange(experts, dtype=jnp.int32)
     lane_range = jnp.arange(TILE, dtype=jnp.int32)[None, :]
+
+    def token_signs(ids):
+        return (ids[:, 1:2] == lane_range).astype(BF) - (ids[:, 0:1] == lane_range).astype(BF)
 
     def dispatch_of(places, ids):
         first = (slot_col == places[:, 0][None, :]).astype(BF)
         second = (slot_col == places[:, 1][None, :]).astype(BF)
-        signs = (ids[:, 1:2] == lane_range).astype(BF) - (ids[:, 0:1] == lane_range).astype(BF)
-        return first + second, contract(first - second, signs, 1, 0).astype(BF)
+        return first + second, contract(first - second, token_signs(ids), 1, 0).astype(BF)
 
     both, signs = dispatch_of(mixed_dest, expert_ids)
-    both_far, signs_far = dispatch_of(routing_far[:, :2], routing_far[:, 2:])
     picks = [(mixed_dest[:, k : k + 1] == slot_row).astype(BF) for k in range(2)]
     router_wide = jnp.pad(w_router, ((0, 0), (0, TILE - experts)))
-    cot_sent = jnp.concatenate([contract(both, cotangent, 1, 0).astype(BF), signs], axis=1)
-    cot_sent = cot_sent.reshape(experts, capacity, width + TILE)
-    cot_far_own = hop(cotangent, far)
-
-    out_rows = head_cols // groups
-    piece = lax.dynamic_slice_in_dim(w_out, dp_at * out_rows, out_rows, 0)
-    w_out_all = lax.all_gather(piece, ("head", "dp"), axis=0, tiled=True)
-    order = [me ^ r for r in range(replicas)]
-    w_out_all = w_out_all.reshape(replicas, head_cols, width)
-    w_out_cat = jnp.concatenate(
-        [lax.dynamic_index_in_dim(w_out_all, o, 0, keepdims=False) for o in order], axis=0
-    )
-
     line = (rel_bucket[::-1][None, :] == jnp.arange(buckets, dtype=jnp.int32)[:, None]).astype(F32)
     line = jnp.pad(line, ((0, 0), (1, 0)))
-    table = skew(contract(pos_bias, line, 0, 0, HIGH))
     input_weights = (w_query, w_key, w_value)
-    attended, probs, cot_here, normed, qkv = attend_all(
-        block_input, norm1_gain[None, :], input_weights, table, cot_sent, length, replicas
+    (
+        attended,
+        probs,
+        cot_here,
+        normed,
+        qkv,
+        w_cat,
+        cot_far,
+        routing_far,
+        mixed,
+        normed2,
+    ) = attend_all(
+        block_input,
+        norm1_gain[None, :],
+        input_weights,
+        contract(pos_bias, line, 0, 0, HIGH)[:, None, :],
+        both,
+        signs,
+        cotangent,
+        routing,
+        w_out,
+        norm2_gain[None, :],
+        groups,
     )
 
-    branch = jnp.dot(attended, w_out_cat, preferred_element_type=F32)
-    inputs_own = lax.dynamic_slice_in_dim(block_input, me * own_rows, own_rows, 0).astype(F32)
-    mixed = inputs_own + branch
-    normed2_full, norm2_pull = jax.vjp(rms_norm, mixed, norm2_gain)
-    normed2 = normed2_full.astype(BF)
-
     gate_w, up_w, down_w = w_gate[0], w_up[0], w_down[0]
-    normed2_far = hop(normed2, far)
     tile = 256
-    (rows_here, hidden_here, ggp_here, gup_here, scaled_here, came_back, grad_back) = expert_stage(
-        normed2, both, cot_here, router_wide, gate_w, up_w, down_w, groups, capacity, tile
+    (
+        rows_here,
+        hidden_here,
+        ggp_here,
+        gup_here,
+        scaled_here,
+        came_back,
+        grad_back,
+        normed2_far,
+        cot_far_rest,
+    ) = expert_stage(
+        normed2,
+        both,
+        cot_here,
+        router_wide,
+        gate_w,
+        up_w,
+        down_w,
+        cotangent,
+        groups,
+        capacity,
+        tile,
     )
     rows_here = rows_here.reshape(slot_count, width)
     scaled_here = scaled_here.reshape(slot_count, width)
-    came_back = came_back.reshape(slot_count, width)
-    grad_back = grad_back.reshape(slot_count, width)
-
-    logits = jnp.dot(normed2, w_router, preferred_element_type=F32)
-    chosen = (expert_ids[:, :, None] == expert_range[None, None, :]).astype(F32)
-    gates = jax.nn.softmax(jnp.sum(chosen * logits[:, None, :], axis=2), axis=-1)
-    chosen_rows = [jnp.dot(pick, came_back, preferred_element_type=F32) for pick in picks]
-    output = mixed + sum(gates[:, k : k + 1] * chosen_rows[k] for k in range(2))
-    grad_output = cotangent.astype(F32)
-    grad_gates = jnp.stack([jnp.sum(grad_output * rows, axis=1) for rows in chosen_rows], axis=1)
-    grad_normed2 = jnp.dot(picks[0] + picks[1], grad_back, preferred_element_type=F32)
-    grad_picked = gates * (grad_gates - jnp.sum(gates * grad_gates, axis=1, keepdims=True))
-    grad_logits = jnp.sum(chosen * grad_picked[:, :, None], axis=1)
-    grad_normed2 = grad_normed2 + contract(grad_logits, w_router.astype(F32), 1, 1, HIGH)
-    grad_router = contract(normed2.astype(F32), grad_logits, 0, 0, HIGH)
-    grad_mixed, grad_norm2 = norm2_pull(grad_normed2)
-    grad_mixed = grad_mixed + grad_output
-    grad_branch = grad_mixed.astype(BF)
-    grad_wout = contract(attended, grad_branch, 0, 0).astype(BF)
-    grad_heads = contract(grad_branch, w_out_cat, 1, 1).astype(BF)
-
-    far_own = jnp.concatenate([normed2_far, cot_far_own], axis=1)
-    far_came, grad_qkv, grad_normed, sums = attend_back(
-        far_own, both_far, signs_far, grad_heads, qkv, probs, input_weights, groups
+
+    output, grad_mixed, grad_branch, grad_heads, grad_router, grad_norm2 = combine(
+        came_back.reshape(slot_count, width),
+        grad_back.reshape(slot_count, width),
+        picks,
+        mixed,
+        normed2,
+        cotangent,
+        token_signs(expert_ids),
+        router_wide,
+        norm2_gain[None, :],
+        w_cat,
+        experts,
     )
-    grad_qkv_w = lax.dot_general(
-        normed, grad_qkv, (((0, 1), (0, 1)), ((), ())), preferred_element_type=F32
-    ).astype(BF)
-    _, norm1_pull = jax.vjp(rms_norm, inputs_own, norm1_gain)
-    grad_first, grad_norm1 = norm1_pull(grad_normed)
-    grad_input = grad_mixed + grad_first
-    grad_bias = contract(line, unskew(sums), 1, 1, HIGH)
-
-    flat = jnp.concatenate(
-        [grad_norm1, grad_norm2, grad_router.reshape(-1), grad_bias.reshape(-1)]
+
+    both_far, signs_far = dispatch_of(routing_far[:, :2], routing_far[:, 2:])
+    inputs_own = lax.dynamic_slice_in_dim(block_input, me * own_rows, own_rows, 0)
+    far_came, grad_qkv_w, grad_wout, grad_input, grad_norm1, lines = attend_back(
+        normed2_far,
+        cot_far,
+        cot_far_rest,
+        both_far,
+        signs_far,
+        grad_heads,
+        qkv,
+        probs,
+        normed,
+        input_weights,
+        attended,
+        grad_branch,
+        grad_mixed,
+        inputs_own,
+        norm1_gain[None, :],
+        groups,
     )
-    small_rows = -(-flat.shape[0] // (8 * TILE)) * 8
-    small = jnp.pad(flat, (0, small_rows * TILE - flat.shape[0])).reshape(small_rows, TILE)
 
     grad_gate_w, grad_up_w, grad_down_w, grad_qkv_w, grad_out_proj, summed = last_stage(
         far_came,
@@ -1697,26 +2073,23 @@
         (ggp_here, gup_here),
         hidden_here,
         grad_qkv_w.reshape(groups, width // groups, 3 * head_cols),
-        grad_wout.reshape(replicas, groups, out_rows, width),
-        small,
+        grad_wout.reshape(replicas, groups, head_cols // groups, width),
+        (grad_norm1, grad_norm2, grad_router, lines),
         tile,
     )
     grad_qkv_w = grad_qkv_w.reshape(width, 3 * head_cols).astype(F32)
     grad_out_proj = grad_out_proj.reshape(head_cols, width).astype(F32)
-    summed = summed.reshape(2, -1)
-    ends = [width, 2 * width, 2 * width + width * experts]
-    grad_bias = summed[0, ends[2] : ends[2] + buckets * heads_here].reshape(buckets, heads_here)
     return (
         output,
         grad_input,
-        summed[1, : ends[0]],
+        summed[1, 0],
         grad_qkv_w[:, :head_cols],
         grad_qkv_w[:, head_cols : 2 * head_cols],
         grad_qkv_w[:, 2 * head_cols :],
         grad_out_proj,
-        grad_bias,
-        summed[1, ends[0] : ends[1]],
-        summed[1, ends[1] : ends[2]].reshape(width, experts),
+        contract(line, summed[0, 2 : 2 + heads_here], 1, 1, HIGH),
+        summed[1, 1],
+        jnp.transpose(summed[1, 8 : 8 + experts]),
         grad_gate_w[None],
         grad_up_w[None],
         grad_down_w[None],

time: 555 us -> 459 us (0.83)
  matrix products: 35.7 us -> 3.44 us
  between operations: 15.2 us -> 1.46 us
  other arithmetic: 24.5 us -> 10.8 us
  waiting for transfers between devices: 13.5 us -> 0 us
  Pallas kernels: 426 us -> 413 us
    dot_general x6 -> x0, matrix products: 21.8 us -> none  [the longest x1 6.88 us: body_steps(): lax.dot_general(normed, grad_qkv, (((0, 1), (0, 1)), ((), ())), preferred...]
    pallas_call x1, Pallas kernels: 56.4 us -> 77.2 us  [attend_all(): pl.pallas_call(attend_all_kernel, out_shape=(jax.ShapeDtypeStruct((length...]
    pallas_call x1, Pallas kernels: 121 us -> 104 us  [attend_back(): pl.pallas_call(attend_back_kernel, out_shape=(jax.ShapeDtypeStruct((group...]
    pallas_call x1, Pallas kernels: 109 us -> 95.3 us  [expert_stage(): pl.pallas_call(functools.partial(expert_kernel, width, tile), out_shape=(...]
    all_gather x1 -> x0, waiting for transfers between devices: 13.5 us -> none  [body_steps(): w_out_all = lax.all_gather(piece, ('head', 'dp'), axis=0, tiled=True)]
    pallas_call x1, Pallas kernels: 133 us -> 120 us  [last_stage(): pl.pallas_call(functools.partial(last_kernel, tile), out_shape=(jax.Shape...]
    dot_general x9 -> x4, matrix products: 13.9 us -> 3.44 us  [contract(): lax.dot_general(left, right, (((left_dim,), (right_dim,)), ((), ())), pre...]
    pallas_call x2 -> x1, Pallas kernels: 6.61 us -> 15.9 us  [combine(): pl.pallas_call(combine_kernel, out_shape=(jax.ShapeDtypeStruct((length, w...]
  transfers between devices with their start and end apart: 4 -> 0, of which waited for: 1 -> 0; matrix products, arithmetic and copies ran while one was open for 9% -> 0% of each run, Pallas kernels for 31% -> 0%
where the time goes in v4:
time: 459 us; the launch traced here: 450 us
  Pallas kernels  413 us (90%)
  local copies, waits for them, and re-layouts  21.9 us (5%)
  other arithmetic  10.8 us (2%)
    pallas_call x1, Pallas kernels, last_stage(): pl.pallas_call(functools.partial(last_kernel, tile), out_shape=(jax.Shape...  120 us
    pallas_call x1, Pallas kernels, attend_back(): pl.pallas_call(attend_back_kernel, out_shape=(jax.ShapeDtypeStruct((group...  104 us
    pallas_call x1, Pallas kernels, expert_stage(): pl.pallas_call(functools.partial(expert_kernel, width, tile), out_shape=(...  95.3 us
    pallas_call x1, Pallas kernels, attend_all(): pl.pallas_call(attend_all_kernel, out_shape=(jax.ShapeDtypeStruct((length...  77.2 us
    pallas_call x1, Pallas kernels, combine(): pl.pallas_call(combine_kernel, out_shape=(jax.ShapeDtypeStruct((length, w...  15.9 us
    unnamed x61, local copies, waits for them, and re-layouts  14.3 us

profile of v4, /device:TPU:0, one launch (start us, length us, event | category | flops | bytes accessed | tf_op | source)
XLA Modules:
  0.0 450.2 jit_solution(11786167274282870752)
XLA Ops:
  0.6 0.0 copy-start
  0.7 0.0 copy-start.25
  0.7 0.0 copy-start.26
  0.7 0.0 copy-start.9
  0.7 0.0 copy-start.8
  0.7 0.0 copy-start.5
  0.7 0.0 copy-start.6
  0.7 0.0 copy-start.7
  0.7 0.0 copy-start.4
  0.8 0.9 fusion.39
  1.6 0.7 broadcast_add_fusion
  2.3 0.7 pad_add_fusion.1
  3.0 1.0 convert_reduce_fusion
  4.1 0.8 convolution_convert_fusion.1.signs_ref
  4.9 1.9 fusion.9.both_ref
  6.8 0.0 copy-done.25
  6.8 0.1 copy.37.routing_hbm
  7.0 0.0 copy-done.26
  7.0 0.1 reverse
  7.1 0.1 slice.94
  7.2 0.0 copy-done
  7.2 0.2 convolution_bitcast_fusion
  7.4 0.0 copy-done.9
  7.5 0.0 copy-done.8
  7.5 0.0 copy-done.5
  7.5 0.0 copy-done.6
  7.5 77.2 %attend_all.1 = (bf16[512,1024]{1,0:T(8,128)(2,1)S(1)}, bf16[4,4,512,512]{3,2,1,0:T(8,128)(2,1)}, bf16[8,160,1152]{2,1,0:T(8,128)(2,1)}, bf16[4,512,1024]{2,1,0:...) custom-call(bf16[2048,1024]{1,0:T(8,128)(2,1)} %input_ref.1, ...), custom_call_target="tpu_custom_call" | custom-call | flops 4294967296 | bytes 16777216 | tf_op jit(solution)/shard_map/attend_all/pallas_call | solution.py:503
  84.7 0.0 copy-start.15
  84.7 1.0 copy-done.15
  85.7 0.8 copy-done.17
  86.5 0.6 slice_reduce_fusion.1
  87.1 0.4 copy-done.10
  87.4 1.6 convolution_convert_fusion.signs_ref
  89.0 0.2 copy.38
  89.2 0.8 pad.13.router_ref
  90.0 95.3 %expert_stage.1 = (bf16[8,160,1024]{2,1,0:T(8,128)(2,1)}, bf16[1280,2816]{1,0:T(8,128)(2,1)}, bf16[1280,2816]{1,0:T(8,128)(2,1)}, bf16[1280,2816]{1,0:T(8,128)(2...) custom-call(bf16[512,1024]{1,0:T(8,128)(2,1)} %copy-done.10, ...), custom_call_target="tpu_custom_call" | custom-call | flops 44291850240 | bytes 38928384 | tf_op jit(solution)/shard_map/expert_stage/pallas_call | solution.py:783
  185.3 0.0 copy-start.2
  185.3 0.0 copy-start.3
  185.3 0.0 copy-start.11
  185.3 0.3 fusion.2.first_ref
  185.6 1.3 fusion.3.second_ref
  187.0 0.2 fusion.23.signs_ref
  187.2 15.9 %combine.1 = (f32[512,1024]{1,0:T(8,128)}, f32[512,1024]{1,0:T(8,128)}, bf16[512,1024]{1,0:T(8,128)(2,1)S(1)}, bf16[512,1024]{1,0:T(8,128)(2,1)S(1)}, f32[8,1024]{1,0:T(8,128)S(1)}, /*index=5*/f32[1,1024]{1,0:T(1,128)S(1)}) custom-call(bf16[1280,1024]{1,0:T(8,128)(2,1)} %bitcast.76, bf16[1280,1024]{1,0:T(8,128)(2,1)} %bitcast.77, ...), custom_call_target="tpu_custom_call" | custom-call | flops 4026531840 | bytes 5242880 | tf_op jit(solution)/shard_map/combine/pallas_call | solution.py:914
  203.1 1.0 copy-done.12
  204.1 1.0 copy-done.13
  205.0 0.6 copy-done.14
  205.7 0.6 copy-done.16
  206.2 1.9 fusion.7.both_ref
  208.1 2.3 constant_dynamic-slice_fusion.input_ref
  210.4 103.8 %attend_back.1 = (bf16[8,160,2176]{2,1,0:T(8,128)(2,1)}, bf16[1024,768]{1,0:T(8,128)(2,1)}, bf16[1024,1024]{1,0:T(8,128)(2,1)}, f32[512,1024]{1,0:T(8,128)}, f32[1,1024]{1,0:T(1,128)}, /*index=5*/f32[4,1,1024]{2,1,0:T(1,128)}) custom-call(bf16[512,1024]{1,0:T(8,128)(2,1)} %get-tuple-element.57.normed2_far, bf16[256,1024]{1,0:T(8,128)(2,1)} %copy-done.17, ...), custom_call_target="tpu_custom_call" | custom-call | flops 8589934592 | bytes 16777216 | tf_op jit(solution)/shard_map/attend_back/pallas_call | solution.py:1223
  314.2 120.4 %last_stage.1 = (f32[256,2816]{1,0:T(8,128)}, f32[256,2816]{1,0:T(8,128)}, f32[704,1024]{1,0:T(8,128)}, bf16[8,128,768]{2,1,0:T(8,128)(2,1)}, bf16[8,32,1024]{2,1,0:T(8,128)(2,1)}, /*index=5*/f32[2,16,1024]{2,1,0:T(8,128)}) custom-call(bf16[8,160,2176]{2,1,0:T(8,128)(2,1)} %get-tuple-element.69.far_ref, bf16[1280,1024]{1,0:T(8,128)(2,1)} %bitcast.74, ...), custom_call_target="tpu_custom_call" | custom-call | flops 44291850240 | bytes 38928384 | tf_op jit(solution)/shard_map/last_stage/pallas_call | solution.py:1568
  434.6 1.6 bitcast_convert_fusion
  436.3 1.7 fusion.35
  438.0 1.1 bitcast_convert_fusion.1
  439.1 0.0 copy-done.23
  439.1 0.8 fusion.27
  440.0 0.6 slice_bitcast_fusion
  440.6 0.6 fusion.36
  441.2 1.3 copy.46
  442.5 1.6 copy.47
  444.1 1.3 copy-done.19
  445.4 1.6 copy.48
  446.9 1.3 copy-done.18
  448.2 1.6 copy.49
  (31 shorter events, 0.1 us)
Async XLA Ops:
  0.6 6.5 %copy-start = (f32[32,4]{0,1:T(4,128)S(1)}, f32[32,4]{0,1:T(4,128)}, u32[]{:S(2)}) copy-start(f32[32,4]{0,1:T(4,128)} %param.26) | copy-start | bytes 1540
  0.7 6.2 %copy-start.25 = (s32[512,2]{0,1:T(2,128)S(1)}, s32[512,2]{0,1:T(2,128)}, u32[]{:S(2)}) copy-start(s32[512,2]{0,1:T(2,128)} %param.18) | copy-start | bytes 12292
  0.7 6.3 %copy-start.26 = (s32[1023]{0:T(1024)S(1)}, s32[1023]{0:T(1024)}, u32[]{:S(2)}) copy-start(s32[1023]{0:T(1024)} %param.20) | copy-start | bytes 12280
  0.7 6.8 %copy-start.9 = (f32[1024]{0:T(1024)S(1)}, f32[1024]{0:T(1024)}, u32[]{:S(2)}) copy-start(f32[1024]{0:T(1024)} %param.21) | copy-start | bytes 12292
  0.7 6.8 %copy-start.8 = (f32[1024]{0:T(1024)S(1)}, f32[1024]{0:T(1024)}, u32[]{:S(2)}) copy-start(f32[1024]{0:T(1024)} %param.27) | copy-start | bytes 12292
  0.7 6.8 %copy-start.5 = (bf16[1024,256]{1,0:T(8,128)(2,1)S(1)}, bf16[1024,256]{1,0:T(8,128)(2,1)}, u32[]{:S(2)}) copy-start(bf16[1024,256]{1,0:T(8,128)(2,1)} %query_w.1) | copy-start | bytes 1572868
  0.7 6.8 %copy-start.6 = (bf16[1024,256]{1,0:T(8,128)(2,1)S(1)}, bf16[1024,256]{1,0:T(8,128)(2,1)}, u32[]{:S(2)}) copy-start(bf16[1024,256]{1,0:T(8,128)(2,1)} %key_w.1) | copy-start | bytes 1572868
  0.7 6.8 %copy-start.7 = (bf16[1024,256]{1,0:T(8,128)(2,1)S(1)}, bf16[1024,256]{1,0:T(8,128)(2,1)}, u32[]{:S(2)}) copy-start(bf16[1024,256]{1,0:T(8,128)(2,1)} %value_w.1) | copy-start | bytes 1572868
  0.7 6.8 %copy-start.4 = (bf16[256,1024]{1,0:T(8,128)(2,1)S(1)}, bf16[256,1024]{1,0:T(8,128)(2,1)}, u32[]{:S(2)}) copy-start(bf16[256,1024]{1,0:T(8,128)(2,1)} %w_out_ref.1) | copy-start | bytes 1572868
  84.7 1.0 copy-start.15
  85.7 0.8 copy-start.17
  86.5 1.0 copy-start.10
  86.5 2.5 copy-start.24
  185.3 1.9 copy-start.2
  185.3 1.9 copy-start.3
  185.3 1.9 copy-start.11
  203.1 1.0 copy-start.12
  204.1 1.0 copy-start.13
  205.0 0.6 copy-start.14
  205.6 0.6 copy-start.16
  436.2 1.8 copy-start.22
  436.2 2.9 copy-start.23
  436.3 4.9 %copy-start.21 = (f32[512,1024]{1,0:T(8,128)S(1)}, f32[512,1024]{1,0:T(8,128)}, u32[]{:S(2)}) copy-start(f32[512,1024]{1,0:T(8,128)} %get-tuple-element.118) | copy-start | bytes 6291460
  438.0 4.5 %copy-start.20 = (f32[256,2816]{1,0:T(8,128)S(1)}, f32[256,2816]{1,0:T(8,128)}, u32[]{:S(2)}) copy-start(f32[256,2816]{1,0:T(8,128)} %get-tuple-element.84) | copy-start | bytes 8650756
  442.5 2.9 copy-start.19
  445.4 2.9 copy-start.18
  445.4 4.4 copy-start.1
